TPU v7x, 32 devices: a whole 2x2x4 slice. The times are simulated.
32 devices in a mesh: gx: 4 (over z), gy: 4 (over y, core), gz: 2 (over x).
Axes of the slice: x: 2, y: 2, z: 4, core: 2. Of those that a mesh axis runs over, the one named last changes fastest.
Arguments:
- features: bfloat16 [64, 8, 32, 256], P(None, 'gx', 'gy', 'gz'), may hold values from -6 to 6
- dest_bricks: int32 [1024, 1], P(('gx', 'gy', 'gz')), may hold values from 0 to 7
- cell_ids: int32 [1024, 64], P(('gx', 'gy', 'gz')), may hold values from 0 to 2047
- cic_masses: bfloat16 [1024, 64], P(('gx', 'gy', 'gz')), may hold values from 0.25 to 4
- live_counts: int32 [32], P(('gx', 'gy', 'gz')), may hold values from 8 to 32
- style_vector: float32 [512], replicated, may hold values from -6 to 6
- affine_first: float32 [512, 64], replicated, may hold values from -0.25 to 0.25
- kernel_first: bfloat16 [27, 64, 64], replicated, may hold values from -0.15625 to 0.15625
- bias_first: float32 [64], replicated, may hold values from -0.5 to 0.5
- gain_first: float32 [64], replicated, may hold values from 1 to 4
- affine_second: float32 [512, 64], replicated, may hold values from -0.25 to 0.25
- kernel_second: bfloat16 [27, 64, 64], replicated, may hold values from -0.15625 to 0.15625
- bias_second: float32 [64], replicated, may hold values from -0.5 to 0.5
- gain_second: float32 [64], replicated, may hold values from 1 to 4
Outputs:
- upsampled: bfloat16 [64, 8, 32, 256], P(None, 'gx', 'gy', 'gz')
All inputs are finite; a program needn't handle non-finite values.
Results may differ from a plain program's by a relative error of at most 0.0054.
Values may be sent and summed in bfloat16 or wider, within the bound.
No kernel may reach another device: no remote copies, remote signals or barrier semaphores. Data moves between devices by JAX's collectives and lax.ppermute only.
A program may use at most 64 MiB of HBM per device.

v0:
```python
import jax
import jax.numpy as jnp
from jax import lax
from jax.sharding import PartitionSpec as P


def extended(cells, sides, width):
    for axis, dim in sides:
        count = lax.axis_size(axis)
        head = lax.slice_in_dim(cells, 0, width, axis=dim)
        tail = lax.slice_in_dim(cells, cells.shape[dim] - width, cells.shape[dim], axis=dim)
        cells = jnp.concatenate(
            [
                lax.ppermute(tail, axis, [(i, (i + 1) % count) for i in range(count)]),
                cells,
                lax.ppermute(head, axis, [((i + 1) % count, i) for i in range(count)]),
            ],
            axis=dim,
        )
    return cells


def modulate(kernel, style_vector, affine):
    styles = (
        jnp.dot(
            style_vector[None, :],
            affine,
            precision=lax.Precision.HIGHEST,
            preferred_element_type=jnp.float32,
        )[0]
        + 1.0
    )
    scaled = kernel.astype(jnp.float32) * styles[None, None, :]
    demod = lax.rsqrt(jnp.sum(scaled * scaled, axis=(0, 2)) + 1e-08)
    return (scaled * demod[None, :, None]).astype(jnp.bfloat16)


def activate(values):
    return jnp.where(values >= 0, values, 0.2 * values) * jnp.sqrt(jnp.float32(2.0))


def convolve(padded, modulated):
    chans = padded.shape[0]
    out_x = padded.shape[1] - 2
    out_y = padded.shape[2] - 2
    out_z = padded.shape[3] - 2
    outputs = modulated.shape[1]
    summed = jnp.zeros((outputs, out_x * out_y * out_z), jnp.float32)
    for offset_x in range(3):
        for offset_y in range(3):
            stacked = jnp.concatenate(
                [
                    padded[
                        :,
                        offset_x : offset_x + out_x,
                        offset_y : offset_y + out_y,
                        offset_z : offset_z + out_z,
                    ]
                    for offset_z in range(3)
                ],
                axis=0,
            ).reshape(3 * chans, -1)
            first_offset = offset_x * 9 + offset_y * 3
            matrix = (
                modulated[first_offset : first_offset + 3]
                .transpose(1, 0, 2)
                .reshape(outputs, 3 * chans)
            )
            summed = summed + jnp.dot(matrix, stacked, preferred_element_type=jnp.float32)
    return summed.reshape(outputs, out_x, out_y, out_z)


def finish_layer(convolved, bias, gain, density):
    return activate(
        convolved + gain[:, None, None, None] * density[None] + bias[:, None, None, None]
    )


def shards(
    features,
    dest_bricks,
    cell_ids,
    cic_masses,
    live_counts,
    style_vector,
    affine_first,
    kernel_first,
    bias_first,
    gain_first,
    affine_second,
    kernel_second,
    bias_second,
    gain_second,
):
    size_x = features.shape[1]
    size_y = features.shape[2]
    size_z = features.shape[3]
    cell_total = size_x * size_y * size_z
    slab_size = lax.axis_size("gy") * lax.axis_size("gz")
    per_block = cell_ids.shape[1]
    cell_iota = jnp.arange(cell_total, dtype=jnp.int32)
    live_count = live_counts[0]
    brick_iota = jnp.arange(slab_size, dtype=jnp.int32)

    def paint_step(position, partial_value):
        first_block = position * 4
        block_dest = lax.dynamic_slice_in_dim(dest_bricks, first_block, 4, 0)[:, 0]
        block_cells = lax.dynamic_slice_in_dim(cell_ids, first_block, 4, 0)
        block_mass = lax.dynamic_slice_in_dim(cic_masses, first_block, 4, 0)
        live_mask = first_block + jnp.arange(4, dtype=jnp.int32) < live_count
        block_mass = block_mass * live_mask[:, None].astype(jnp.bfloat16)
        dest_onehot = (block_dest[:, None] == brick_iota[None, :]).astype(jnp.bfloat16)
        spread = (dest_onehot[:, None, :] * block_mass[:, :, None]).reshape(
            4 * per_block, slab_size
        )
        cell_onehot = (block_cells.reshape(-1)[:, None] == cell_iota[None, :]).astype(jnp.bfloat16)
        return partial_value + jnp.dot(spread.T, cell_onehot, preferred_element_type=jnp.float32)

    painted = lax.fori_loop(
        0, (live_count + 3) // 4, paint_step, jnp.zeros((slab_size, cell_total), jnp.float32)
    )
    by_column = lax.psum_scatter(
        painted.reshape(lax.axis_size("gy"), lax.axis_size("gz"), cell_total),
        "gz",
        scatter_dimension=1,
        tiled=True,
    )
    own_density = lax.psum_scatter(by_column, "gy", scatter_dimension=0, tiled=True)
    density = own_density.reshape(size_x, size_y, size_z)
    modulated_first = modulate(kernel_first, style_vector, affine_first)
    modulated_second = modulate(kernel_second, style_vector, affine_second)
    padded = extended(features, (("gx", 1), ("gy", 2), ("gz", 3)), 1)
    hidden = finish_layer(
        convolve(padded, modulated_first), bias_first, gain_first, density
    ).astype(jnp.bfloat16)
    hidden_padded = extended(hidden, (("gx", 1), ("gy", 2), ("gz", 3)), 1)
    result = finish_layer(
        convolve(hidden_padded, modulated_second), bias_second, gain_second, density
    )
    return result.astype(jnp.bfloat16)


def solution(mesh):
    return jax.shard_map(
        shards,
        mesh=mesh,
        in_specs=(
            P(None, "gx", "gy", "gz"),
            P(("gx", "gy", "gz"), None),
            P(("gx", "gy", "gz"), None),
            P(("gx", "gy", "gz"), None),
            P(("gx", "gy", "gz")),
            P(),
            P(),
            P(),
            P(),
            P(),
            P(),
            P(),
            P(),
            P(),
        ),
        out_specs=P(None, "gx", "gy", "gz"),
        check_vma=False,
    )
```

profile of v0, /device:TPU:0, one launch (start us, length us, event | category | flops | bytes accessed | tf_op | source)
XLA Modules:
  0.0 148.1 jit_solution(6205014098920659196)
XLA Ops:
  6.5 1.1 copy.112
  7.6 3.1 %collective-permute-start = (bf16[64,1,8,128]{3,0,2,1:T(8,128)(2,1)S(1)}, bf16[64,1,8,128]{3,0,2,1:T(8,128)(2,1)S(1)}, u32[]{:S(2)}, u32[]{:S(2)}) collective-permute-start(bf16[64,1,8,128]{3,0,2,1:T(8,128)(2,1)S(1)} %get-tuple-element.177), channel_id=1, source_target_pairs={{0,8},{8,16},{16,24},{24,0},{1,9},{9,17},{17,25},{25,1},{2,10},{10... | collective-permute-start | bytes 393224 | tf_op jit(solution)/shard_map/ppermute | solution.py:14
  10.7 2.1 %collective-permute-start.1 = (bf16[64,1,8,128]{3,0,2,1:T(8,128)(2,1)S(1)}, bf16[64,1,8,128]{3,0,2,1:T(8,128)(2,1)S(1)}, u32[]{:S(2)}, u32[]{:S(2)}) collective-permute-start(bf16[64,1,8,128]{3,0,2,1:T(8,128)(2,1)S(1)} %get-tuple-element.176), channel_id=1, source_target_pairs={{8,0},{16,8},{24,16},{0,24},{9,1},{17,9},{25,17},{1,25},{10,2},{18... | collective-permute-start | bytes 393224 | tf_op jit(solution)/shard_map/ppermute | solution.py:16
  13.5 14.8 %while.11 = (s32[]{:T(128)}, f32[8,2048]{1,0:T(8,128)S(1)}, s32[]{:T(128)}, s32[32,1]{0,1:T(1,128)}, bf16[32,64]{1,0:T(8,128)(2,1)}, /*index=5*/s32[]{:T(128)}, ...) while((s32[]{:T(128)}, f32[8,2048]{1,0:T(8,128)S(1)}, s32[]{:T(128)}, ...), condition=%wide.region_3.4_spmd.clone, body=%wide.region_2.3_spmd.clone.sunk | while | flops 8932434 | bytes 147311 | solution.py:119
  37.4 26.2 %all-reduce.4.cloned.1.call-done = f32[4,2,2048]{2,0,1:T(4,128)} async-done(((f32[4,2,2048]{2,0,1:T(4,128)}), f32[4,2,2048]{2,0,1:T(4,128)}) %all-reduce.4.cloned.1.call-update) | async-done | bytes 65552
  63.6 1.4 constant_dynamic-slice_fusion.3
  65.1 10.6 %all-reduce.1 = f32[4,1,2048]{2,1,0:T(1,128)S(1)} all-reduce(f32[4,1,2048]{2,1,0:T(1,128)S(1)} %copy.140), channel_id=3, replica_groups=mesh['gx'=4,'gy'=4,'gz'=2] {'gy'}, use_global_device_ids=true, to_apply=%region_5.6.clone | all-reduce | flops 8192 | bytes 65536
  76.0 1.7 %collective-permute-start.3 = (bf16[64,4,1,128]{3,0,2,1:T(8,128)(2,1)S(1)}, bf16[64,4,1,128]{3,0,2,1:T(8,128)(2,1)S(1)}, u32[]{:S(2)}, u32[]{:S(2)}) collective-permute-start(bf16[64,4,1,128]{3,0,2,1:T(8,128)(2,1)S(1)} %get-tuple-element.149), channel_id=1, source_target_pairs={{2,0},{4,2},{6,4},{0,6},{3,1},{5,3},{7,5},{1,7},{10,8},{12,10},{14... | collective-permute-start | bytes 196616 | tf_op jit(solution)/shard_map/ppermute | solution.py:16
  77.7 1.2 constant_dynamic-slice_fusion.2
  80.1 1.1 copy.165
  82.2 1.5 %collective-permute-start.5 = (bf16[64,4,10,1]{0,2,3,1:T(8,128)(2,1)S(1)}, bf16[64,4,10,1]{0,2,3,1:T(8,128)(2,1)}, u32[]{:S(2)}, u32[]{:S(2)}) collective-permute-start(bf16[64,4,10,1]{0,2,3,1:T(8,128)(2,1)S(1)} %copy.166), channel_id=1, source_target_pairs={{1,0},{0,1},{3,2},{2,3},{5,4},{4,5},{7,6},{6,7},{9,8},{8,9},{11,10... | collective-permute-start | bytes 15368 | tf_op jit(solution)/shard_map/ppermute | solution.py:16
  86.2 1.1 copy.118
  88.2 1.1 fusion.73
  100.3 1.4 collective-permute-start.6
  101.7 2.5 %collective-permute-start.7 = (bf16[64,1,8,128]{3,0,2,1:T(8,128)(2,1)S(1)}, bf16[64,1,8,128]{3,0,2,1:T(8,128)(2,1)S(1)}, u32[]{:S(2)}, u32[]{:S(2)}) collective-permute-start(bf16[64,1,8,128]{3,0,2,1:T(8,128)(2,1)S(1)} %get-tuple-element.172), channel_id=1, source_target_pairs={{8,0},{16,8},{24,16},{0,24},{9,1},{17,9},{25,17},{1,25},{10,2},{18... | collective-permute-start | bytes 393224 | tf_op jit(solution)/shard_map/ppermute | solution.py:16
  104.3 4.2 %collective-permute-done.6 = bf16[64,1,8,128]{3,0,2,1:T(8,128)(2,1)S(1)} collective-permute-done((bf16[64,1,8,128]{3,0,2,1:T(8,128)(2,1)S(1)}, bf16[64,1,8,128]{3,0,2,1:T(8,128)(2,1)S(1)}, u32[]{:S(2)}, u32[]{:S(2)}) %collective-permute-start.6) | collective-permute-done | bytes 131104 | tf_op jit(solution)/shard_map/ppermute | solution.py:14
  108.5 1.2 collective-permute-done.7
  109.8 1.7 %collective-permute-start.9 = (bf16[64,4,1,128]{3,0,2,1:T(8,128)(2,1)S(1)}, bf16[64,4,1,128]{3,0,2,1:T(8,128)(2,1)S(1)}, u32[]{:S(2)}, u32[]{:S(2)}) collective-permute-start(bf16[64,4,1,128]{3,0,2,1:T(8,128)(2,1)S(1)} %get-tuple-element.143), channel_id=1, source_target_pairs={{2,0},{4,2},{6,4},{0,6},{3,1},{5,3},{7,5},{1,7},{10,8},{12,10},{14... | collective-permute-start | bytes 196616 | tf_op jit(solution)/shard_map/ppermute | solution.py:16
  119.0 1.1 copy.167
  120.1 1.5 collective-permute-start.10
  122.8 1.3 collective-permute-done.10
  124.4 1.5 collective-permute-done.11
  125.9 1.1 copy.145
  127.0 1.6 %maximum_maximum_fusion.1 = (bf16[64,4,10,129]{3,0,2,1:T(8,128)(2,1)S(1)}, bf16[64,4,10,129]{3,0,2,1:T(8,128)(2,1)S(1)}) fusion(bf16[64,4,1,128]{3,0,2,1:T(8,128)(2,1)S(1)} %copy-done.7, bf16[64,1,8,128]{3,0,2,1:T(8,128)(2,1)S(1)} %collective-permute-done.7, bf16[64,2,8,128]{3,0,2,1:T(8,128)(2,1)S(1)} %fusion.62, ...), kind=kLoop, calls=%fused_computation.33 | loop fusion | flops 7925760 | bytes 1986560 | tf_op jit(solution)/shard_map/concatenate | solution.py:12
  (240 shorter events, 61.8 us)
Async XLA Ops:
  6.5 22.6 %copy-start = (f32[512,64]{0,1:T(8,128)S(1)}, f32[512,64]{0,1:T(8,128)}, u32[]{:S(2)}) copy-start(f32[512,64]{0,1:T(8,128)} %param.22) | copy-start | bytes 393220
  6.5 57.1 %all-reduce.4.cloned.1.call-start = ((), (), s32[]{:S(2)}) async-start(), calls=%async_computation | async-start | bytes 131072
  7.6 68.1 %collective-permute-start = (bf16[64,1,8,128]{3,0,2,1:T(8,128)(2,1)S(1)}, bf16[64,1,8,128]{3,0,2,1:T(8,128)(2,1)S(1)}, u32[]{:S(2)}, u32[]{:S(2)}) collective-permute-start(bf16[64,1,8,128]{3,0,2,1:T(8,128)(2,1)S(1)} %get-tuple-element.177), channel_id=1, source_target_pairs={{0,8},{8,16},{16,24},{24,0},{1,9},{9,17},{17,25},{25,1},{2,10},{10... | collective-permute-start | bytes 393224 | tf_op jit(solution)/shard_map/ppermute | solution.py:14
  10.7 65.1 %collective-permute-start.1 = (bf16[64,1,8,128]{3,0,2,1:T(8,128)(2,1)S(1)}, bf16[64,1,8,128]{3,0,2,1:T(8,128)(2,1)S(1)}, u32[]{:S(2)}, u32[]{:S(2)}) collective-permute-start(bf16[64,1,8,128]{3,0,2,1:T(8,128)(2,1)S(1)} %get-tuple-element.176), channel_id=1, source_target_pairs={{8,0},{16,8},{24,16},{0,24},{9,1},{17,9},{25,17},{1,25},{10,2},{18... | collective-permute-start | bytes 393224 | tf_op jit(solution)/shard_map/ppermute | solution.py:16
  13.5 15.6 %copy-start.30 = (f32[512]{0:T(512)S(1)}, f32[512]{0:T(512)}, u32[]{:S(2)}) copy-start(f32[512]{0:T(512)} %param.21) | copy-start | bytes 6148
  13.5 15.8 %copy-start.2 = (bf16[27,64,64]{2,1,0:T(8,128)(2,1)S(1)}, bf16[27,64,64]{2,1,0:T(8,128)(2,1)}, u32[]{:S(2)}) copy-start(bf16[27,64,64]{2,1,0:T(8,128)(2,1)} %param.23) | copy-start | bytes 663556
  29.8 6.3 %copy-start.39 = (u32[32]{0:T(128)S(1)}, u32[32]{0:T(128)}, u32[]{:S(2)}) copy-start(u32[32]{0:T(128)} %constant.42) | copy-start | bytes 388
  29.8 7.0 %copy-start.38 = (u32[32]{0:T(128)S(1)}, u32[32]{0:T(128)}, u32[]{:S(2)}) copy-start(u32[32]{0:T(128)} %constant.46) | copy-start | bytes 388
  29.8 45.9 %copy-start.4 = (bf16[64,2,8,128]{3,2,1,0:T(8,128)(2,1)S(1)}, bf16[64,2,8,128]{3,2,1,0:T(8,128)(2,1)}, u32[]{:S(2)}) copy-start(bf16[64,2,8,128]{3,2,1,0:T(8,128)(2,1)} %param.16) | copy-start | bytes 786436
  30.1 45.6 %copy-start.31 = (f32[64]{0:T(128)}, f32[64]{0:T(128)S(1)}, u32[]{:S(2)}) copy-start(f32[64]{0:T(128)S(1)} %fusion.9) | copy-start | bytes 772
  75.7 3.9 %copy-start.8 = (bf16[64,1,8,128]{3,0,2,1:T(8,128)(2,1)}, bf16[64,1,8,128]{3,0,2,1:T(8,128)(2,1)S(1)}, u32[]{:S(2)}) copy-start(bf16[64,1,8,128]{3,0,2,1:T(8,128)(2,1)S(1)} %collective-permute-done) | copy-start | bytes 393220
  75.9 3.7 %collective-permute-start.2 = (bf16[64,4,1,128]{3,0,2,1:T(8,128)(2,1)S(1)}, bf16[64,4,1,128]{3,0,2,1:T(8,128)(2,1)S(1)}, u32[]{:S(2)}, u32[]{:S(2)}) collective-permute-start(bf16[64,4,1,128]{3,0,2,1:T(8,128)(2,1)S(1)} %get-tuple-element.148), channel_id=1, source_target_pairs={{0,2},{2,4},{4,6},{6,0},{1,3},{3,5},{5,7},{7,1},{8,10},{10,12},{12... | collective-permute-start | bytes 196616 | tf_op jit(solution)/shard_map/ppermute | solution.py:14
  76.0 3.7 %collective-permute-start.3 = (bf16[64,4,1,128]{3,0,2,1:T(8,128)(2,1)S(1)}, bf16[64,4,1,128]{3,0,2,1:T(8,128)(2,1)S(1)}, u32[]{:S(2)}, u32[]{:S(2)}) collective-permute-start(bf16[64,4,1,128]{3,0,2,1:T(8,128)(2,1)S(1)} %get-tuple-element.149), channel_id=1, source_target_pairs={{2,0},{4,2},{6,4},{0,6},{3,1},{5,3},{7,5},{1,7},{10,8},{12,10},{14... | collective-permute-start | bytes 196616 | tf_op jit(solution)/shard_map/ppermute | solution.py:16
  81.1 3.9 %collective-permute-start.4 = (bf16[64,4,10,1]{0,2,3,1:T(8,128)(2,1)}, bf16[64,4,10,1]{0,2,3,1:T(8,128)(2,1)S(1)}, u32[]{:S(2)}, u32[]{:S(2)}) collective-permute-start(bf16[64,4,10,1]{0,2,3,1:T(8,128)(2,1)} %copy.165), channel_id=1, source_target_pairs={{0,1},{1,0},{2,3},{3,2},{4,5},{5,4},{6,7},{7,6},{8,9},{9,8},{10,11... | collective-permute-start | bytes 15368 | tf_op jit(solution)/shard_map/ppermute | solution.py:14
  82.2 4.0 %collective-permute-start.5 = (bf16[64,4,10,1]{0,2,3,1:T(8,128)(2,1)S(1)}, bf16[64,4,10,1]{0,2,3,1:T(8,128)(2,1)}, u32[]{:S(2)}, u32[]{:S(2)}) collective-permute-start(bf16[64,4,10,1]{0,2,3,1:T(8,128)(2,1)S(1)} %copy.166), channel_id=1, source_target_pairs={{1,0},{0,1},{3,2},{2,3},{5,4},{4,5},{7,6},{6,7},{9,8},{8,9},{11,10... | collective-permute-start | bytes 15368 | tf_op jit(solution)/shard_map/ppermute | solution.py:16
  99.6 4.6 %copy-start.32 = (f32[64]{0:T(128)S(1)}, f32[64]{0:T(128)}, u32[]{:S(2)}) copy-start(f32[64]{0:T(128)} %copy-done.31) | copy-start | bytes 772
  99.6 4.6 %copy-start.37 = (f32[64]{0:T(128)S(1)}, f32[64]{0:T(128)}, u32[]{:S(2)}) copy-start(f32[64]{0:T(128)} %add_rsqrt_fusion.1) | copy-start | bytes 772
  100.3 8.2 %collective-permute-start.6 = (bf16[64,1,8,128]{3,0,2,1:T(8,128)(2,1)S(1)}, bf16[64,1,8,128]{3,0,2,1:T(8,128)(2,1)S(1)}, u32[]{:S(2)}, u32[]{:S(2)}) collective-permute-start(bf16[64,1,8,128]{3,0,2,1:T(8,128)(2,1)S(1)} %get-tuple-element.171), channel_id=1, source_target_pairs={{0,8},{8,16},{16,24},{24,0},{1,9},{9,17},{17,25},{25,1},{2,10},{10... | collective-permute-start | bytes 393224 | tf_op jit(solution)/shard_map/ppermute | solution.py:14
  101.7 8.0 %collective-permute-start.7 = (bf16[64,1,8,128]{3,0,2,1:T(8,128)(2,1)S(1)}, bf16[64,1,8,128]{3,0,2,1:T(8,128)(2,1)S(1)}, u32[]{:S(2)}, u32[]{:S(2)}) collective-permute-start(bf16[64,1,8,128]{3,0,2,1:T(8,128)(2,1)S(1)} %get-tuple-element.172), channel_id=1, source_target_pairs={{8,0},{16,8},{24,16},{0,24},{9,1},{17,9},{25,17},{1,25},{10,2},{18... | collective-permute-start | bytes 393224 | tf_op jit(solution)/shard_map/ppermute | solution.py:16
  109.7 8.2 %collective-permute-start.8 = (bf16[64,4,1,128]{3,0,2,1:T(8,128)(2,1)S(1)}, bf16[64,4,1,128]{3,0,2,1:T(8,128)(2,1)S(1)}, u32[]{:S(2)}, u32[]{:S(2)}) collective-permute-start(bf16[64,4,1,128]{3,0,2,1:T(8,128)(2,1)S(1)} %get-tuple-element.142), channel_id=1, source_target_pairs={{0,2},{2,4},{4,6},{6,0},{1,3},{3,5},{5,7},{7,1},{8,10},{10,12},{12... | collective-permute-start | bytes 196616 | tf_op jit(solution)/shard_map/ppermute | solution.py:14
  109.8 8.1 %collective-permute-start.9 = (bf16[64,4,1,128]{3,0,2,1:T(8,128)(2,1)S(1)}, bf16[64,4,1,128]{3,0,2,1:T(8,128)(2,1)S(1)}, u32[]{:S(2)}, u32[]{:S(2)}) collective-permute-start(bf16[64,4,1,128]{3,0,2,1:T(8,128)(2,1)S(1)} %get-tuple-element.143), channel_id=1, source_target_pairs={{2,0},{4,2},{6,4},{0,6},{3,1},{5,3},{7,5},{1,7},{10,8},{12,10},{14... | collective-permute-start | bytes 196616 | tf_op jit(solution)/shard_map/ppermute | solution.py:16
  120.1 3.9 %collective-permute-start.10 = (bf16[64,4,10,1]{0,2,3,1:T(8,128)(2,1)}, bf16[64,4,10,1]{0,2,3,1:T(8,128)(2,1)S(1)}, u32[]{:S(2)}, u32[]{:S(2)}) collective-permute-start(bf16[64,4,10,1]{0,2,3,1:T(8,128)(2,1)} %copy.167), channel_id=1, source_target_pairs={{0,1},{1,0},{2,3},{3,2},{4,5},{5,4},{6,7},{7,6},{8,9},{9,8},{10,11... | collective-permute-start | bytes 15368 | tf_op jit(solution)/shard_map/ppermute | solution.py:14
  122.0 3.9 %collective-permute-start.11 = (bf16[64,4,10,1]{0,2,3,1:T(8,128)(2,1)S(1)}, bf16[64,4,10,1]{0,2,3,1:T(8,128)(2,1)}, u32[]{:S(2)}, u32[]{:S(2)}) collective-permute-start(bf16[64,4,10,1]{0,2,3,1:T(8,128)(2,1)S(1)} %copy.168), channel_id=1, source_target_pairs={{1,0},{0,1},{3,2},{2,3},{5,4},{4,5},{7,6},{6,7},{9,8},{8,9},{11,10... | collective-permute-start | bytes 15368 | tf_op jit(solution)/shard_map/ppermute | solution.py:16
  122.6 4.4 %copy-start.7 = (bf16[64,4,1,128]{3,0,2,1:T(8,128)(2,1)S(1)}, bf16[64,4,1,128]{3,0,2,1:T(8,128)(2,1)}, u32[]{:S(2)}) copy-start(bf16[64,4,1,128]{3,0,2,1:T(8,128)(2,1)} %copy-done.6) | copy-start | bytes 196612
  (29 other events, 29.2 us)
Sparse Core Ops, SparseCore 0:
  29.2 34.3 all-reduce.3
where the time goes:
time: 150 us; the launch traced here: 148 us
  local copies, waits for them, and re-layouts  48 us (32%)
  waiting for transfers between devices  36.5 us (24%)
  starting transfers between devices  16.8 us (11%)
  between operations  15.1 us (10%)
  other arithmetic  13.4 us (9%)
  blocking collectives  10.6 us (7%)
  matrix products  7.49 us (5%)
    unnamed x2, waiting for transfers between devices  26.3 us
    unnamed x93, local copies, waits for them, and re-layouts  12.9 us
    transpose x20, local copies, waits for them, and re-layouts, convolve(): matrix = modulated[first_offset:first_offset + 3].transpose(1, 0, 2).resh...  11.6 us
    unnamed x1, blocking collectives  10.6 us
    ppermute x6, starting transfers between devices, extended(): lax.ppermute(head, axis, [((i + 1) % count, i) for i in range(count)])  10.1 us
    concatenate x18, local copies, waits for them, and re-layouts, convolve(): jnp.concatenate([padded[:, offset_x:offset_x + out_x, offset_y:offset_y +...  9.22 us
    ppermute x6, waiting for transfers between devices, extended(): lax.ppermute(tail, axis, [(i, (i + 1) % count) for i in range(count)])  6.84 us
    ppermute x6, starting transfers between devices, extended(): lax.ppermute(tail, axis, [(i, (i + 1) % count) for i in range(count)])  6.66 us
  transfers between devices with their start and end apart: 13, of which 8 were waited for; matrix products, arithmetic and copies ran while one was open for 24% of the time, Pallas kernels for 0%

commit v1 on v0

v1 whole, which is shorter than its diff:
```python
import functools

import jax
import jax.numpy as jnp
from jax import lax
from jax.experimental import pallas as pl
from jax.experimental.pallas import tpu as pltpu
from jax.sharding import PartitionSpec as P

F32 = jnp.float32
BF16 = jnp.bfloat16
SMEM = pltpu.SMEM


def shift(cells, axis, step):
    count = lax.axis_size(axis)
    return lax.ppermute(cells, axis, [(i, (i + step) % count) for i in range(count)])


def call(body, outs, name, flops=0, smem=(), scratch=()):
    def run(*args):
        size = sum(a.size * a.dtype.itemsize for a in args)
        specs = [
            pl.BlockSpec(memory_space=SMEM if i in smem else pltpu.VMEM)
            for i in range(len(args))
        ]
        return pl.pallas_call(
            body,
            out_shape=tuple(jax.ShapeDtypeStruct(s, d) for s, d in outs),
            in_specs=specs,
            out_specs=tuple(pl.BlockSpec(memory_space=pltpu.VMEM) for _ in outs),
            scratch_shapes=list(scratch),
            name=name,
            cost_estimate=pl.CostEstimate(
                flops=flops, bytes_accessed=size, transcendentals=0
            ),
        )(*args)

    return run


def lanes_of(shape):
    return lax.broadcasted_iota(jnp.int32, shape, len(shape) - 1)


def rolled(values, amount, axis):
    amount = amount % values.shape[axis]
    return values if amount == 0 else pltpu.roll(values, amount, axis)


def halves(values):
    high = values.astype(BF16)
    return high, (values - high.astype(F32)).astype(BF16)


def split_body(cells, *planes):
    for at, plane in enumerate(planes):
        part = cells[:, at].astype(F32)
        plane[...] = jnp.swapaxes(part, 0, 1).astype(BF16)


def column_of(row):
    size = row.shape[1]
    wide = jnp.broadcast_to(row, (size, size))
    same = lax.broadcasted_iota(jnp.int32, (size, size), 0) == lanes_of((size, size))
    return jnp.sum(jnp.where(same, wide, 0.0), axis=1, keepdims=True)


def modulate_body(style, affine, kernel, bias, gain, weights, columns):
    styles = (
        jnp.dot(
            style[...],
            affine[...],
            precision=lax.Precision.HIGHEST,
            preferred_element_type=F32,
        )
        + 1.0
    )
    chans = kernel.shape[1]
    total = jnp.zeros((chans, kernel.shape[2]), F32)
    for k in range(27):
        scaled = kernel[k].astype(F32) * styles
        total = total + scaled * scaled
    demod = lax.rsqrt(jnp.sum(total, axis=1, keepdims=True) + 1e-08)
    for g in range(3):
        blocks = [
            (kernel[3 * j + g].astype(F32) * styles * demod).astype(BF16)
            for j in range(9)
        ]
        weights[g * chans : (g + 1) * chans, :] = jnp.concatenate(blocks, axis=1)
    columns[0] = jnp.broadcast_to(column_of(bias[...]), columns.shape[1:])
    columns[1] = jnp.broadcast_to(column_of(gain[...]), columns.shape[1:])


def paint_body(rows_y, counts, where, live, dest, cells, masses, *refs):
    count_y, count_z = counts
    size_x = len(rows_y)
    planes, messages, own = refs[:size_x], refs[size_x:-1], refs[-1]
    size_y, chans, size_z = planes[0].shape
    blocks, per = cells.shape
    half = blocks // 2
    rank_y, rank_z = where[0], where[1]
    shape = (blocks, per)
    target = jnp.broadcast_to(dest[...], shape)
    to_y = lax.div(target, jnp.full(shape, count_z, jnp.int32))
    to_z = target - to_y * count_z - rank_z
    to_y = to_y - rank_y
    to_y = jnp.where(to_y < 0, to_y + count_y, to_y)
    to_z = jnp.where(to_z < 0, to_z + count_z, to_z)
    cell = cells[...]
    cell_row = lax.div(cell, jnp.full(shape, size_z, jnp.int32))
    at_z = cell - cell_row * size_z
    at_x = lax.div(cell_row, jnp.full(shape, size_y, jnp.int32))
    at_y = cell_row - at_x * size_y
    row = ((to_z * size_x + at_x) * count_y + to_y) * size_y + at_y
    alive = lax.broadcasted_iota(jnp.int32, shape, 0) < live[0]
    mass = jnp.where(alive, masses[...].astype(F32), 0.0)

    def paired(values):
        return jnp.concatenate([values[:half], values[half:]], axis=1)

    row, at_z, mass = paired(row), paired(at_z), paired(mass)
    width = 2 * per
    group = size_x * count_y * size_y
    total = count_z * group
    iota_rows = lax.broadcasted_iota(jnp.int32, (total, width), 0)
    iota_z = lax.broadcasted_iota(jnp.int32, (size_z, width), 0)
    left, right = [], []
    for r in range(half):
        left.append(
            jnp.where(iota_rows == row[r : r + 1], mass[r : r + 1], 0.0).astype(BF16)
        )
        right.append(jnp.where(iota_z == at_z[r : r + 1], 1.0, 0.0).astype(BF16))
    painted = lax.dot_general(
        jnp.concatenate(left, axis=1),
        jnp.concatenate(right, axis=1),
        (((1,), (1,)), ((), ())),
        preferred_element_type=F32,
    )
    parts = [painted[s * group : (s + 1) * group] for s in range(count_z)]
    lane = lanes_of((group, size_z))

    def beside(s):
        after = parts[(s + 1) % count_z]
        before = parts[(s - 1) % count_z]
        return jnp.where(lane == 0, after, jnp.where(lane == size_z - 1, before, 0.0))

    own[:group] = parts[0]
    own[group:] = beside(0)
    lane = lanes_of((chans, size_z))
    tile = jnp.zeros((chans, size_z), F32)
    for x in range(size_x):
        for y in range(size_y):
            j = x * size_y + y
            turned = rolled(planes[x][y].astype(F32), 4 * j + 2, 1)
            tile = jnp.where((lane >= 4 * j) & (lane < 4 * j + 4), turned, tile)
    tile = tile.astype(BF16)
    for s in range(1, count_z):
        message = messages[s - 1]
        message[:chans] = tile
        base = chans
        for part in halves(parts[s]) + halves(beside(s)):
            message[base : base + group] = part
            base += group


def pack_y_body(count_y, count_z, size_x, *refs):
    planes = refs[:size_x]
    own = refs[size_x]
    received = refs[size_x + 1 : size_x + count_z]
    outs = refs[size_x + count_z :]
    size_y, chans, size_z = planes[0].shape
    group = own.shape[0] // 2
    lane = lanes_of((chans, size_z))
    before = received[0][:chans].astype(F32)
    after = received[-1][:chans].astype(F32)
    tile = jnp.where(lane % 4 < 2, before, after).astype(BF16)
    main, beside = own[:group], own[group:]
    for message in received:
        pieces = [
            message[chans + i * group : chans + (i + 1) * group].astype(F32)
            for i in range(4)
        ]
        main = main + (pieces[0] + pieces[1])
        beside = beside + (pieces[2] + pieces[3])
    tall = count_y * size_y
    width = 16

    def extended(s):
        found = []
        for values in (main, beside):
            for x in range(size_x):
                part = values[x * tall : (x + 1) * tall]
                found.append(rolled(part, 1 - s * size_y, 0)[:width])
        return jnp.concatenate(found, axis=0)

    tile_out, own_out = outs[0], outs[1]
    tile_out[...] = tile
    own_out[...] = extended(0)
    for s in range(1, count_y):
        message = outs[1 + s]
        high, low = halves(extended(s))
        depth = high.shape[0]
        message[:depth] = high
        message[depth : 2 * depth] = low
        base = 2 * depth
        if s in (1, count_y - 1):
            message[base : base + chans] = tile
            base += chans
            first = size_y - 2 if s == 1 else 0
            for x in range(size_x):
                for y in range(first, first + 2):
                    message[base : base + chans] = planes[x][y]
                    base += chans


def pack_x_body(count_y, size_x, size_y, chans, tile, own, *refs):
    received = refs[: count_y - 1]
    dens, outs = refs[count_y - 1], refs[count_y:]
    depth = own.shape[0]
    total = own[...]
    for message in received:
        total = total + (
            message[:depth].astype(F32) + message[depth : 2 * depth].astype(F32)
        )
    dens[...] = total
    base = 2 * depth
    below, above = received[0], received[-1]
    size_z = tile.shape[1]
    lane = lanes_of((chans, size_z))
    mine = tile[...].astype(F32)
    low = below[base : base + chans].astype(F32)
    high = above[base : base + chans].astype(F32)
    base += chans
    for x in range(size_x):
        first = 4 * x * size_y
        edge = rolled(low, -(first + 4 * (size_y - 2)), 1)
        edge = jnp.where(lane < 8, edge, rolled(mine, 8 - first, 1))
        edge = jnp.where(
            lane < 8 + 4 * size_y, edge, rolled(high, 8 + 4 * size_y - first, 1)
        )
        out = outs[x]
        out[:chans] = edge.astype(BF16)
        start = base + 2 * x * chans
        out[chans : 3 * chans] = below[start : start + 2 * chans]
        out[3 * chans : 5 * chans] = above[start : start + 2 * chans]


def spread(tile, y, width, start):
    lane = lanes_of(tile.shape)
    size = tile.shape[1]
    turned = rolled(tile, size - 2 - 4 * y, 1)
    keep = (lane < 2) | (lane >= size - 2)
    return jnp.where(keep, turned, 0.0).astype(BF16)


def activate(values):
    return jnp.where(values >= 0, values, 0.2 * values) * jnp.sqrt(jnp.float32(2.0))


def column(stack, weights, columns, density, x, y, chans):
    taps = stack[pl.ds(x, 3), pl.ds(y, 3)]
    wide = taps.shape[-1]
    taps = taps.reshape(9 * chans, wide)
    found = jnp.dot(weights[...], taps, preferred_element_type=F32)
    summed = (
        pltpu.roll(found[:chans], 1, 1)
        + found[chans : 2 * chans]
        + pltpu.roll(found[2 * chans :], wide - 1, 1)
    )
    gain = jnp.concatenate([columns[1], columns[1]], axis=1)
    bias = jnp.concatenate([columns[0], columns[0]], axis=1)
    return activate(summed + gain * density + bias)


def first_body(size_x, size_y, *refs):
    own = refs[:size_x]
    edges = refs[size_x : 2 * size_x]
    main_below, main_above, edge_below, edge_above = refs[2 * size_x : 2 * size_x + 4]
    dens, weights, columns = refs[2 * size_x + 4 : 2 * size_x + 7]
    hidden, low_out, high_out, stack, dense, tiles = refs[2 * size_x + 7 :]
    chans, size_z = own[0].shape[1:]
    tall = size_y + 4
    planes = (
        [(main_below, edge_below)] + list(zip(own, edges)) + [(main_above, edge_above)]
    )
    for at, (main, edge) in enumerate(planes):
        stack[at, 2 : 2 + size_y, :, :size_z] = main[...]
        tile = edge[:chans].astype(F32)
        for i, y in enumerate((0, 1, tall - 2, tall - 1)):
            stack[at, y, :, :size_z] = edge[(1 + i) * chans : (2 + i) * chans]
        for y in range(tall):
            stack[at, y, :, size_z:] = spread(tile, y, size_z, 0)
    width = 16
    for x in range(size_x):
        dense[x * width : (x + 1) * width, :size_z] = dens[x * width : (x + 1) * width]
        other = (size_x + x) * width
        dense[x * width : (x + 1) * width, size_z:] = dens[other : other + width]
    lane = lanes_of((chans, size_z))
    for x in range(size_x):
        tiles[...] = jnp.zeros_like(tiles)

        def step(y, carry):
            density = dense[pl.ds(x * width + y, 1), :]
            found = column(stack, weights, columns, density, x, y, chans).astype(BF16)
            hidden[x, y] = found
            beside = found[:, size_z:].astype(F32)
            turned = pltpu.roll(beside, 4 * y + 2, 1)
            keep = (lane >= 4 * y) & (lane < 4 * y + 4)
            tiles[...] = jnp.where(keep, turned, tiles[...])
            return carry

        lax.fori_loop(0, size_y + 2, step, 0)
        out = {0: low_out, size_x - 1: high_out}.get(x)
        if out is not None:
            out[:chans] = tiles[...].astype(BF16)
            for y in range(size_y + 2):
                out[(1 + y) * chans : (2 + y) * chans] = hidden[x, y, :, :size_z]


def second_body(size_x, size_y, hidden, below, above, dens, weights, columns, *refs):
    out, stack, dense, turned = refs
    chans = hidden.shape[2]
    size_z = hidden.shape[3] // 2
    tall = size_y + 2
    stack[1 : 1 + size_x] = hidden[...]
    for at, message in ((0, below), (size_x + 1, above)):
        tile = message[:chans].astype(F32)
        for y in range(tall):
            stack[at, y, :, :size_z] = message[(1 + y) * chans : (2 + y) * chans]
            stack[at, y, :, size_z:] = spread(tile, y, size_z, 0)
    width = 16
    for x in range(size_x):
        dense[x * width : (x + 1) * width, :size_z] = dens[x * width : (x + 1) * width]
        dense[x * width : (x + 1) * width, size_z:] = jnp.zeros((width, size_z), F32)
    for x in range(size_x):

        def step(y, carry):
            density = dense[pl.ds(x * width + y + 1, 1), :]
            found = column(stack, weights, columns, density, x, y, chans)
            turned[y] = found[:, :size_z]
            return carry

        lax.fori_loop(0, size_y, step, 0)
        out[:, x] = jnp.swapaxes(turned[...], 0, 1).astype(BF16)


def shards(
    features,
    dest_bricks,
    cell_ids,
    cic_masses,
    live_counts,
    style_vector,
    affine_first,
    kernel_first,
    bias_first,
    gain_first,
    affine_second,
    kernel_second,
    bias_second,
    gain_second,
):
    chans, size_x, size_y, size_z = features.shape
    count_y, count_z = lax.axis_size("gy"), lax.axis_size("gz")
    group = size_x * count_y * size_y
    depth = 2 * size_x * 16
    planes = call(
        split_body, [((size_y, chans, size_z), BF16)] * size_x, "split"
    )(features)
    main_below = shift(planes[-1], "gx", 1)
    main_above = shift(planes[0], "gx", -1)
    where = jnp.stack([lax.axis_index("gy"), lax.axis_index("gz")]).astype(jnp.int32)
    painted = call(
        functools.partial(paint_body, range(size_x), (count_y, count_z)),
        [((chans + 4 * group, size_z), BF16)] * (count_z - 1)
        + [((2 * group, size_z), F32)],
        "paint",
        smem=(0, 1),
    )(where, live_counts, dest_bricks, cell_ids, cic_masses, *planes)
    from_z = [shift(painted[s - 1], "gz", s) for s in range(1, count_z)]
    rows = [
        2 * depth + ((1 + 2 * size_x) * chans if s in (1, count_y - 1) else 0)
        for s in range(1, count_y)
    ]
    packed = call(
        functools.partial(pack_y_body, count_y, count_z, size_x),
        [((chans, size_z), BF16), ((depth, size_z), F32)]
        + [((r, size_z), BF16) for r in rows],
        "pack_y",
    )(*planes, painted[-1], *from_z)
    from_y = [shift(packed[1 + s], "gy", s) for s in range(1, count_y)]
    weights = []
    for args in (
        (affine_first, kernel_first, bias_first, gain_first),
        (affine_second, kernel_second, bias_second, gain_second),
    ):
        affine, kernel, bias, gain = args
        weights.append(
            call(
                modulate_body,
                [((3 * chans, 9 * chans), BF16), ((2, chans, size_z), F32)],
                "modulate",
            )(
                style_vector[None, :],
                affine,
                kernel,
                bias[None, :],
                gain[None, :],
            )
        )
    edges = call(
        functools.partial(pack_x_body, count_y, size_x, size_y, chans),
        [((depth, size_z), F32)] + [((5 * chans, size_z), BF16)] * size_x,
        "pack_x",
    )(packed[0], packed[1], *from_y)
    dens, edges = edges[0], edges[1:]
    edge_below = shift(edges[-1], "gx", 1)
    edge_above = shift(edges[0], "gx", -1)
    flops = 2 * 27 * chans * chans * 2 * size_z
    hidden, low, high = call(
        functools.partial(first_body, size_x, size_y),
        [
            ((size_x, size_y + 2, chans, 2 * size_z), BF16),
            (((size_y + 3) * chans, size_z), BF16),
            (((size_y + 3) * chans, size_z), BF16),
        ],
        "first",
        flops=flops * size_x * (size_y + 2),
        scratch=[
            pltpu.VMEM((size_x + 2, size_y + 4, chans, 2 * size_z), BF16),
            pltpu.VMEM((size_x * 16, 2 * size_z), F32),
            pltpu.VMEM((chans, size_z), F32),
        ],
    )(
        *planes,
        *edges,
        main_below,
        main_above,
        edge_below,
        edge_above,
        dens,
        *weights[0],
    )
    hidden_below = shift(high, "gx", 1)
    hidden_above = shift(low, "gx", -1)
    (result,) = call(
        functools.partial(second_body, size_x, size_y),
        [((chans, size_x, size_y, size_z), BF16)],
        "second",
        flops=flops * size_x * size_y,
        scratch=[
            pltpu.VMEM((size_x + 2, size_y + 2, chans, 2 * size_z), BF16),
            pltpu.VMEM((size_x * 16, 2 * size_z), F32),
            pltpu.VMEM((size_y, chans, size_z), F32),
        ],
    )(hidden, hidden_below, hidden_above, dens, *weights[1])
    return result


def solution(mesh):
    return jax.shard_map(
        shards,
        mesh=mesh,
        in_specs=(
            P(None, "gx", "gy", "gz"),
            P(("gx", "gy", "gz"), None),
            P(("gx", "gy", "gz"), None),
            P(("gx", "gy", "gz"), None),
            P(("gx", "gy", "gz")),
        )
        + (P(),) * 9,
        out_specs=P(None, "gx", "gy", "gz"),
        check_vma=False,
    )
```

time: 150 us -> 62.7 us (0.42); the launches traced: 148 us -> 62.4 us
  local copies, waits for them, and re-layouts: 48 us -> 5.76 us
  Pallas kernels: 0 us -> 30.3 us
  waiting for transfers between devices: 36.5 us -> 6.81 us
  between operations: 15.1 us -> 0.74 us
  other arithmetic: 13.4 us -> 0.58 us
  blocking collectives: 10.6 us -> 0 us
  matrix products: 7.49 us -> 0 us
    pallas_call x0 -> x8, Pallas kernels: none -> 30.3 us  [run(): pl.pallas_call(body, out_shape=tuple((jax.ShapeDtypeStruct(s, d) for s, d...]
    unnamed x2 -> x0, waiting for transfers between devices: 26.3 us -> none
    transpose x20 -> x0, local copies, waits for them, and re-layouts: 11.6 us -> none  [convolve(): matrix = modulated[first_offset:first_offset + 3].transpose(1, 0, 2).resh...]
    unnamed x1 -> x0, blocking collectives: 10.6 us -> none
    concatenate x19 -> x0, local copies, waits for them, and re-layouts: 9.24 us -> none  [the longest x18 9.22 us: convolve(): jnp.concatenate([padded[:, offset_x:offset_x + out_x, offset_y:offset_y +...]
    dot_general x24 -> x0, matrix products: 7.49 us -> none  [the longest x18 5.18 us: convolve(): jnp.dot(matrix, stacked, preferred_element_type=jnp.float32)]
    unnamed x93 -> x33, local copies, waits for them, and re-layouts: 12.9 us -> 5.76 us
    concatenate x19 -> x0, other arithmetic: 4.97 us -> none  [the longest x6 3.58 us: extended(): jnp.concatenate([lax.ppermute(tail, axis, [(i, (i + 1) % count) for i in...]
  transfers between devices with their start and end apart: 13 -> 10, of which waited for: 8 -> 3; matrix products, arithmetic and copies ran while one was open for 24% -> 3% of each run, Pallas kernels for 0% -> 11%
where the time goes in v1:
time: 62.7 us; the launch traced here: 62.4 us
  Pallas kernels  30.3 us (48%)
  starting transfers between devices  18.2 us (29%)
  waiting for transfers between devices  6.81 us (11%)
  local copies, waits for them, and re-layouts  5.76 us (9%)
  between operations  0.74 us (1%)
    pallas_call x8, Pallas kernels, run(): pl.pallas_call(body, out_shape=tuple((jax.ShapeDtypeStruct(s, d) for s, d...  30.3 us
    ppermute x10, starting transfers between devices, shift(): lax.ppermute(cells, axis, [(i, (i + step) % count) for i in range(count)])  18.2 us
    ppermute x10, waiting for transfers between devices, shift(): lax.ppermute(cells, axis, [(i, (i + step) % count) for i in range(count)])  6.81 us
    unnamed x33, local copies, waits for them, and re-layouts  5.76 us
  transfers between devices with their start and end apart: 10, of which 3 were waited for; matrix products, arithmetic and copies ran while one was open for 3% of the time, Pallas kernels for 11%

profile of v1, /device:TPU:0, one launch (start us, length us, event | category | flops | bytes accessed | tf_op | source)
XLA Modules:
  0.0 62.4 jit_solution(180260176337053804)
XLA Ops:
  0.0 1.7 %split.1 = (bf16[8,64,128]{2,1,0:T(8,128)(2,1)}, bf16[8,64,128]{2,1,0:T(8,128)(2,1)}) custom-call(bf16[64,2,8,128]{3,2,1,0:T(8,128)(2,1)} %cells.2), custom_call_target="tpu_custom_call" | custom-call | bytes 262144 | tf_op jit(solution)/shard_map/split/pallas_call | solution.py:27
  1.7 0.7 %copy-done.8 = s32[32,1]{0,1:T(1,128)S(1)} copy-done((s32[32,1]{0,1:T(1,128)S(1)}, s32[32,1]{0,1:T(1,128)}, u32[]{:S(2)}) %copy-start.8) | copy-done | bytes 152
  2.4 0.7 %copy.15.dest = s32[32,1]{1,0:T(8,128)} copy(s32[32,1]{0,1:T(1,128)S(1)} %copy-done.8) | data formatting | bytes 256 | tf_op args[1]
  4.3 2.2 %paint.1 = (bf16[320,128]{1,0:T(8,128)(2,1)}, f32[128,128]{1,0:T(8,128)}) custom-call(s32[2]{0:T(128)} %pad_add_fusion.where, s32[1]{0:T(128)S(6)} %copy.18.live, s32[32,1]{1,0:T(8,128)} %copy.15.dest, s32[32,64]{1,0:T(8,128)} %cells.3, bf16[32,64]{1,0:T(8,128)(2,1)} %masses.1, bf16[8,64,128]{2,1,0:T(8,128)(2,1)} %get-tuple-element.24.refs_0_, ...), custom_call_target="tpu_custom_call" | custom-call | bytes 274572 | tf_op jit(solution)/shard_map/paint/pallas_call | solution.py:27
  6.5 3.0 %collective-permute-start = (bf16[320,128]{1,0:T(8,128)(2,1)}, bf16[320,128]{1,0:T(8,128)(2,1)S(1)}, u32[]{:S(2)}, u32[]{:S(2)}) collective-permute-start(bf16[320,128]{1,0:T(8,128)(2,1)} %get-tuple-element.27), channel_id=1, source_target_pairs={{0,1},{1,0},{2,3},{3,2},{4,5},{5,4},{6,7},{7,6},{8,9},{9,8},{10,11... | collective-permute-start | bytes 245768 | tf_op jit(solution)/shard_map/ppermute | solution.py:17
  9.4 2.7 %collective-permute-done.refs_3_ = bf16[320,128]{1,0:T(8,128)(2,1)S(1)} collective-permute-done((bf16[320,128]{1,0:T(8,128)(2,1)}, bf16[320,128]{1,0:T(8,128)(2,1)S(1)}, u32[]{:S(2)}, u32[]{:S(2)}) %collective-permute-start) | collective-permute-done | bytes 81952 | tf_op jit(solution)/shard_map/ppermute | solution.py:17
  12.1 0.6 %copy-done.6 = bf16[320,128]{1,0:T(8,128)(2,1)} copy-done((bf16[320,128]{1,0:T(8,128)(2,1)}, bf16[320,128]{1,0:T(8,128)(2,1)S(1)}, u32[]{:S(2)}) %copy-start.6) | copy-done | bytes 81944
  12.7 1.8 %pack_y.1 = (bf16[64,128]{1,0:T(8,128)(2,1)}, f32[64,128]{1,0:T(8,128)}, bf16[448,128]{1,0:T(8,128)(2,1)}, bf16[128,128]{1,0:T(8,128)(2,1)}, bf16[448,128]{1,0:T(8,128)(2,1)}) custom-call(bf16[8,64,128]{2,1,0:T(8,128)(2,1)} %get-tuple-element.24.refs_0_, bf16[8,64,128]{2,1,0:T(8,128)(2,1)} %get-tuple-element.25.refs_1_, ...), custom_call_target="tpu_custom_call" | custom-call | bytes 409600 | tf_op jit(solution)/shard_map/pack_y/pallas_call | solution.py:27
  14.5 1.7 %collective-permute-start.3 = (bf16[448,128]{1,0:T(8,128)(2,1)}, bf16[448,128]{1,0:T(8,128)(2,1)S(1)}, u32[]{:S(2)}, u32[]{:S(2)}) collective-permute-start(bf16[448,128]{1,0:T(8,128)(2,1)} %get-tuple-element.32), channel_id=1, source_target_pairs={{0,6},{2,0},{4,2},{6,4},{1,7},{3,1},{5,3},{7,5},{8,14},{10,8},{12,... | collective-permute-start | bytes 344072 | tf_op jit(solution)/shard_map/ppermute | solution.py:17
  16.3 2.1 %collective-permute-start.4 = (bf16[8,64,128]{2,1,0:T(8,128)(2,1)S(1)}, bf16[8,64,128]{2,1,0:T(8,128)(2,1)S(1)}, u32[]{:S(2)}, u32[]{:S(2)}) collective-permute-start(bf16[8,64,128]{2,1,0:T(8,128)(2,1)S(1)} %copy-done.1), channel_id=1, source_target_pairs={{0,8},{8,16},{16,24},{24,0},{1,9},{9,17},{17,25},{25,1},{2,10},{10... | collective-permute-start | bytes 393224 | tf_op jit(solution)/shard_map/ppermute | solution.py:17
  18.4 2.1 %collective-permute-start.5 = (bf16[8,64,128]{2,1,0:T(8,128)(2,1)S(1)}, bf16[8,64,128]{2,1,0:T(8,128)(2,1)S(1)}, u32[]{:S(2)}, u32[]{:S(2)}) collective-permute-start(bf16[8,64,128]{2,1,0:T(8,128)(2,1)S(1)} %copy-done), channel_id=1, source_target_pairs={{0,24},{8,0},{16,8},{24,16},{1,25},{9,1},{17,9},{25,17},{2,26},{10... | collective-permute-start | bytes 393224 | tf_op jit(solution)/shard_map/ppermute | solution.py:17
  20.5 1.7 %collective-permute-start.2 = (bf16[128,128]{1,0:T(8,128)(2,1)}, bf16[128,128]{1,0:T(8,128)(2,1)S(1)}, u32[]{:S(2)}, u32[]{:S(2)}) collective-permute-start(bf16[128,128]{1,0:T(8,128)(2,1)} %get-tuple-element.31), channel_id=1, source_target_pairs={{0,4},{2,6},{4,0},{6,2},{1,5},{3,7},{5,1},{7,3},{8,12},{10,14},{12... | collective-permute-start | bytes 98312 | tf_op jit(solution)/shard_map/ppermute | solution.py:17
  22.1 2.4 %collective-permute-done.2.refs_1_ = bf16[128,128]{1,0:T(8,128)(2,1)S(1)} collective-permute-done((bf16[128,128]{1,0:T(8,128)(2,1)}, bf16[128,128]{1,0:T(8,128)(2,1)S(1)}, u32[]{:S(2)}, u32[]{:S(2)}) %collective-permute-start.2) | collective-permute-done | bytes 32800 | tf_op jit(solution)/shard_map/ppermute | solution.py:17
  25.3 1.8 %pack_x.1 = (f32[64,128]{1,0:T(8,128)}, bf16[320,128]{1,0:T(8,128)(2,1)}, bf16[320,128]{1,0:T(8,128)(2,1)}) custom-call(bf16[64,128]{1,0:T(8,128)(2,1)} %get-tuple-element.28.tile, f32[64,128]{1,0:T(8,128)} %get-tuple-element.29.own, bf16[448,128]{1,0:T(8,128)(2,1)} %copy-done.4, bf16[128,128]{1,0:T(8,128)(2,1)} %copy-done.7, bf16[448,128]{1,0:T(8,128)(2,1)} %copy-done.5), custom_call_target="tpu_custom_call" | custom-call | bytes 311296 | tf_op jit(solution)/shard_map/pack_x/pallas_call | solution.py:27
  27.1 3.8 %collective-permute-start.7 = (bf16[320,128]{1,0:T(8,128)(2,1)}, bf16[320,128]{1,0:T(8,128)(2,1)S(1)}, u32[]{:S(2)}, u32[]{:S(2)}) collective-permute-start(bf16[320,128]{1,0:T(8,128)(2,1)} %get-tuple-element.33.refs_2_), channel_id=1, source_target_pairs={{0,24},{8,0},{16,8},{24,16},{1,25},{9,1},{17,9},{25,17},{2,26},{10... | collective-permute-start | bytes 245768 | tf_op jit(solution)/shard_map/ppermute | solution.py:17
  30.9 0.8 %copy.16.affine = f32[512,64]{1,0:T(8,128)} copy(f32[512,64]{0,1:T(8,128)S(1)} %copy-done.2) | data formatting | bytes 262144 | tf_op args[6]
  31.7 2.4 %modulate.2 = (bf16[192,576]{1,0:T(8,128)(2,1)}, f32[2,64,128]{2,1,0:T(8,128)}) custom-call(f32[1,512]{1,0:T(1,128)} %bitcast.7, f32[512,64]{1,0:T(8,128)} %copy.16.affine, bf16[27,64,64]{2,1,0:T(8,128)(2,1)} %kernel.2, f32[1,64]{1,0:T(1,128)} %bitcast.9, f32[1,64]{1,0:T(1,128)} %bitcast.10), custom_call_target="tpu_custom_call" | custom-call | bytes 354816 | tf_op jit(solution)/shard_map/modulate/pallas_call | solution.py:27
  34.9 10.4 %first.1 = (bf16[2,10,64,256]{3,2,1,0:T(8,128)(2,1)}, bf16[704,128]{1,0:T(8,128)(2,1)}, bf16[704,128]{1,0:T(8,128)(2,1)}) custom-call(bf16[8,64,128]{2,1,0:T(8,128)(2,1)} %get-tuple-element.24.refs_0_, bf16[8,64,128]{2,1,0:T(8,128)(2,1)} %get-tuple-element.25.refs_1_, bf16[320,128]{1,0:T(8,128)(2,1)} %get-tuple-element.33.refs_2_, ...), custom_call_target="tpu_custom_call" | custom-call | flops 1132462080 | bytes 1171456 | tf_op jit(solution)/shard_map/first/pallas_call | solution.py:27
  45.3 3.8 %collective-permute-start.9 = (bf16[704,128]{1,0:T(8,128)(2,1)}, bf16[704,128]{1,0:T(8,128)(2,1)S(1)}, u32[]{:S(2)}, u32[]{:S(2)}) collective-permute-start(bf16[704,128]{1,0:T(8,128)(2,1)} %get-tuple-element.40), channel_id=1, source_target_pairs={{0,24},{8,0},{16,8},{24,16},{1,25},{9,1},{17,9},{25,17},{2,26},{10... | collective-permute-start | bytes 540680 | tf_op jit(solution)/shard_map/ppermute | solution.py:17
  49.2 0.8 %copy.17.affine = f32[512,64]{1,0:T(8,128)} copy(f32[512,64]{0,1:T(8,128)S(1)} %copy-done.3) | data formatting | bytes 262144 | tf_op args[10]
  50.0 2.4 %modulate.3 = (bf16[192,576]{1,0:T(8,128)(2,1)}, f32[2,64,128]{2,1,0:T(8,128)}) custom-call(f32[1,512]{1,0:T(1,128)} %bitcast.8, f32[512,64]{1,0:T(8,128)} %copy.17.affine, bf16[27,64,64]{2,1,0:T(8,128)(2,1)} %kernel.3, f32[1,64]{1,0:T(1,128)} %bitcast.11, f32[1,64]{1,0:T(1,128)} %bitcast.12), custom_call_target="tpu_custom_call" | custom-call | bytes 354816 | tf_op jit(solution)/shard_map/modulate/pallas_call | solution.py:27
  52.4 1.7 %collective-permute-done.8.below = bf16[704,128]{1,0:T(8,128)(2,1)S(1)} collective-permute-done((bf16[704,128]{1,0:T(8,128)(2,1)}, bf16[704,128]{1,0:T(8,128)(2,1)S(1)}, u32[]{:S(2)}, u32[]{:S(2)}) %collective-permute-start.8) | collective-permute-done | bytes 180256 | tf_op jit(solution)/shard_map/ppermute | solution.py:17
  54.1 0.7 %copy-done.9 = bf16[704,128]{1,0:T(8,128)(2,1)} copy-done((bf16[704,128]{1,0:T(8,128)(2,1)}, bf16[704,128]{1,0:T(8,128)(2,1)S(1)}, u32[]{:S(2)}) %copy-start.9) | copy-done | bytes 180248
  54.8 7.5 %second.1 = bf16[64,2,8,128]{3,2,1,0:T(8,128)(2,1)} custom-call(bf16[2,10,64,256]{3,2,1,0:T(8,128)(2,1)} %get-tuple-element.38.hidden, bf16[704,128]{1,0:T(8,128)(2,1)} %copy-done.9, bf16[704,128]{1,0:T(8,128)(2,1)} %copy-done.10, f32[64,128]{1,0:T(8,128)} %get-tuple-element.35.refs_8_.dens, bf16[192,576]{1,0:T(8,128)(2,1)} %get-tuple-element.41.weights, ...), custom_call_target="tpu_custom_call" | custom-call | flops 905969664 | bytes 1335296 | tf_op jit(solution)/shard_map/second/pallas_call | solution.py:27
  (38 shorter events, 2.1 us)
Async XLA Ops:
  1.7 0.7 %copy-start.8 = (s32[32,1]{0,1:T(1,128)S(1)}, s32[32,1]{0,1:T(1,128)}, u32[]{:S(2)}) copy-start(s32[32,1]{0,1:T(1,128)} %param.15) | copy-start | bytes 388
  6.5 5.6 %collective-permute-start = (bf16[320,128]{1,0:T(8,128)(2,1)}, bf16[320,128]{1,0:T(8,128)(2,1)S(1)}, u32[]{:S(2)}, u32[]{:S(2)}) collective-permute-start(bf16[320,128]{1,0:T(8,128)(2,1)} %get-tuple-element.27), channel_id=1, source_target_pairs={{0,1},{1,0},{2,3},{3,2},{4,5},{5,4},{6,7},{7,6},{8,9},{9,8},{10,11... | collective-permute-start | bytes 245768 | tf_op jit(solution)/shard_map/ppermute | solution.py:17
  12.1 0.6 %copy-start.6 = (bf16[320,128]{1,0:T(8,128)(2,1)}, bf16[320,128]{1,0:T(8,128)(2,1)S(1)}, u32[]{:S(2)}) copy-start(bf16[320,128]{1,0:T(8,128)(2,1)S(1)} %collective-permute-done.refs_3_) | copy-start | bytes 245764
  12.7 3.6 %copy-start.1 = (bf16[8,64,128]{2,1,0:T(8,128)(2,1)S(1)}, bf16[8,64,128]{2,1,0:T(8,128)(2,1)}, u32[]{:S(2)}) copy-start(bf16[8,64,128]{2,1,0:T(8,128)(2,1)} %get-tuple-element.25.refs_1_) | copy-start | bytes 393220
  12.7 5.7 %copy-start = (bf16[8,64,128]{2,1,0:T(8,128)(2,1)S(1)}, bf16[8,64,128]{2,1,0:T(8,128)(2,1)}, u32[]{:S(2)}) copy-start(bf16[8,64,128]{2,1,0:T(8,128)(2,1)} %get-tuple-element.24.refs_0_) | copy-start | bytes 393220
  14.5 10.1 %collective-permute-start.1 = (bf16[448,128]{1,0:T(8,128)(2,1)}, bf16[448,128]{1,0:T(8,128)(2,1)S(1)}, u32[]{:S(2)}, u32[]{:S(2)}) collective-permute-start(bf16[448,128]{1,0:T(8,128)(2,1)} %get-tuple-element.30), channel_id=1, source_target_pairs={{0,2},{2,4},{4,6},{6,0},{1,3},{3,5},{5,7},{7,1},{8,10},{10,12},{12... | collective-permute-start | bytes 344072 | tf_op jit(solution)/shard_map/ppermute | solution.py:17
  14.5 10.1 %collective-permute-start.3 = (bf16[448,128]{1,0:T(8,128)(2,1)}, bf16[448,128]{1,0:T(8,128)(2,1)S(1)}, u32[]{:S(2)}, u32[]{:S(2)}) collective-permute-start(bf16[448,128]{1,0:T(8,128)(2,1)} %get-tuple-element.32), channel_id=1, source_target_pairs={{0,6},{2,0},{4,2},{6,4},{1,7},{3,1},{5,3},{7,5},{8,14},{10,8},{12,... | collective-permute-start | bytes 344072 | tf_op jit(solution)/shard_map/ppermute | solution.py:17
  16.3 17.8 %collective-permute-start.4 = (bf16[8,64,128]{2,1,0:T(8,128)(2,1)S(1)}, bf16[8,64,128]{2,1,0:T(8,128)(2,1)S(1)}, u32[]{:S(2)}, u32[]{:S(2)}) collective-permute-start(bf16[8,64,128]{2,1,0:T(8,128)(2,1)S(1)} %copy-done.1), channel_id=1, source_target_pairs={{0,8},{8,16},{16,24},{24,0},{1,9},{9,17},{17,25},{25,1},{2,10},{10... | collective-permute-start | bytes 393224 | tf_op jit(solution)/shard_map/ppermute | solution.py:17
  18.4 15.8 %collective-permute-start.5 = (bf16[8,64,128]{2,1,0:T(8,128)(2,1)S(1)}, bf16[8,64,128]{2,1,0:T(8,128)(2,1)S(1)}, u32[]{:S(2)}, u32[]{:S(2)}) collective-permute-start(bf16[8,64,128]{2,1,0:T(8,128)(2,1)S(1)} %copy-done), channel_id=1, source_target_pairs={{0,24},{8,0},{16,8},{24,16},{1,25},{9,1},{17,9},{25,17},{2,26},{10... | collective-permute-start | bytes 393224 | tf_op jit(solution)/shard_map/ppermute | solution.py:17
  20.5 4.1 %collective-permute-start.2 = (bf16[128,128]{1,0:T(8,128)(2,1)}, bf16[128,128]{1,0:T(8,128)(2,1)S(1)}, u32[]{:S(2)}, u32[]{:S(2)}) collective-permute-start(bf16[128,128]{1,0:T(8,128)(2,1)} %get-tuple-element.31), channel_id=1, source_target_pairs={{0,4},{2,6},{4,0},{6,2},{1,5},{3,7},{5,1},{7,3},{8,12},{10,14},{12... | collective-permute-start | bytes 98312 | tf_op jit(solution)/shard_map/ppermute | solution.py:17
  24.6 0.7 %copy-start.4 = (bf16[448,128]{1,0:T(8,128)(2,1)}, bf16[448,128]{1,0:T(8,128)(2,1)S(1)}, u32[]{:S(2)}) copy-start(bf16[448,128]{1,0:T(8,128)(2,1)S(1)} %collective-permute-done.1.refs_0_) | copy-start | bytes 344068
  24.6 0.7 %copy-start.5 = (bf16[448,128]{1,0:T(8,128)(2,1)}, bf16[448,128]{1,0:T(8,128)(2,1)S(1)}, u32[]{:S(2)}) copy-start(bf16[448,128]{1,0:T(8,128)(2,1)S(1)} %collective-permute-done.3.refs_2_) | copy-start | bytes 344068
  25.3 5.6 %copy-start.2 = (f32[512,64]{0,1:T(8,128)S(1)}, f32[512,64]{0,1:T(8,128)}, u32[]{:S(2)}) copy-start(f32[512,64]{0,1:T(8,128)} %param.20) | copy-start | bytes 393220
  27.1 7.1 %collective-permute-start.6 = (bf16[320,128]{1,0:T(8,128)(2,1)}, bf16[320,128]{1,0:T(8,128)(2,1)S(1)}, u32[]{:S(2)}, u32[]{:S(2)}) collective-permute-start(bf16[320,128]{1,0:T(8,128)(2,1)} %get-tuple-element.34.refs_3_), channel_id=1, source_target_pairs={{0,8},{8,16},{16,24},{24,0},{1,9},{9,17},{17,25},{25,1},{2,10},{10... | collective-permute-start | bytes 245768 | tf_op jit(solution)/shard_map/ppermute | solution.py:17
  27.1 7.1 %collective-permute-start.7 = (bf16[320,128]{1,0:T(8,128)(2,1)}, bf16[320,128]{1,0:T(8,128)(2,1)S(1)}, u32[]{:S(2)}, u32[]{:S(2)}) collective-permute-start(bf16[320,128]{1,0:T(8,128)(2,1)} %get-tuple-element.33.refs_2_), channel_id=1, source_target_pairs={{0,24},{8,0},{16,8},{24,16},{1,25},{9,1},{17,9},{25,17},{2,26},{10... | collective-permute-start | bytes 245768 | tf_op jit(solution)/shard_map/ppermute | solution.py:17
  34.1 0.7 %copy-start.11 = (bf16[8,64,128]{2,1,0:T(8,128)(2,1)}, bf16[8,64,128]{2,1,0:T(8,128)(2,1)S(1)}, u32[]{:S(2)}) copy-start(bf16[8,64,128]{2,1,0:T(8,128)(2,1)S(1)} %collective-permute-done.4.refs_4_) | copy-start | bytes 393220
  34.2 0.7 %copy-start.12 = (bf16[8,64,128]{2,1,0:T(8,128)(2,1)}, bf16[8,64,128]{2,1,0:T(8,128)(2,1)S(1)}, u32[]{:S(2)}) copy-start(bf16[8,64,128]{2,1,0:T(8,128)(2,1)S(1)} %collective-permute-done.5.refs_5_) | copy-start | bytes 393220
  34.2 0.7 %copy-start.13 = (bf16[320,128]{1,0:T(8,128)(2,1)}, bf16[320,128]{1,0:T(8,128)(2,1)S(1)}, u32[]{:S(2)}) copy-start(bf16[320,128]{1,0:T(8,128)(2,1)S(1)} %collective-permute-done.6.refs_6_) | copy-start | bytes 245764
  34.2 0.7 %copy-start.14 = (bf16[320,128]{1,0:T(8,128)(2,1)}, bf16[320,128]{1,0:T(8,128)(2,1)S(1)}, u32[]{:S(2)}) copy-start(bf16[320,128]{1,0:T(8,128)(2,1)S(1)} %collective-permute-done.7.refs_7_) | copy-start | bytes 245764
  34.9 14.3 %copy-start.3 = (f32[512,64]{0,1:T(8,128)S(1)}, f32[512,64]{0,1:T(8,128)}, u32[]{:S(2)}) copy-start(f32[512,64]{0,1:T(8,128)} %param.24) | copy-start | bytes 393220
  45.3 8.7 %collective-permute-start.8 = (bf16[704,128]{1,0:T(8,128)(2,1)}, bf16[704,128]{1,0:T(8,128)(2,1)S(1)}, u32[]{:S(2)}, u32[]{:S(2)}) collective-permute-start(bf16[704,128]{1,0:T(8,128)(2,1)} %get-tuple-element.39), channel_id=1, source_target_pairs={{0,8},{8,16},{16,24},{24,0},{1,9},{9,17},{17,25},{25,1},{2,10},{10... | collective-permute-start | bytes 540680 | tf_op jit(solution)/shard_map/ppermute | solution.py:17
  45.3 8.8 %collective-permute-start.9 = (bf16[704,128]{1,0:T(8,128)(2,1)}, bf16[704,128]{1,0:T(8,128)(2,1)S(1)}, u32[]{:S(2)}, u32[]{:S(2)}) collective-permute-start(bf16[704,128]{1,0:T(8,128)(2,1)} %get-tuple-element.40), channel_id=1, source_target_pairs={{0,24},{8,0},{16,8},{24,16},{1,25},{9,1},{17,9},{25,17},{2,26},{10... | collective-permute-start | bytes 540680 | tf_op jit(solution)/shard_map/ppermute | solution.py:17
  54.1 0.7 %copy-start.9 = (bf16[704,128]{1,0:T(8,128)(2,1)}, bf16[704,128]{1,0:T(8,128)(2,1)S(1)}, u32[]{:S(2)}) copy-start(bf16[704,128]{1,0:T(8,128)(2,1)S(1)} %collective-permute-done.8.below) | copy-start | bytes 540676
  54.1 0.7 %copy-start.10 = (bf16[704,128]{1,0:T(8,128)(2,1)}, bf16[704,128]{1,0:T(8,128)(2,1)S(1)}, u32[]{:S(2)}) copy-start(bf16[704,128]{1,0:T(8,128)(2,1)S(1)} %collective-permute-done.9.above) | copy-start | bytes 540676
  (1 other events, 0.6 us)

commit v2 on v1

--- a/solution.py
+++ b/solution.py
@@ -9,7 +9,6 @@
 
 F32 = jnp.float32
 BF16 = jnp.bfloat16
-SMEM = pltpu.SMEM
 
 
 def shift(cells, axis, step):
@@ -17,13 +16,10 @@
     return lax.ppermute(cells, axis, [(i, (i + step) % count) for i in range(count)])
 
 
-def call(body, outs, name, flops=0, smem=(), scratch=()):
+def call(body, outs, name, flops=0, scratch=(), limit=12):
     def run(*args):
         size = sum(a.size * a.dtype.itemsize for a in args)
-        specs = [
-            pl.BlockSpec(memory_space=SMEM if i in smem else pltpu.VMEM)
-            for i in range(len(args))
-        ]
+        specs = [pl.BlockSpec(memory_space=pltpu.VMEM) for _ in args]
         return pl.pallas_call(
             body,
             out_shape=tuple(jax.ShapeDtypeStruct(s, d) for s, d in outs),
@@ -31,6 +27,7 @@
             out_specs=tuple(pl.BlockSpec(memory_space=pltpu.VMEM) for _ in outs),
             scratch_shapes=list(scratch),
             name=name,
+            compiler_params=pltpu.CompilerParams(vmem_limit_bytes=limit << 20),
             cost_estimate=pl.CostEstimate(
                 flops=flops, bytes_accessed=size, transcendentals=0
             ),
@@ -53,55 +50,55 @@
     return high, (values - high.astype(F32)).astype(BF16)
 
 
-def split_body(cells, *planes):
-    for at, plane in enumerate(planes):
-        part = cells[:, at].astype(F32)
-        plane[...] = jnp.swapaxes(part, 0, 1).astype(BF16)
-
-
 def column_of(row):
     size = row.shape[1]
     wide = jnp.broadcast_to(row, (size, size))
     same = lax.broadcasted_iota(jnp.int32, (size, size), 0) == lanes_of((size, size))
-    return jnp.sum(jnp.where(same, wide, 0.0), axis=1, keepdims=True)
-
-
-def modulate_body(style, affine, kernel, bias, gain, weights, columns):
-    styles = (
-        jnp.dot(
-            style[...],
-            affine[...],
-            precision=lax.Precision.HIGHEST,
-            preferred_element_type=F32,
+    return jnp.sum(jnp.where(same, wide, jnp.zeros_like(wide)), axis=1, keepdims=True)
+
+
+def modulate_body(style, *refs):
+    for layer in range(2):
+        affine, kernel, bias, gain = refs[4 * layer : 4 * layer + 4]
+        weights, columns = refs[8 + 2 * layer : 10 + 2 * layer]
+        styles = (
+            lax.dot_general(
+                style[...],
+                affine[...],
+                (((1,), (1,)), ((), ())),
+                precision=lax.Precision.HIGHEST,
+                preferred_element_type=F32,
+            )
+            + 1.0
         )
-        + 1.0
-    )
-    chans = kernel.shape[1]
-    total = jnp.zeros((chans, kernel.shape[2]), F32)
-    for k in range(27):
-        scaled = kernel[k].astype(F32) * styles
-        total = total + scaled * scaled
-    demod = lax.rsqrt(jnp.sum(total, axis=1, keepdims=True) + 1e-08)
-    for g in range(3):
-        blocks = [
-            (kernel[3 * j + g].astype(F32) * styles * demod).astype(BF16)
-            for j in range(9)
-        ]
-        weights[g * chans : (g + 1) * chans, :] = jnp.concatenate(blocks, axis=1)
-    columns[0] = jnp.broadcast_to(column_of(bias[...]), columns.shape[1:])
-    columns[1] = jnp.broadcast_to(column_of(gain[...]), columns.shape[1:])
-
-
-def paint_body(rows_y, counts, where, live, dest, cells, masses, *refs):
-    count_y, count_z = counts
-    size_x = len(rows_y)
+        chans = kernel.shape[1]
+        total = jnp.zeros((chans, kernel.shape[2]), F32)
+        for k in range(27):
+            scaled = kernel[k].astype(F32) * styles
+            total = total + scaled * scaled
+        demod = lax.rsqrt(jnp.sum(total, axis=1, keepdims=True) + 1e-08)
+        for g in range(3):
+            blocks = [
+                (kernel[3 * j + g].astype(F32) * styles * demod).astype(BF16)
+                for j in range(9)
+            ]
+            weights[g * chans : (g + 1) * chans, :] = jnp.concatenate(blocks, axis=1)
+        columns[0] = jnp.broadcast_to(column_of(bias[...]), columns.shape[1:])
+        columns[1] = jnp.broadcast_to(column_of(gain[...]), columns.shape[1:])
+
+
+def paint_body(count_y, count_z, features, live, dest, cells, masses, *refs):
+    size_x = features.shape[1]
     planes, messages, own = refs[:size_x], refs[size_x:-1], refs[-1]
+    for at, plane in enumerate(planes):
+        part = features[:, at].astype(F32)
+        plane[...] = jnp.swapaxes(part, 0, 1).astype(BF16)
     size_y, chans, size_z = planes[0].shape
     blocks, per = cells.shape
     half = blocks // 2
-    rank_y, rank_z = where[0], where[1]
+    rank_y, rank_z = lax.axis_index("gy"), lax.axis_index("gz")
     shape = (blocks, per)
-    target = jnp.broadcast_to(dest[...], shape)
+    target = jnp.broadcast_to(column_of(dest[...]), shape)
     to_y = lax.div(target, jnp.full(shape, count_z, jnp.int32))
     to_z = target - to_y * count_z - rank_z
     to_y = to_y - rank_y
@@ -113,7 +110,7 @@
     at_x = lax.div(cell_row, jnp.full(shape, size_y, jnp.int32))
     at_y = cell_row - at_x * size_y
     row = ((to_z * size_x + at_x) * count_y + to_y) * size_y + at_y
-    alive = lax.broadcasted_iota(jnp.int32, shape, 0) < live[0]
+    alive = lax.broadcasted_iota(jnp.int32, shape, 0) < jnp.broadcast_to(live[...], shape)
     mass = jnp.where(alive, masses[...].astype(F32), 0.0)
 
     def paired(values):
@@ -310,7 +307,7 @@
             tiles[...] = jnp.where(keep, turned, tiles[...])
             return carry
 
-        lax.fori_loop(0, size_y + 2, step, 0)
+        [step(y, 0) for y in range(size_y + 2)]
         out = {0: low_out, size_x - 1: high_out}.get(x)
         if out is not None:
             out[:chans] = tiles[...].astype(BF16)
@@ -341,7 +338,7 @@
             turned[y] = found[:, :size_z]
             return carry
 
-        lax.fori_loop(0, size_y, step, 0)
+        [step(y, 0) for y in range(size_y)]
         out[:, x] = jnp.swapaxes(turned[...], 0, 1).astype(BF16)
 
 
@@ -365,19 +362,16 @@
     count_y, count_z = lax.axis_size("gy"), lax.axis_size("gz")
     group = size_x * count_y * size_y
     depth = 2 * size_x * 16
-    planes = call(
-        split_body, [((size_y, chans, size_z), BF16)] * size_x, "split"
-    )(features)
+    painted = call(
+        functools.partial(paint_body, count_y, count_z),
+        [((size_y, chans, size_z), BF16)] * size_x
+        + [((chans + 4 * group, size_z), BF16)] * (count_z - 1)
+        + [((2 * group, size_z), F32)],
+        "paint",
+    )(features, live_counts[None, :], dest_bricks.T, cell_ids, cic_masses)
+    planes, painted = painted[:size_x], painted[size_x:]
     main_below = shift(planes[-1], "gx", 1)
     main_above = shift(planes[0], "gx", -1)
-    where = jnp.stack([lax.axis_index("gy"), lax.axis_index("gz")]).astype(jnp.int32)
-    painted = call(
-        functools.partial(paint_body, range(size_x), (count_y, count_z)),
-        [((chans + 4 * group, size_z), BF16)] * (count_z - 1)
-        + [((2 * group, size_z), F32)],
-        "paint",
-        smem=(0, 1),
-    )(where, live_counts, dest_bricks, cell_ids, cic_masses, *planes)
     from_z = [shift(painted[s - 1], "gz", s) for s in range(1, count_z)]
     rows = [
         2 * depth + ((1 + 2 * size_x) * chans if s in (1, count_y - 1) else 0)
@@ -390,25 +384,22 @@
         "pack_y",
     )(*planes, painted[-1], *from_z)
     from_y = [shift(packed[1 + s], "gy", s) for s in range(1, count_y)]
-    weights = []
-    for args in (
-        (affine_first, kernel_first, bias_first, gain_first),
-        (affine_second, kernel_second, bias_second, gain_second),
-    ):
-        affine, kernel, bias, gain = args
-        weights.append(
-            call(
-                modulate_body,
-                [((3 * chans, 9 * chans), BF16), ((2, chans, size_z), F32)],
-                "modulate",
-            )(
-                style_vector[None, :],
-                affine,
-                kernel,
-                bias[None, :],
-                gain[None, :],
-            )
-        )
+    modulated = call(
+        modulate_body,
+        [((3 * chans, 9 * chans), BF16), ((2, chans, size_z), F32)] * 2,
+        "modulate",
+        flops=1 << 22,
+    )(
+        style_vector[None, :],
+        affine_first.T,
+        kernel_first,
+        bias_first[None, :],
+        gain_first[None, :],
+        affine_second.T,
+        kernel_second,
+        bias_second[None, :],
+        gain_second[None, :],
+    )
     edges = call(
         functools.partial(pack_x_body, count_y, size_x, size_y, chans),
         [((depth, size_z), F32)] + [((5 * chans, size_z), BF16)] * size_x,
@@ -426,6 +417,7 @@
             (((size_y + 3) * chans, size_z), BF16),
         ],
         "first",
+        limit=24,
         flops=flops * size_x * (size_y + 2),
         scratch=[
             pltpu.VMEM((size_x + 2, size_y + 4, chans, 2 * size_z), BF16),
@@ -440,7 +432,7 @@
         edge_below,
         edge_above,
         dens,
-        *weights[0],
+        *modulated[:2],
     )
     hidden_below = shift(high, "gx", 1)
     hidden_above = shift(low, "gx", -1)
@@ -448,13 +440,14 @@
         functools.partial(second_body, size_x, size_y),
         [((chans, size_x, size_y, size_z), BF16)],
         "second",
+        limit=24,
         flops=flops * size_x * size_y,
         scratch=[
             pltpu.VMEM((size_x + 2, size_y + 2, chans, 2 * size_z), BF16),
             pltpu.VMEM((size_x * 16, 2 * size_z), F32),
             pltpu.VMEM((size_y, chans, size_z), F32),
         ],
-    )(hidden, hidden_below, hidden_above, dens, *weights[1])
+    )(hidden, hidden_below, hidden_above, dens, *modulated[2:])
     return result
 
 

time: 62.7 us -> 42.2 us (0.67)
  Pallas kernels: 30.3 us -> 6.01 us
  waiting for transfers between devices: 6.81 us -> 12.3 us
  local copies, waits for them, and re-layouts: 5.76 us -> 4.59 us
    pallas_call x8 -> x6, Pallas kernels: 30.3 us -> 6.01 us  [run(): pl.pallas_call(body, out_shape=tuple((jax.ShapeDtypeStruct(s, d) for s, d...]
    ppermute x10, waiting for transfers between devices: 6.81 us -> 12.3 us  [shift(): lax.ppermute(cells, axis, [(i, (i + step) % count) for i in range(count)])]
    unnamed x33 -> x26, local copies, waits for them, and re-layouts: 5.76 us -> 4.59 us
  transfers between devices with their start and end apart: 10 -> 10, of which waited for: 3 -> 5; matrix products, arithmetic and copies ran while one was open for 3% -> 0% of each run, Pallas kernels for 11% -> 2%
where the time goes in v2:
time: 42.2 us; the launch traced here: 41.9 us
  starting transfers between devices  18.2 us (43%)
  waiting for transfers between devices  12.3 us (29%)
  Pallas kernels  6.01 us (14%)
  local copies, waits for them, and re-layouts  4.59 us (11%)
  between operations  0.79 us (2%)
    ppermute x10, starting transfers between devices, shift(): lax.ppermute(cells, axis, [(i, (i + step) % count) for i in range(count)])  18.2 us
    ppermute x10, waiting for transfers between devices, shift(): lax.ppermute(cells, axis, [(i, (i + step) % count) for i in range(count)])  12.3 us
    pallas_call x6, Pallas kernels, run(): pl.pallas_call(body, out_shape=tuple((jax.ShapeDtypeStruct(s, d) for s, d...  6.01 us
    unnamed x26, local copies, waits for them, and re-layouts  4.59 us
  transfers between devices with their start and end apart: 10, of which 5 were waited for; matrix products, arithmetic and copies ran while one was open for 0% of the time, Pallas kernels for 2%

profile of v2, /device:TPU:0, one launch (start us, length us, event | category | flops | bytes accessed | tf_op | source)
XLA Modules:
  0.0 41.9 jit_solution(5467361805875205642)
XLA Ops:
  0.7 0.6 %copy-done.8 = s32[32,1]{0,1:T(1,128)S(1)} copy-done((s32[32,1]{0,1:T(1,128)S(1)}, s32[32,1]{0,1:T(1,128)}, u32[]{:S(2)}) %copy-start.8) | copy-done | bytes 152
  1.3 0.9 %copy-done.2 = bf16[64,2,8,128]{3,2,1,0:T(8,128)(2,1)S(1)} copy-done((bf16[64,2,8,128]{3,2,1,0:T(8,128)(2,1)S(1)}, bf16[64,2,8,128]{3,2,1,0:T(8,128)(2,1)}, u32[]{:S(2)}) %copy-start.2) | copy-done | bytes 262168
  2.3 0.7 %copy-done.5 = s32[32,64]{1,0:T(8,128)S(1)} copy-done((s32[32,64]{1,0:T(8,128)S(1)}, s32[32,64]{1,0:T(8,128)}, u32[]{:S(2)}) %copy-start.5) | copy-done | bytes 8216
  3.0 0.7 %copy-done.6 = bf16[32,64]{1,0:T(8,128)(2,1)S(1)} copy-done((bf16[32,64]{1,0:T(8,128)(2,1)S(1)}, bf16[32,64]{1,0:T(8,128)(2,1)}, u32[]{:S(2)}) %copy-start.6) | copy-done | bytes 4120
  3.7 0.7 %paint.1 = (bf16[8,64,128]{2,1,0:T(8,128)(2,1)S(1)}, bf16[8,64,128]{2,1,0:T(8,128)(2,1)S(1)}, bf16[320,128]{1,0:T(8,128)(2,1)S(1)}, f32[128,128]{1,0:T(8,128)S(1)}) custom-call(bf16[64,2,8,128]{3,2,1,0:T(8,128)(2,1)S(1)} %copy-done.2, s32[1,1]{1,0:T(1,128)} %bitcast.9.live, s32[1,32]{1,0:T(1,128)S(1)} %bitcast.13, s32[32,64]{1,0:T(8,128)S(1)} %copy-done.5, ...), custom_call_target="tpu_custom_call" | custom-call | bytes 274564 | tf_op jit(solution)/shard_map/paint/pallas_call | solution.py:23
  4.3 3.0 %collective-permute-start = (bf16[320,128]{1,0:T(8,128)(2,1)S(1)}, bf16[320,128]{1,0:T(8,128)(2,1)S(1)}, u32[]{:S(2)}, u32[]{:S(2)}) collective-permute-start(bf16[320,128]{1,0:T(8,128)(2,1)S(1)} %get-tuple-element.27), channel_id=1, source_target_pairs={{0,1},{1,0},{2,3},{3,2},{4,5},{5,4},{6,7},{7,6},{8,9},{9,8},{10,11... | collective-permute-start | bytes 245768 | tf_op jit(solution)/shard_map/ppermute | solution.py:16
  7.4 2.4 %collective-permute-done.refs_3_ = bf16[320,128]{1,0:T(8,128)(2,1)S(1)} collective-permute-done((bf16[320,128]{1,0:T(8,128)(2,1)S(1)}, bf16[320,128]{1,0:T(8,128)(2,1)S(1)}, u32[]{:S(2)}, u32[]{:S(2)}) %collective-permute-start) | collective-permute-done | bytes 81952 | tf_op jit(solution)/shard_map/ppermute | solution.py:16
  9.9 0.1 collective-permute-start.1
  9.9 1.7 %collective-permute-start.3 = (bf16[448,128]{1,0:T(8,128)(2,1)S(1)}, bf16[448,128]{1,0:T(8,128)(2,1)S(1)}, u32[]{:S(2)}, u32[]{:S(2)}) collective-permute-start(bf16[448,128]{1,0:T(8,128)(2,1)S(1)} %get-tuple-element.32), channel_id=1, source_target_pairs={{0,6},{2,0},{4,2},{6,4},{1,7},{3,1},{5,3},{7,5},{8,14},{10,8},{12,... | collective-permute-start | bytes 344072 | tf_op jit(solution)/shard_map/ppermute | solution.py:16
  11.7 4.1 %collective-permute-start.5 = (bf16[8,64,128]{2,1,0:T(8,128)(2,1)S(1)}, bf16[8,64,128]{2,1,0:T(8,128)(2,1)S(1)}, u32[]{:S(2)}, u32[]{:S(2)}) collective-permute-start(bf16[8,64,128]{2,1,0:T(8,128)(2,1)S(1)} %get-tuple-element.24.refs_0_), channel_id=1, source_target_pairs={{0,24},{8,0},{16,8},{24,16},{1,25},{9,1},{17,9},{25,17},{2,26},{10... | collective-permute-start | bytes 393224 | tf_op jit(solution)/shard_map/ppermute | solution.py:16
  15.8 1.5 %collective-permute-start.2 = (bf16[128,128]{1,0:T(8,128)(2,1)S(1)}, bf16[128,128]{1,0:T(8,128)(2,1)S(1)}, u32[]{:S(2)}, u32[]{:S(2)}) collective-permute-start(bf16[128,128]{1,0:T(8,128)(2,1)S(1)} %get-tuple-element.31), channel_id=1, source_target_pairs={{0,4},{2,6},{4,0},{6,2},{1,5},{3,7},{5,1},{7,3},{8,12},{10,14},{12... | collective-permute-start | bytes 98312 | tf_op jit(solution)/shard_map/ppermute | solution.py:16
  17.3 2.4 %collective-permute-done.2.refs_1_ = bf16[128,128]{1,0:T(8,128)(2,1)S(1)} collective-permute-done((bf16[128,128]{1,0:T(8,128)(2,1)S(1)}, bf16[128,128]{1,0:T(8,128)(2,1)S(1)}, u32[]{:S(2)}, u32[]{:S(2)}) %collective-permute-start.2) | collective-permute-done | bytes 32800 | tf_op jit(solution)/shard_map/ppermute | solution.py:16
  19.7 0.1 pack_x.1
  19.8 3.9 %collective-permute-start.7 = (bf16[320,128]{1,0:T(8,128)(2,1)S(1)}, bf16[320,128]{1,0:T(8,128)(2,1)S(1)}, u32[]{:S(2)}, u32[]{:S(2)}) collective-permute-start(bf16[320,128]{1,0:T(8,128)(2,1)S(1)} %get-tuple-element.33.refs_2_), channel_id=1, source_target_pairs={{0,24},{8,0},{16,8},{24,16},{1,25},{9,1},{17,9},{25,17},{2,26},{10... | collective-permute-start | bytes 245768 | tf_op jit(solution)/shard_map/ppermute | solution.py:16
  23.7 0.6 %copy-done.12 = f32[64]{0:T(128)S(1)} copy-done((f32[64]{0:T(128)S(1)}, f32[64]{0:T(128)}, u32[]{:S(2)}) %copy-start.12) | copy-done | bytes 280
  24.4 0.9 %copy-done.4 = f32[512,64]{0,1:T(8,128)S(1)} copy-done((f32[512,64]{0,1:T(8,128)S(1)}, f32[512,64]{0,1:T(8,128)}, u32[]{:S(2)}) %copy-start.4) | copy-done | bytes 131096
  25.3 0.8 %modulate.1 = (bf16[192,576]{1,0:T(8,128)(2,1)S(1)}, f32[2,64,128]{2,1,0:T(8,128)S(1)}, bf16[192,576]{1,0:T(8,128)(2,1)S(1)}, f32[2,64,128]{2,1,0:T(8,128)S(1)}) custom-call(f32[1,512]{1,0:T(1,128)S(1)} %bitcast.12, f32[64,512]{1,0:T(8,128)S(1)} %bitcast.10, bf16[27,64,64]{2,1,0:T(8,128)(2,1)S(1)} %copy-done, f32[1,64]{1,0:T(1,128)S(1)} %bitcast.14, ...), custom_call_target="tpu_custom_call" | custom-call | flops 4194304 | bytes 707584 | tf_op jit(solution)/shard_map/modulate/pallas_call | solution.py:23
  26.1 3.8 %collective-permute-done.6.refs_6_ = bf16[320,128]{1,0:T(8,128)(2,1)S(1)} collective-permute-done((bf16[320,128]{1,0:T(8,128)(2,1)S(1)}, bf16[320,128]{1,0:T(8,128)(2,1)S(1)}, u32[]{:S(2)}, u32[]{:S(2)}) %collective-permute-start.6) | collective-permute-done | bytes 81952 | tf_op jit(solution)/shard_map/ppermute | solution.py:16
  29.9 2.1 %first.1 = (bf16[2,10,64,256]{3,2,1,0:T(8,128)(2,1)S(1)}, bf16[704,128]{1,0:T(8,128)(2,1)S(1)}, bf16[704,128]{1,0:T(8,128)(2,1)S(1)}) custom-call(bf16[8,64,128]{2,1,0:T(8,128)(2,1)S(1)} %get-tuple-element.24.refs_0_, bf16[8,64,128]{2,1,0:T(8,128)(2,1)S(1)} %get-tuple-element.25.refs_1_, bf16[320,128]{1,0:T(8,128)(2,1)S(1)} %get-tuple-element.33.refs_2_, ...), custom_call_target="tpu_custom_call" | custom-call | flops 1132462080 | bytes 1171456 | tf_op jit(solution)/shard_map/first/pallas_call | solution.py:23
  32.0 0.1 collective-permute-start.8
  32.1 3.8 %collective-permute-start.9 = (bf16[704,128]{1,0:T(8,128)(2,1)S(1)}, bf16[704,128]{1,0:T(8,128)(2,1)S(1)}, u32[]{:S(2)}, u32[]{:S(2)}) collective-permute-start(bf16[704,128]{1,0:T(8,128)(2,1)S(1)} %get-tuple-element.40), channel_id=1, source_target_pairs={{0,24},{8,0},{16,8},{24,16},{1,25},{9,1},{17,9},{25,17},{2,26},{10... | collective-permute-start | bytes 540680 | tf_op jit(solution)/shard_map/ppermute | solution.py:16
  35.9 3.6 %collective-permute-done.8.below = bf16[704,128]{1,0:T(8,128)(2,1)S(1)} collective-permute-done((bf16[704,128]{1,0:T(8,128)(2,1)S(1)}, bf16[704,128]{1,0:T(8,128)(2,1)S(1)}, u32[]{:S(2)}, u32[]{:S(2)}) %collective-permute-start.8) | collective-permute-done | bytes 180256 | tf_op jit(solution)/shard_map/ppermute | solution.py:16
  39.5 0.1 collective-permute-done.9.above
  39.6 2.3 %second.1 = bf16[64,2,8,128]{3,2,1,0:T(8,128)(2,1)} custom-call(bf16[2,10,64,256]{3,2,1,0:T(8,128)(2,1)S(1)} %get-tuple-element.38.hidden, bf16[704,128]{1,0:T(8,128)(2,1)S(1)} %collective-permute-done.8.below, bf16[704,128]{1,0:T(8,128)(2,1)S(1)} %collective-permute-done.9.above, f32[64,128]{1,0:T(8,128)S(1)} %get-tuple-element.35.refs_8_.dens, ...), custom_call_target="tpu_custom_call" | custom-call | flops 905969664 | bytes 1335296 | tf_op jit(solution)/shard_map/second/pallas_call | solution.py:23
  (28 shorter events, 0.1 us)
Async XLA Ops:
  0.7 0.7 %copy-start.8 = (s32[32,1]{0,1:T(1,128)S(1)}, s32[32,1]{0,1:T(1,128)}, u32[]{:S(2)}) copy-start(s32[32,1]{0,1:T(1,128)} %param.15) | copy-start | bytes 388
  1.3 0.9 %copy-start.2 = (bf16[64,2,8,128]{3,2,1,0:T(8,128)(2,1)S(1)}, bf16[64,2,8,128]{3,2,1,0:T(8,128)(2,1)}, u32[]{:S(2)}) copy-start(bf16[64,2,8,128]{3,2,1,0:T(8,128)(2,1)} %features.1) | copy-start | bytes 786436
  2.3 0.7 %copy-start.5 = (s32[32,64]{1,0:T(8,128)S(1)}, s32[32,64]{1,0:T(8,128)}, u32[]{:S(2)}) copy-start(s32[32,64]{1,0:T(8,128)} %cells.1) | copy-start | bytes 24580
  3.0 0.7 %copy-start.6 = (bf16[32,64]{1,0:T(8,128)(2,1)S(1)}, bf16[32,64]{1,0:T(8,128)(2,1)}, u32[]{:S(2)}) copy-start(bf16[32,64]{1,0:T(8,128)(2,1)} %masses.1) | copy-start | bytes 12292
  3.7 20.0 %copy-start.1 = (bf16[27,64,64]{2,1,0:T(8,128)(2,1)S(1)}, bf16[27,64,64]{2,1,0:T(8,128)(2,1)}, u32[]{:S(2)}) copy-start(bf16[27,64,64]{2,1,0:T(8,128)(2,1)} %refs_5_.1) | copy-start | bytes 663556
  4.3 19.4 %copy-start = (bf16[27,64,64]{2,1,0:T(8,128)(2,1)S(1)}, bf16[27,64,64]{2,1,0:T(8,128)(2,1)}, u32[]{:S(2)}) copy-start(bf16[27,64,64]{2,1,0:T(8,128)(2,1)} %refs_1_.1) | copy-start | bytes 663556
  4.3 5.5 %collective-permute-start = (bf16[320,128]{1,0:T(8,128)(2,1)S(1)}, bf16[320,128]{1,0:T(8,128)(2,1)S(1)}, u32[]{:S(2)}, u32[]{:S(2)}) collective-permute-start(bf16[320,128]{1,0:T(8,128)(2,1)S(1)} %get-tuple-element.27), channel_id=1, source_target_pairs={{0,1},{1,0},{2,3},{3,2},{4,5},{5,4},{6,7},{7,6},{8,9},{9,8},{10,11... | collective-permute-start | bytes 245768 | tf_op jit(solution)/shard_map/ppermute | solution.py:16
  9.9 9.8 %collective-permute-start.1 = (bf16[448,128]{1,0:T(8,128)(2,1)S(1)}, bf16[448,128]{1,0:T(8,128)(2,1)S(1)}, u32[]{:S(2)}, u32[]{:S(2)}) collective-permute-start(bf16[448,128]{1,0:T(8,128)(2,1)S(1)} %get-tuple-element.30), channel_id=1, source_target_pairs={{0,2},{2,4},{4,6},{6,0},{1,3},{3,5},{5,7},{7,1},{8,10},{10,12},{12... | collective-permute-start | bytes 344072 | tf_op jit(solution)/shard_map/ppermute | solution.py:16
  9.9 9.8 %collective-permute-start.3 = (bf16[448,128]{1,0:T(8,128)(2,1)S(1)}, bf16[448,128]{1,0:T(8,128)(2,1)S(1)}, u32[]{:S(2)}, u32[]{:S(2)}) collective-permute-start(bf16[448,128]{1,0:T(8,128)(2,1)S(1)} %get-tuple-element.32), channel_id=1, source_target_pairs={{0,6},{2,0},{4,2},{6,4},{1,7},{3,1},{5,3},{7,5},{8,14},{10,8},{12,... | collective-permute-start | bytes 344072 | tf_op jit(solution)/shard_map/ppermute | solution.py:16
  11.7 14.4 %collective-permute-start.5 = (bf16[8,64,128]{2,1,0:T(8,128)(2,1)S(1)}, bf16[8,64,128]{2,1,0:T(8,128)(2,1)S(1)}, u32[]{:S(2)}, u32[]{:S(2)}) collective-permute-start(bf16[8,64,128]{2,1,0:T(8,128)(2,1)S(1)} %get-tuple-element.24.refs_0_), channel_id=1, source_target_pairs={{0,24},{8,0},{16,8},{24,16},{1,25},{9,1},{17,9},{25,17},{2,26},{10... | collective-permute-start | bytes 393224 | tf_op jit(solution)/shard_map/ppermute | solution.py:16
  15.8 10.3 %collective-permute-start.4 = (bf16[8,64,128]{2,1,0:T(8,128)(2,1)S(1)}, bf16[8,64,128]{2,1,0:T(8,128)(2,1)S(1)}, u32[]{:S(2)}, u32[]{:S(2)}) collective-permute-start(bf16[8,64,128]{2,1,0:T(8,128)(2,1)S(1)} %get-tuple-element.25.refs_1_), channel_id=1, source_target_pairs={{0,8},{8,16},{16,24},{24,0},{1,9},{9,17},{17,25},{25,1},{2,10},{10... | collective-permute-start | bytes 393224 | tf_op jit(solution)/shard_map/ppermute | solution.py:16
  15.8 3.9 %collective-permute-start.2 = (bf16[128,128]{1,0:T(8,128)(2,1)S(1)}, bf16[128,128]{1,0:T(8,128)(2,1)S(1)}, u32[]{:S(2)}, u32[]{:S(2)}) collective-permute-start(bf16[128,128]{1,0:T(8,128)(2,1)S(1)} %get-tuple-element.31), channel_id=1, source_target_pairs={{0,4},{2,6},{4,0},{6,2},{1,5},{3,7},{5,1},{7,3},{8,12},{10,14},{12... | collective-permute-start | bytes 98312 | tf_op jit(solution)/shard_map/ppermute | solution.py:16
  19.7 4.0 %copy-start.3 = (f32[512,64]{0,1:T(8,128)S(1)}, f32[512,64]{0,1:T(8,128)}, u32[]{:S(2)}) copy-start(f32[512,64]{0,1:T(8,128)} %param.20) | copy-start | bytes 393220
  19.8 6.3 %collective-permute-start.7 = (bf16[320,128]{1,0:T(8,128)(2,1)S(1)}, bf16[320,128]{1,0:T(8,128)(2,1)S(1)}, u32[]{:S(2)}, u32[]{:S(2)}) collective-permute-start(bf16[320,128]{1,0:T(8,128)(2,1)S(1)} %get-tuple-element.33.refs_2_), channel_id=1, source_target_pairs={{0,24},{8,0},{16,8},{24,16},{1,25},{9,1},{17,9},{25,17},{2,26},{10... | collective-permute-start | bytes 245768 | tf_op jit(solution)/shard_map/ppermute | solution.py:16
  23.7 6.2 %collective-permute-start.6 = (bf16[320,128]{1,0:T(8,128)(2,1)S(1)}, bf16[320,128]{1,0:T(8,128)(2,1)S(1)}, u32[]{:S(2)}, u32[]{:S(2)}) collective-permute-start(bf16[320,128]{1,0:T(8,128)(2,1)S(1)} %get-tuple-element.34.refs_3_), channel_id=1, source_target_pairs={{0,8},{8,16},{16,24},{24,0},{1,9},{9,17},{17,25},{25,1},{2,10},{10... | collective-permute-start | bytes 245768 | tf_op jit(solution)/shard_map/ppermute | solution.py:16
  23.7 0.7 %copy-start.12 = (f32[64]{0:T(128)S(1)}, f32[64]{0:T(128)}, u32[]{:S(2)}) copy-start(f32[64]{0:T(128)} %param.27) | copy-start | bytes 772
  23.7 0.7 %copy-start.7 = (f32[512]{0:T(512)S(1)}, f32[512]{0:T(512)}, u32[]{:S(2)}) copy-start(f32[512]{0:T(512)} %param.19) | copy-start | bytes 6148
  23.7 0.7 %copy-start.9 = (f32[64]{0:T(128)S(1)}, f32[64]{0:T(128)}, u32[]{:S(2)}) copy-start(f32[64]{0:T(128)} %param.22) | copy-start | bytes 772
  23.7 0.7 %copy-start.10 = (f32[64]{0:T(128)S(1)}, f32[64]{0:T(128)}, u32[]{:S(2)}) copy-start(f32[64]{0:T(128)} %param.23) | copy-start | bytes 772
  23.7 0.7 %copy-start.11 = (f32[64]{0:T(128)S(1)}, f32[64]{0:T(128)}, u32[]{:S(2)}) copy-start(f32[64]{0:T(128)} %param.26) | copy-start | bytes 772
  24.4 0.9 %copy-start.4 = (f32[512,64]{0,1:T(8,128)S(1)}, f32[512,64]{0,1:T(8,128)}, u32[]{:S(2)}) copy-start(f32[512,64]{0,1:T(8,128)} %param.24) | copy-start | bytes 393220
  32.0 7.4 %collective-permute-start.8 = (bf16[704,128]{1,0:T(8,128)(2,1)S(1)}, bf16[704,128]{1,0:T(8,128)(2,1)S(1)}, u32[]{:S(2)}, u32[]{:S(2)}) collective-permute-start(bf16[704,128]{1,0:T(8,128)(2,1)S(1)} %get-tuple-element.39), channel_id=1, source_target_pairs={{0,8},{8,16},{16,24},{24,0},{1,9},{9,17},{17,25},{25,1},{2,10},{10... | collective-permute-start | bytes 540680 | tf_op jit(solution)/shard_map/ppermute | solution.py:16
  32.1 7.5 %collective-permute-start.9 = (bf16[704,128]{1,0:T(8,128)(2,1)S(1)}, bf16[704,128]{1,0:T(8,128)(2,1)S(1)}, u32[]{:S(2)}, u32[]{:S(2)}) collective-permute-start(bf16[704,128]{1,0:T(8,128)(2,1)S(1)} %get-tuple-element.40), channel_id=1, source_target_pairs={{0,24},{8,0},{16,8},{24,16},{1,25},{9,1},{17,9},{25,17},{2,26},{10... | collective-permute-start | bytes 540680 | tf_op jit(solution)/shard_map/ppermute | solution.py:16

commit v3 on v2

v3 whole, which is shorter than its diff:
```python
import functools

import jax
import jax.numpy as jnp
from jax import lax
from jax.experimental import pallas as pl
from jax.experimental.pallas import tpu as pltpu
from jax.sharding import PartitionSpec as P


F32 = jnp.float32
BF16 = jnp.bfloat16


def shift(cells, axis, step):
    count = lax.axis_size(axis)
    pairs = [(i, (i + step) % count) for i in range(count)]
    return lax.ppermute(cells, axis, pairs)


def call(body, outs, flops=0, scratch=(), limit=12, fetched=()):
    def run(*args):
        size = sum(a.size * a.dtype.itemsize for a in args)
        specs = [
            pl.BlockSpec(memory_space=pltpu.HBM if i in fetched else pltpu.VMEM)
            for i in range(len(args))
        ]
        buffers = [pltpu.VMEM(args[i].shape, args[i].dtype) for i in fetched]
        extra = [pltpu.SemaphoreType.DMA((len(fetched),))] if fetched else []

        def wrapped(*refs):
            refs = list(refs)
            if fetched:
                done = refs.pop()
                held = refs[-len(fetched) :]
                refs = refs[: -len(fetched)]
                copies = [
                    pltpu.make_async_copy(refs[i], held[at], done.at[at])
                    for at, i in enumerate(fetched)
                ]
                for copy in copies:
                    copy.start()
                for copy in copies:
                    copy.wait()
                for at, i in enumerate(fetched):
                    refs[i] = held[at]
            body(*refs)

        kernel = pl.pallas_call(
            wrapped,
            out_shape=tuple(jax.ShapeDtypeStruct(s, d) for s, d in outs),
            in_specs=specs,
            out_specs=tuple(pl.BlockSpec(memory_space=pltpu.VMEM) for _ in outs),
            scratch_shapes=list(scratch) + buffers + extra,
            compiler_params=pltpu.CompilerParams(vmem_limit_bytes=limit << 20),
            cost_estimate=pl.CostEstimate(
                flops=flops, bytes_accessed=size, transcendentals=0
            ),
        )
        args = [
            pltpu.with_memory_space_constraint(a, pltpu.HBM) if i in fetched else a
            for i, a in enumerate(args)
        ]
        return kernel(*args)

    return run


def lanes_of(shape):
    return lax.broadcasted_iota(jnp.int32, shape, len(shape) - 1)


def rolled(values, amount, axis):
    amount = amount % values.shape[axis]
    return values if amount == 0 else pltpu.roll(values, amount, axis)


def ends(values, base):
    lane = lanes_of(values.shape)
    high = rolled(values, -(base + 1), 1)
    low = rolled(values, -(base + 3), 1)
    return jnp.where((lane == 0) | (lane == values.shape[1] - 1), high + low, 0.0)


def with_ends(tile, values, base):
    lane = lanes_of(tile.shape)
    high, low = (part.astype(F32) for part in halves(values))
    tile = jnp.where(
        (lane == base) | (lane == base + 1), rolled(high, base + 1, 1), tile
    )
    return jnp.where(
        (lane == base + 2) | (lane == base + 3), rolled(low, base + 3, 1), tile
    )


def halves(values):
    high = values.astype(BF16)
    return high, (values - high.astype(F32)).astype(BF16)


def store_halves(message, start, values):
    size = values.shape[0]
    message[start : start + size], message[start + size : start + 2 * size] = halves(
        values
    )


def load_halves(message, start, size):
    return message[start : start + size].astype(F32) + message[
        start + size : start + 2 * size
    ].astype(F32)


def column_of(row):
    size = row.shape[1]
    wide = jnp.broadcast_to(row, (size, size))
    same = lax.broadcasted_iota(jnp.int32, (size, size), 0) == lanes_of((size, size))
    return jnp.sum(jnp.where(same, wide, jnp.zeros_like(wide)), axis=1, keepdims=True)


def modulate_body(style, *refs):
    for layer in range(2):
        affine, kernel, bias, gain = refs[4 * layer : 4 * layer + 4]
        weights, columns = refs[8 + 2 * layer : 10 + 2 * layer]
        styles = (
            lax.dot_general(
                style[...],
                affine[...],
                (((1,), (1,)), ((), ())),
                precision=lax.Precision.HIGHEST,
                preferred_element_type=F32,
            )
            + 1.0
        )
        chans = kernel.shape[1]
        total = jnp.zeros((chans, kernel.shape[2]), F32)
        for k in range(27):
            scaled = kernel[k].astype(F32) * styles
            total = total + scaled * scaled
        demod = lax.rsqrt(jnp.sum(total, axis=1, keepdims=True) + 1e-08)
        for g in range(3):
            blocks = [
                (kernel[3 * j + g].astype(F32) * styles * demod).astype(BF16)
                for j in range(9)
            ]
            weights[g * chans : (g + 1) * chans, :] = jnp.concatenate(blocks, axis=1)
        columns[0] = jnp.broadcast_to(column_of(bias[...]), columns.shape[1:])
        columns[1] = jnp.broadcast_to(column_of(gain[...]), columns.shape[1:])


def paint_body(count_y, count_z, features, live, dest, cells, masses, *refs):
    size_x = features.shape[1]
    planes, messages, own = refs[0], refs[1:-1], refs[-1]
    for at in range(size_x):
        part = features[:, at].astype(F32)
        planes[at] = jnp.swapaxes(part, 0, 1).astype(BF16)
    size_y, chans, size_z = planes.shape[1:]
    blocks, per = cells.shape
    half = blocks // 2
    rank_y, rank_z = lax.axis_index("gy"), lax.axis_index("gz")
    shape = (blocks, per)
    target = jnp.broadcast_to(column_of(dest[...]), shape)
    to_y = lax.div(target, jnp.full(shape, count_z, jnp.int32))
    to_z = target - to_y * count_z - rank_z
    to_y = to_y - rank_y
    to_y = jnp.where(to_y < 0, to_y + count_y, to_y)
    to_z = jnp.where(to_z < 0, to_z + count_z, to_z)
    cell = cells[...]
    cell_row = lax.div(cell, jnp.full(shape, size_z, jnp.int32))
    at_z = cell - cell_row * size_z
    at_x = lax.div(cell_row, jnp.full(shape, size_y, jnp.int32))
    at_y = cell_row - at_x * size_y
    row = ((to_z * size_x + at_x) * count_y + to_y) * size_y + at_y
    alive = lax.broadcasted_iota(jnp.int32, shape, 0) < jnp.broadcast_to(live[...], shape)
    mass = jnp.where(alive, masses[...].astype(F32), 0.0)

    def paired(values):
        return jnp.concatenate([values[:half], values[half:]], axis=1)

    row, at_z, mass = paired(row), paired(at_z), paired(mass)
    width = 2 * per
    group = size_x * count_y * size_y
    total = count_z * group
    iota_rows = lax.broadcasted_iota(jnp.int32, (total, width), 0)
    iota_z = lax.broadcasted_iota(jnp.int32, (size_z, width), 0)
    left, right = [], []
    for r in range(half):
        left.append(
            jnp.where(iota_rows == row[r : r + 1], mass[r : r + 1], 0.0).astype(BF16)
        )
        right.append(jnp.where(iota_z == at_z[r : r + 1], 1.0, 0.0).astype(BF16))
    painted = lax.dot_general(
        jnp.concatenate(left, axis=1),
        jnp.concatenate(right, axis=1),
        (((1,), (1,)), ((), ())),
        preferred_element_type=F32,
    )
    parts = [painted[s * group : (s + 1) * group] for s in range(count_z)]
    lane = lanes_of((group, size_z))

    def beside(s):
        after = parts[(s + 1) % count_z]
        before = parts[(s - 1) % count_z]
        return jnp.where(lane == 0, after, jnp.where(lane == size_z - 1, before, 0.0))

    own[:group] = parts[0]
    own[group:] = beside(0)
    lane = lanes_of((chans, size_z))
    tile = jnp.zeros((chans, size_z), F32)
    for x in range(size_x):
        for y in range(size_y):
            j = x * size_y + y
            turned = rolled(planes[x, y].astype(F32), 4 * j + 2, 1)
            tile = jnp.where((lane >= 4 * j) & (lane < 4 * j + 4), turned, tile)
    base = 4 * size_x * size_y
    for s in range(1, count_z):
        message = messages[s - 1]
        message[:chans] = with_ends(tile, beside(s), base).astype(BF16)
        store_halves(message, chans, parts[s])


def pack_y_body(count_y, count_z, size_x, *refs):
    planes, own = refs[:2]
    received = refs[2 : 1 + count_z]
    outs = refs[1 + count_z :]
    size_y, chans, size_z = planes.shape[1:]
    group = own.shape[0] // 2
    lane = lanes_of((chans, size_z))
    before = received[0][:chans].astype(F32)
    after = received[-1][:chans].astype(F32)
    tile = jnp.where(lane % 4 < 2, before, after)
    base = 4 * size_x * size_y
    main, beside = own[:group], own[group:]
    for message in received:
        main = main + load_halves(message, chans, group)
        beside = beside + ends(message[:chans].astype(F32), base)
    tall = count_y * size_y
    width = 16

    def extended(s, values):
        found = []
        for x in range(size_x):
            part = values[x * tall : (x + 1) * tall]
            found.append(rolled(part, 1 - s * size_y, 0)[:width])
        return jnp.concatenate(found, axis=0)

    tile_out, own_out = outs[0], outs[1]
    tile_out[...] = tile.astype(BF16)
    depth = size_x * width
    own_out[:depth] = extended(0, main)
    own_out[depth:] = extended(0, beside)
    for s in range(1, count_y):
        message = outs[1 + s]
        store_halves(message, 0, extended(s, main))
        edge = extended(s, beside)
        if s not in (1, count_y - 1):
            message[2 * depth :] = with_ends(edge, edge, base).astype(BF16)
            continue
        edge = jnp.concatenate([edge, jnp.zeros((chans - depth, size_z), F32)], axis=0)
        message[2 * depth : 2 * depth + chans] = with_ends(tile, edge, base).astype(BF16)
        at = 2 * depth + chans
        first = size_y - 2 if s == 1 else 0
        for x in range(size_x):
            for y in range(first, first + 2):
                message[at : at + chans] = planes[x, y]
                at += chans


def pack_x_body(count_y, size_x, size_y, chans, tile, own, *refs):
    received = refs[: count_y - 1]
    dens, out = refs[count_y - 1], refs[count_y]
    depth = own.shape[0] // 2
    base = 4 * size_x * size_y
    main, beside = own[:depth], own[depth:]
    for message in received:
        main = main + load_halves(message, 0, depth)
        beside = beside + ends(message[2 * depth : 3 * depth].astype(F32), base)
    dens[:depth] = main
    dens[depth:] = beside
    base = 2 * depth
    below, above = received[0], received[-1]
    size_z = tile.shape[1]
    lane = lanes_of((chans, size_z))
    mine = tile[...].astype(F32)
    low = below[base : base + chans].astype(F32)
    high = above[base : base + chans].astype(F32)
    base += chans
    at = chans
    tall = size_y + 4
    edge = jnp.zeros((chans, size_z), F32)
    for x in range(size_x):
        first = 4 * x * size_y
        to = 4 * x * tall
        edge = jnp.where(
            lane >= to, rolled(low, to - first - 4 * (size_y - 2), 1), edge
        )
        edge = jnp.where(lane >= to + 8, rolled(mine, to + 8 - first, 1), edge)
        edge = jnp.where(
            lane >= to + 8 + 4 * size_y,
            rolled(high, to + 8 + 4 * size_y - first, 1),
            edge,
        )
        start = base + 2 * x * chans
        for message in (below, above):
            out[at : at + 2 * chans] = message[start : start + 2 * chans]
            at += 2 * chans
    beside = jnp.concatenate([beside, jnp.zeros((chans - depth, size_z), F32)], axis=0)
    out[:chans] = with_ends(edge, beside, 4 * size_x * tall).astype(BF16)
    store_halves(out, at, main)


def spread(tile, y):
    lane = lanes_of(tile.shape)
    size = tile.shape[1]
    turned = rolled(tile, size - 2 - 4 * y, 1)
    keep = (lane < 2) | (lane >= size - 2)
    return jnp.where(keep, turned, 0.0).astype(BF16)


def activate(values):
    return jnp.where(values >= 0, values, 0.2 * values) * jnp.sqrt(jnp.float32(2.0))


def column(stack, weights, columns, density, x, y, chans):
    taps = stack[pl.ds(x, 3), pl.ds(y, 3)]
    wide = taps.shape[-1]
    taps = taps.reshape(9 * chans, wide)
    found = jnp.dot(weights[...], taps, preferred_element_type=F32)
    summed = (
        pltpu.roll(found[:chans], 1, 1)
        + found[chans : 2 * chans]
        + pltpu.roll(found[2 * chans :], wide - 1, 1)
    )
    gain = jnp.concatenate([columns[1], columns[1]], axis=1)
    bias = jnp.concatenate([columns[0], columns[0]], axis=1)
    return activate(summed + gain * density + bias)


def both_body(size_x, size_y, *refs):
    own, own_edge, main_below, main_above, edge_below, edge_above, dens = refs[:7]
    first, first_columns, second, second_columns = refs[7:11]
    out, stack, hidden, dense, turned = refs[11:]
    chans, size_z = own.shape[2:]
    tall = size_y + 4
    width = 16
    depth = size_x * width
    sources = [(main_below, edge_below, main_below.shape[0] - 2 + i) for i in range(2)]
    sources += [(own, own_edge, x) for x in range(size_x)]
    sources += [(main_above, edge_above, i) for i in range(2)]
    last = size_x - 1
    for at, (main, edge, x) in enumerate(sources):
        stack[at, 2 : 2 + size_y, :, :size_z] = main[x]
        tile = edge[:chans].astype(F32)
        start = (1 + 4 * x) * chans
        for i, y in enumerate((0, 1, tall - 2, tall - 1)):
            stack[at, y, :, :size_z] = edge[start + i * chans : start + (i + 1) * chans]
        for y in range(tall):
            stack[at, y, :, size_z:] = spread(tile, x * tall + y)
    dense[width : width + depth, :size_z] = dens[:depth]
    dense[width : width + depth, size_z:] = dens[depth:]
    start = (1 + 4 * size_x) * chans
    for edge, x, at in (
        (edge_below, last, 0),
        (edge_above, 0, width + depth),
    ):
        main = load_halves(edge, start, depth)
        beside = ends(edge[:depth].astype(F32), 4 * size_x * tall)
        dense[at : at + width, :size_z] = main[x * width : (x + 1) * width]
        dense[at : at + width, size_z:] = beside[x * width : (x + 1) * width]
    for x in range(size_x + 2):
        for y in range(size_y + 2):
            density = dense[pl.ds(x * width + y, 1), :]
            found = column(stack, first, first_columns, density, x, y, chans)
            hidden[x, y] = found.astype(BF16)
    for x in range(size_x):
        for y in range(size_y):
            density = dense[pl.ds((x + 1) * width + y + 1, 1), :]
            found = column(hidden, second, second_columns, density, x, y, chans)
            turned[y] = found[:, :size_z]
        out[:, x] = jnp.swapaxes(turned[...], 0, 1).astype(BF16)


def shards(
    features,
    dest_bricks,
    cell_ids,
    cic_masses,
    live_counts,
    style_vector,
    affine_first,
    kernel_first,
    bias_first,
    gain_first,
    affine_second,
    kernel_second,
    bias_second,
    gain_second,
):
    chans, size_x, size_y, size_z = features.shape
    count_y, count_z = lax.axis_size("gy"), lax.axis_size("gz")
    group = size_x * count_y * size_y
    assert group == chans and 4 * size_x * (size_y + 4) + 4 <= size_z
    depth = size_x * 16
    painted = call(
        functools.partial(paint_body, count_y, count_z),
        [((size_x, size_y, chans, size_z), BF16)]
        + [((chans + 2 * group, size_z), BF16)] * (count_z - 1)
        + [((2 * group, size_z), F32)],
        fetched=(0, 2, 3, 4),
    )(features, live_counts[None, :], dest_bricks.T, cell_ids, cic_masses)
    planes, painted = painted[0], painted[1:]
    main_below = shift(planes[size_x - 2 :], "gx", 1)
    main_above = shift(planes[:2], "gx", -1)
    from_z = [shift(painted[s - 1], "gz", s) for s in range(1, count_z)]
    rows = [
        2 * depth + ((1 + 2 * size_x) * chans if s in (1, count_y - 1) else depth)
        for s in range(1, count_y)
    ]
    packed = call(
        functools.partial(pack_y_body, count_y, count_z, size_x),
        [((chans, size_z), BF16), ((2 * depth, size_z), F32)]
        + [((r, size_z), BF16) for r in rows],
    )(planes, painted[-1], *from_z)
    from_y = [shift(packed[1 + s], "gy", s) for s in range(1, count_y)]
    modulated = call(
        modulate_body,
        [((3 * chans, 9 * chans), BF16), ((2, chans, size_z), F32)] * 2,
        flops=1 << 22,
        fetched=tuple(range(9)),
    )(
        style_vector[None, :],
        affine_first.T,
        kernel_first,
        bias_first[None, :],
        gain_first[None, :],
        affine_second.T,
        kernel_second,
        bias_second[None, :],
        gain_second[None, :],
    )
    dens, edges = call(
        functools.partial(pack_x_body, count_y, size_x, size_y, chans),
        [
            ((2 * depth, size_z), F32),
            (((1 + 4 * size_x) * chans + 2 * depth, size_z), BF16),
        ],
    )(packed[0], packed[1], *from_y)
    edge_below = shift(edges, "gx", 1)
    edge_above = shift(edges, "gx", -1)
    columns = (size_x + 2) * (size_y + 2) + size_x * size_y
    (result,) = call(
        functools.partial(both_body, size_x, size_y),
        [((chans, size_x, size_y, size_z), BF16)],
        limit=24,
        flops=2 * 27 * chans * chans * 2 * size_z * columns,
        scratch=[
            pltpu.VMEM((size_x + 4, size_y + 4, chans, 2 * size_z), BF16),
            pltpu.VMEM((size_x + 2, size_y + 2, chans, 2 * size_z), BF16),
            pltpu.VMEM(((size_x + 2) * 16, 2 * size_z), F32),
            pltpu.VMEM((size_y, chans, size_z), F32),
        ],
    )(
        planes,
        edges,
        main_below,
        main_above,
        edge_below,
        edge_above,
        dens,
        *modulated,
    )
    return result


def solution(mesh):
    return jax.shard_map(
        shards,
        mesh=mesh,
        in_specs=(
            P(None, "gx", "gy", "gz"),
            P(("gx", "gy", "gz"), None),
            P(("gx", "gy", "gz"), None),
            P(("gx", "gy", "gz"), None),
            P(("gx", "gy", "gz")),
        )
        + (P(),) * 9,
        out_specs=P(None, "gx", "gy", "gz"),
        check_vma=False,
    )
```

time: 42.2 us -> 38.4 us (0.910)
  local copies, waits for them, and re-layouts: 4.59 us -> 0 us
  starting transfers between devices: 18.2 us -> 14.3 us
  Pallas kernels: 6.01 us -> 9.57 us
  waiting for transfers between devices: 12.3 us -> 13.6 us
    unnamed x26 -> x0, local copies, waits for them, and re-layouts: 4.59 us -> none
    ppermute x10 -> x8, starting transfers between devices: 18.2 us -> 14.3 us  [shift(): return lax.ppermute(cells, axis, pairs)]
    pallas_call x6 -> x5, Pallas kernels: 6.01 us -> 9.57 us  [run(): return kernel(*args)]
    ppermute x10 -> x8, waiting for transfers between devices: 12.3 us -> 13.6 us  [shift(): return lax.ppermute(cells, axis, pairs)]
  transfers between devices with their start and end apart: 10 -> 8, of which waited for: 5 -> 5; matrix products, arithmetic and copies ran while one was open for 0% -> 0% of each run, Pallas kernels for 2% -> 6%
where the time goes in v3:
time: 38.4 us; the launch traced here: 38.2 us
  starting transfers between devices  14.3 us (37%)
  waiting for transfers between devices  13.6 us (35%)
  Pallas kernels  9.57 us (25%)
  between operations  0.7 us (2%)
    ppermute x8, starting transfers between devices, shift(): return lax.ppermute(cells, axis, pairs)  14.3 us
    ppermute x8, waiting for transfers between devices, shift(): return lax.ppermute(cells, axis, pairs)  13.6 us
    pallas_call x5, Pallas kernels, run(): return kernel(*args)  9.57 us
  transfers between devices with their start and end apart: 8, of which 5 were waited for; matrix products, arithmetic and copies ran while one was open for 0% of the time, Pallas kernels for 6%

profile of v3, /device:TPU:0, one launch (start us, length us, event | category | flops | bytes accessed | tf_op | source)
XLA Modules:
  0.0 38.2 jit_solution(17321215481220606040)
XLA Ops:
  0.7 1.6 %shard_map.136 = (bf16[2,8,64,128]{3,2,1,0:T(8,128)(2,1)S(1)}, bf16[192,128]{1,0:T(8,128)(2,1)S(1)}, f32[128,128]{1,0:T(8,128)S(1)}) custom-call(bf16[64,2,8,128]{3,2,1,0:T(8,128)(2,1)} %refs_0_.1, s32[1,1]{1,0:T(1,128)} %bitcast.9.refs_1_, s32[1,32]{1,0:T(1,128)} %bitcast.13, s32[32,64]{1,0:T(8,128)} %refs_3_.1, bf16[32,64]{1,0:T(8,128)(2,1)} %refs_4_.1), custom_call_target="tpu_custom_call" | custom-call | bytes 274564 | tf_op jit(solution)/shard_map/pallas_call | solution.py:64
  2.3 3.0 %collective-permute-start = (bf16[192,128]{1,0:T(8,128)(2,1)S(1)}, bf16[192,128]{1,0:T(8,128)(2,1)S(1)}, u32[]{:S(2)}, u32[]{:S(2)}) collective-permute-start(bf16[192,128]{1,0:T(8,128)(2,1)S(1)} %get-tuple-element.21), channel_id=1, source_target_pairs={{0,1},{1,0},{2,3},{3,2},{4,5},{5,4},{6,7},{7,6},{8,9},{9,8},{10,11... | collective-permute-start | bytes 147464 | tf_op jit(solution)/shard_map/ppermute | solution.py:18
  5.3 2.1 %collective-permute-done.refs_2_ = bf16[192,128]{1,0:T(8,128)(2,1)S(1)} collective-permute-done((bf16[192,128]{1,0:T(8,128)(2,1)S(1)}, bf16[192,128]{1,0:T(8,128)(2,1)S(1)}, u32[]{:S(2)}, u32[]{:S(2)}) %collective-permute-start) | collective-permute-done | bytes 49184 | tf_op jit(solution)/shard_map/ppermute | solution.py:18
  7.4 0.2 shard_map.137
  7.6 0.1 collective-permute-start.1
  7.6 1.7 %collective-permute-start.3 = (bf16[384,128]{1,0:T(8,128)(2,1)S(1)}, bf16[384,128]{1,0:T(8,128)(2,1)S(1)}, u32[]{:S(2)}, u32[]{:S(2)}) collective-permute-start(bf16[384,128]{1,0:T(8,128)(2,1)S(1)} %get-tuple-element.26), channel_id=1, source_target_pairs={{0,6},{2,0},{4,2},{6,4},{1,7},{3,1},{5,3},{7,5},{8,14},{10,8},{12,... | collective-permute-start | bytes 294920 | tf_op jit(solution)/shard_map/ppermute | solution.py:18
  9.4 4.1 %collective-permute-start.5 = (bf16[2,8,64,128]{3,2,1,0:T(8,128)(2,1)S(1)}, bf16[2,8,64,128]{3,2,1,0:T(8,128)(2,1)S(1)}, u32[]{:S(2)}, u32[]{:S(2)}) collective-permute-start(bf16[2,8,64,128]{3,2,1,0:T(8,128)(2,1)S(1)} %get-tuple-element.19.refs_0_), channel_id=1, source_target_pairs={{0,24},{8,0},{16,8},{24,16},{1,25},{9,1},{17,9},{25,17},{2,26},{10... | collective-permute-start | bytes 786440 | tf_op jit(solution)/shard_map/ppermute | solution.py:18
  13.5 0.0 collective-permute-start.4
  13.5 1.5 %collective-permute-start.2 = (bf16[96,128]{1,0:T(8,128)(2,1)S(1)}, bf16[96,128]{1,0:T(8,128)(2,1)S(1)}, u32[]{:S(2)}, u32[]{:S(2)}) collective-permute-start(bf16[96,128]{1,0:T(8,128)(2,1)S(1)} %get-tuple-element.25), channel_id=1, source_target_pairs={{0,4},{2,6},{4,0},{6,2},{1,5},{3,7},{5,1},{7,3},{8,12},{10,14},{12... | collective-permute-start | bytes 73736 | tf_op jit(solution)/shard_map/ppermute | solution.py:18
  15.0 2.3 %collective-permute-done.2.refs_3_ = bf16[96,128]{1,0:T(8,128)(2,1)S(1)} collective-permute-done((bf16[96,128]{1,0:T(8,128)(2,1)S(1)}, bf16[96,128]{1,0:T(8,128)(2,1)S(1)}, u32[]{:S(2)}, u32[]{:S(2)}) %collective-permute-start.2) | collective-permute-done | bytes 24608 | tf_op jit(solution)/shard_map/ppermute | solution.py:18
  17.3 0.0 collective-permute-done.1.refs_2_
  17.3 0.0 collective-permute-done.3.refs_4_
  17.3 0.2 shard_map.138
  17.5 3.8 %collective-permute-start.7 = (bf16[640,128]{1,0:T(8,128)(2,1)S(1)}, bf16[640,128]{1,0:T(8,128)(2,1)S(1)}, u32[]{:S(2)}, u32[]{:S(2)}) collective-permute-start(bf16[640,128]{1,0:T(8,128)(2,1)S(1)} %get-tuple-element.27.refs_1_), channel_id=1, source_target_pairs={{0,24},{8,0},{16,8},{24,16},{1,25},{9,1},{17,9},{25,17},{2,26},{10... | collective-permute-start | bytes 491528 | tf_op jit(solution)/shard_map/ppermute | solution.py:18
  21.3 0.0 collective-permute-start.6
  21.3 2.1 %shard_map.139 = (bf16[192,576]{1,0:T(8,128)(2,1)S(1)}, f32[2,64,128]{2,1,0:T(8,128)S(1)}, bf16[192,576]{1,0:T(8,128)(2,1)S(1)}, f32[2,64,128]{2,1,0:T(8,128)S(1)}) custom-call(f32[1,512]{1,0:T(1,128)} %bitcast.12, f32[64,512]{1,0:T(8,128)} %bitcast.10, bf16[27,64,64]{2,1,0:T(8,128)(2,1)} %refs_2_.1, f32[1,64]{1,0:T(1,128)} %bitcast.14, f32[1,64]{1,0:T(1,128)} %bitcast.15, ...), custom_call_target="tpu_custom_call" | custom-call | flops 4194304 | bytes 707584 | tf_op jit(solution)/shard_map/pallas_call | solution.py:64
  23.5 0.0 collective-permute-done.5.refs_3_
  23.5 3.3 %collective-permute-done.4.refs_2_ = bf16[2,8,64,128]{3,2,1,0:T(8,128)(2,1)S(1)} collective-permute-done((bf16[2,8,64,128]{3,2,1,0:T(8,128)(2,1)S(1)}, bf16[2,8,64,128]{3,2,1,0:T(8,128)(2,1)S(1)}, u32[]{:S(2)}, u32[]{:S(2)}) %collective-permute-start.4) | collective-permute-done | bytes 262176 | tf_op jit(solution)/shard_map/ppermute | solution.py:18
  26.8 2.6 %collective-permute-done.7.refs_5_ = bf16[640,128]{1,0:T(8,128)(2,1)S(1)} collective-permute-done((bf16[640,128]{1,0:T(8,128)(2,1)S(1)}, bf16[640,128]{1,0:T(8,128)(2,1)S(1)}, u32[]{:S(2)}, u32[]{:S(2)}) %collective-permute-start.7) | collective-permute-done | bytes 163872 | tf_op jit(solution)/shard_map/ppermute | solution.py:18
  29.4 3.3 %collective-permute-done.6.refs_4_ = bf16[640,128]{1,0:T(8,128)(2,1)S(1)} collective-permute-done((bf16[640,128]{1,0:T(8,128)(2,1)S(1)}, bf16[640,128]{1,0:T(8,128)(2,1)S(1)}, u32[]{:S(2)}, u32[]{:S(2)}) %collective-permute-start.6) | collective-permute-done | bytes 163872 | tf_op jit(solution)/shard_map/ppermute | solution.py:18
  32.7 5.5 %shard_map.140 = bf16[64,2,8,128]{3,2,1,0:T(8,128)(2,1)} custom-call(bf16[2,8,64,128]{3,2,1,0:T(8,128)(2,1)S(1)} %get-tuple-element.19.refs_0_, bf16[640,128]{1,0:T(8,128)(2,1)S(1)} %get-tuple-element.27.refs_1_, bf16[2,8,64,128]{3,2,1,0:T(8,128)(2,1)S(1)} %collective-permute-done.4.refs_2_, bf16[2,8,64,128]{3,2,1,0:T(8,128)(2,1)S(1)} %collective-permute-done.5.refs_3_, ...), custom_call_target="tpu_custom_call" | custom-call | flops 3170893824 | bytes 1884160 | tf_op jit(solution)/shard_map/pallas_call | solution.py:64
Async XLA Ops:
  2.3 5.1 %collective-permute-start = (bf16[192,128]{1,0:T(8,128)(2,1)S(1)}, bf16[192,128]{1,0:T(8,128)(2,1)S(1)}, u32[]{:S(2)}, u32[]{:S(2)}) collective-permute-start(bf16[192,128]{1,0:T(8,128)(2,1)S(1)} %get-tuple-element.21), channel_id=1, source_target_pairs={{0,1},{1,0},{2,3},{3,2},{4,5},{5,4},{6,7},{7,6},{8,9},{9,8},{10,11... | collective-permute-start | bytes 147464 | tf_op jit(solution)/shard_map/ppermute | solution.py:18
  7.6 9.8 %collective-permute-start.1 = (bf16[384,128]{1,0:T(8,128)(2,1)S(1)}, bf16[384,128]{1,0:T(8,128)(2,1)S(1)}, u32[]{:S(2)}, u32[]{:S(2)}) collective-permute-start(bf16[384,128]{1,0:T(8,128)(2,1)S(1)} %get-tuple-element.24), channel_id=1, source_target_pairs={{0,2},{2,4},{4,6},{6,0},{1,3},{3,5},{5,7},{7,1},{8,10},{10,12},{12... | collective-permute-start | bytes 294920 | tf_op jit(solution)/shard_map/ppermute | solution.py:18
  7.6 9.7 %collective-permute-start.3 = (bf16[384,128]{1,0:T(8,128)(2,1)S(1)}, bf16[384,128]{1,0:T(8,128)(2,1)S(1)}, u32[]{:S(2)}, u32[]{:S(2)}) collective-permute-start(bf16[384,128]{1,0:T(8,128)(2,1)S(1)} %get-tuple-element.26), channel_id=1, source_target_pairs={{0,6},{2,0},{4,2},{6,4},{1,7},{3,1},{5,3},{7,5},{8,14},{10,8},{12,... | collective-permute-start | bytes 294920 | tf_op jit(solution)/shard_map/ppermute | solution.py:18
  9.4 14.1 %collective-permute-start.5 = (bf16[2,8,64,128]{3,2,1,0:T(8,128)(2,1)S(1)}, bf16[2,8,64,128]{3,2,1,0:T(8,128)(2,1)S(1)}, u32[]{:S(2)}, u32[]{:S(2)}) collective-permute-start(bf16[2,8,64,128]{3,2,1,0:T(8,128)(2,1)S(1)} %get-tuple-element.19.refs_0_), channel_id=1, source_target_pairs={{0,24},{8,0},{16,8},{24,16},{1,25},{9,1},{17,9},{25,17},{2,26},{10... | collective-permute-start | bytes 786440 | tf_op jit(solution)/shard_map/ppermute | solution.py:18
  13.5 13.3 %collective-permute-start.4 = (bf16[2,8,64,128]{3,2,1,0:T(8,128)(2,1)S(1)}, bf16[2,8,64,128]{3,2,1,0:T(8,128)(2,1)S(1)}, u32[]{:S(2)}, u32[]{:S(2)}) collective-permute-start(bf16[2,8,64,128]{3,2,1,0:T(8,128)(2,1)S(1)} %get-tuple-element.19.refs_0_), channel_id=1, source_target_pairs={{0,8},{8,16},{16,24},{24,0},{1,9},{9,17},{17,25},{25,1},{2,10},{10... | collective-permute-start | bytes 786440 | tf_op jit(solution)/shard_map/ppermute | solution.py:18
  13.5 3.8 %collective-permute-start.2 = (bf16[96,128]{1,0:T(8,128)(2,1)S(1)}, bf16[96,128]{1,0:T(8,128)(2,1)S(1)}, u32[]{:S(2)}, u32[]{:S(2)}) collective-permute-start(bf16[96,128]{1,0:T(8,128)(2,1)S(1)} %get-tuple-element.25), channel_id=1, source_target_pairs={{0,4},{2,6},{4,0},{6,2},{1,5},{3,7},{5,1},{7,3},{8,12},{10,14},{12... | collective-permute-start | bytes 73736 | tf_op jit(solution)/shard_map/ppermute | solution.py:18
  17.5 11.9 %collective-permute-start.7 = (bf16[640,128]{1,0:T(8,128)(2,1)S(1)}, bf16[640,128]{1,0:T(8,128)(2,1)S(1)}, u32[]{:S(2)}, u32[]{:S(2)}) collective-permute-start(bf16[640,128]{1,0:T(8,128)(2,1)S(1)} %get-tuple-element.27.refs_1_), channel_id=1, source_target_pairs={{0,24},{8,0},{16,8},{24,16},{1,25},{9,1},{17,9},{25,17},{2,26},{10... | collective-permute-start | bytes 491528 | tf_op jit(solution)/shard_map/ppermute | solution.py:18
  21.3 11.4 %collective-permute-start.6 = (bf16[640,128]{1,0:T(8,128)(2,1)S(1)}, bf16[640,128]{1,0:T(8,128)(2,1)S(1)}, u32[]{:S(2)}, u32[]{:S(2)}) collective-permute-start(bf16[640,128]{1,0:T(8,128)(2,1)S(1)} %get-tuple-element.27.refs_1_), channel_id=1, source_target_pairs={{0,8},{8,16},{16,24},{24,0},{1,9},{9,17},{17,25},{25,1},{2,10},{10... | collective-permute-start | bytes 491528 | tf_op jit(solution)/shard_map/ppermute | solution.py:18

commit v4 on v3

--- a/solution.py
+++ b/solution.py
@@ -18,7 +18,7 @@
     return lax.ppermute(cells, axis, pairs)
 
 
-def call(body, outs, flops=0, scratch=(), limit=12, fetched=()):
+def call(body, outs, flops=0, scratch=(), limit=12, fetched=(), late=()):
     def run(*args):
         size = sum(a.size * a.dtype.itemsize for a in args)
         specs = [
@@ -40,10 +40,12 @@
                 ]
                 for copy in copies:
                     copy.start()
-                for copy in copies:
-                    copy.wait()
                 for at, i in enumerate(fetched):
                     refs[i] = held[at]
+                    if i not in late:
+                        copies[at].wait()
+                if late:
+                    refs.insert(0, [copies[fetched.index(i)] for i in late])
             body(*refs)
 
         kernel = pl.pallas_call(
@@ -138,22 +140,24 @@
             scaled = kernel[k].astype(F32) * styles
             total = total + scaled * scaled
         demod = lax.rsqrt(jnp.sum(total, axis=1, keepdims=True) + 1e-08)
-        for g in range(3):
-            blocks = [
-                (kernel[3 * j + g].astype(F32) * styles * demod).astype(BF16)
-                for j in range(9)
-            ]
-            weights[g * chans : (g + 1) * chans, :] = jnp.concatenate(blocks, axis=1)
+        for e in range(3):
+            for g in range(3):
+                blocks = [
+                    (kernel[9 * e + 3 * f + g].astype(F32) * styles * demod).astype(
+                        BF16
+                    )
+                    for f in range(3)
+                ]
+                weights[e, g * chans : (g + 1) * chans, :] = jnp.concatenate(
+                    blocks, axis=1
+                )
         columns[0] = jnp.broadcast_to(column_of(bias[...]), columns.shape[1:])
         columns[1] = jnp.broadcast_to(column_of(gain[...]), columns.shape[1:])
 
 
-def paint_body(count_y, count_z, features, live, dest, cells, masses, *refs):
+def paint_body(count_y, count_z, pending, features, live, dest, cells, masses, *refs):
     size_x = features.shape[1]
     planes, messages, own = refs[0], refs[1:-1], refs[-1]
-    for at in range(size_x):
-        part = features[:, at].astype(F32)
-        planes[at] = jnp.swapaxes(part, 0, 1).astype(BF16)
     size_y, chans, size_z = planes.shape[1:]
     blocks, per = cells.shape
     half = blocks // 2
@@ -205,6 +209,11 @@
 
     own[:group] = parts[0]
     own[group:] = beside(0)
+    for copy in pending:
+        copy.wait()
+    for at in range(size_x):
+        part = features[:, at].astype(F32)
+        planes[at] = jnp.swapaxes(part, 0, 1).astype(BF16)
     lane = lanes_of((chans, size_z))
     tile = jnp.zeros((chans, size_z), F32)
     for x in range(size_x):
@@ -284,8 +293,6 @@
     mine = tile[...].astype(F32)
     low = below[base : base + chans].astype(F32)
     high = above[base : base + chans].astype(F32)
-    base += chans
-    at = chans
     tall = size_y + 4
     edge = jnp.zeros((chans, size_z), F32)
     for x in range(size_x):
@@ -300,13 +307,9 @@
             rolled(high, to + 8 + 4 * size_y - first, 1),
             edge,
         )
-        start = base + 2 * x * chans
-        for message in (below, above):
-            out[at : at + 2 * chans] = message[start : start + 2 * chans]
-            at += 2 * chans
     beside = jnp.concatenate([beside, jnp.zeros((chans - depth, size_z), F32)], axis=0)
     out[:chans] = with_ends(edge, beside, 4 * size_x * tall).astype(BF16)
-    store_halves(out, at, main)
+    store_halves(out, chans, main)
 
 
 def spread(tile, y):
@@ -321,62 +324,111 @@
     return jnp.where(values >= 0, values, 0.2 * values) * jnp.sqrt(jnp.float32(2.0))
 
 
-def column(stack, weights, columns, density, x, y, chans):
-    taps = stack[pl.ds(x, 3), pl.ds(y, 3)]
-    wide = taps.shape[-1]
-    taps = taps.reshape(9 * chans, wide)
-    found = jnp.dot(weights[...], taps, preferred_element_type=F32)
-    summed = (
+def taps_of(stack, weights, taps, y, chans):
+    found = None
+    for tap, plane in taps:
+        rows = stack[plane, pl.ds(y, 3)]
+        rows = rows.reshape(3 * chans, rows.shape[-1])
+        part = jnp.dot(weights[tap], rows, preferred_element_type=F32)
+        found = part if found is None else found + part
+    wide = found.shape[1]
+    return (
         pltpu.roll(found[:chans], 1, 1)
         + found[chans : 2 * chans]
         + pltpu.roll(found[2 * chans :], wide - 1, 1)
     )
-    gain = jnp.concatenate([columns[1], columns[1]], axis=1)
-    bias = jnp.concatenate([columns[0], columns[0]], axis=1)
+
+
+def finish(summed, columns, density):
+    copies = summed.shape[1] // columns.shape[2]
+    gain = jnp.concatenate([columns[1]] * copies, axis=1)
+    bias = jnp.concatenate([columns[0]] * copies, axis=1)
     return activate(summed + gain * density + bias)
 
 
-def both_body(size_x, size_y, *refs):
-    own, own_edge, main_below, main_above, edge_below, edge_above, dens = refs[:7]
-    first, first_columns, second, second_columns = refs[7:11]
-    out, stack, hidden, dense, turned = refs[11:]
-    chans, size_z = own.shape[2:]
+def fill(stack, at, main, low, high, start, tile, x, size_y):
+    chans, size_z = main.shape[1:]
+    tall = size_y + 4
+    stack[at, 2 : 2 + size_y, :, :size_z] = main[...]
+    for i in range(2):
+        rows = slice(start + i * chans, start + (i + 1) * chans)
+        stack[at, i, :, :size_z] = low[rows]
+        stack[at, tall - 2 + i, :, :size_z] = high[rows]
+    edge = tile[:chans].astype(F32)
+    for y in range(tall):
+        stack[at, y, :, size_z:] = spread(edge, x * tall + y)
+
+
+def own_body(size_x, size_y, planes, low, high, tile, weights, partial, stack):
+    chans = planes.shape[2]
+    for x in range(size_x):
+        start = low.shape[0] - 2 * (size_x - x) * chans
+        fill(stack, x, planes.at[x], low, high, start, tile, x, size_y)
+    for at in range(size_x + 2):
+        taps = [(e, at + e - 2) for e in range(3) if 0 <= at + e - 2 < size_x]
+        for y in range(size_y + 2):
+            partial[at, y] = taps_of(stack, weights, taps, y, chans)
+
+
+def turn_body(below, above, low_side, high_side, first, last):
+    chans, _, size_y = below.shape[:3]
+    at = 0
+    for source, out in ((below, low_side), (above, high_side)):
+        for x in range(2):
+            part = source[:, x].astype(F32)
+            out[x] = jnp.swapaxes(part, 0, 1).astype(BF16)
+            for y in range(2):
+                first[at : at + chans] = out[x, y]
+                last[at : at + chans] = out[x, size_y - 2 + y]
+                at += chans
+
+
+def rest_body(size_x, size_y, *refs):
+    partial, main_below, main_above, edge_below, edge_above, low, high = refs[:7]
+    dens, first, first_columns, second, second_columns = refs[7:12]
+    out, stack, hidden, dense, turned = refs[12:]
+    chans, size_z = main_below.shape[2:]
     tall = size_y + 4
     width = 16
     depth = size_x * width
-    sources = [(main_below, edge_below, main_below.shape[0] - 2 + i) for i in range(2)]
-    sources += [(own, own_edge, x) for x in range(size_x)]
-    sources += [(main_above, edge_above, i) for i in range(2)]
-    last = size_x - 1
-    for at, (main, edge, x) in enumerate(sources):
-        stack[at, 2 : 2 + size_y, :, :size_z] = main[x]
-        tile = edge[:chans].astype(F32)
-        start = (1 + 4 * x) * chans
-        for i, y in enumerate((0, 1, tall - 2, tall - 1)):
-            stack[at, y, :, :size_z] = edge[start + i * chans : start + (i + 1) * chans]
-        for y in range(tall):
-            stack[at, y, :, size_z:] = spread(tile, x * tall + y)
+    for i in range(2):
+        for side, main, edge, x in (
+            (0, main_below, edge_below, size_x - 2 + i),
+            (2, main_above, edge_above, i),
+        ):
+            at = side + i
+            fill(stack, at, main.at[i], low, high, 2 * at * chans, edge, x, size_y)
     dense[width : width + depth, :size_z] = dens[:depth]
     dense[width : width + depth, size_z:] = dens[depth:]
-    start = (1 + 4 * size_x) * chans
     for edge, x, at in (
-        (edge_below, last, 0),
+        (edge_below, size_x - 1, 0),
         (edge_above, 0, width + depth),
     ):
-        main = load_halves(edge, start, depth)
+        main = load_halves(edge, chans, depth)
         beside = ends(edge[:depth].astype(F32), 4 * size_x * tall)
         dense[at : at + width, :size_z] = main[x * width : (x + 1) * width]
         dense[at : at + width, size_z:] = beside[x * width : (x + 1) * width]
-    for x in range(size_x + 2):
+    for at in range(size_x + 2):
+        taps = []
+        for e in range(3):
+            plane = at + e - 2
+            if plane < 0:
+                taps.append((e, plane + 2))
+            elif plane >= size_x:
+                taps.append((e, plane - size_x + 2))
         for y in range(size_y + 2):
-            density = dense[pl.ds(x * width + y, 1), :]
-            found = column(stack, first, first_columns, density, x, y, chans)
-            hidden[x, y] = found.astype(BF16)
+            summed = partial[at, y]
+            if taps:
+                summed = summed + taps_of(stack, first, taps, y, chans)
+            density = dense[at * width + y : at * width + y + 1, :]
+            hidden[at, y] = finish(summed, first_columns, density).astype(BF16)
     for x in range(size_x):
         for y in range(size_y):
-            density = dense[pl.ds((x + 1) * width + y + 1, 1), :]
-            found = column(hidden, second, second_columns, density, x, y, chans)
-            turned[y] = found[:, :size_z]
+            row = (x + 1) * width + y + 1
+            taps = [(e, x + e) for e in range(3)]
+            summed = taps_of(hidden, second, taps, y, chans)[:, :size_z]
+            density = dense[row : row + 1, :size_z]
+            turned[y] = finish(summed, second_columns, density)
         out[:, x] = jnp.swapaxes(turned[...], 0, 1).astype(BF16)
 
 
@@ -401,16 +453,17 @@
     group = size_x * count_y * size_y
     assert group == chans and 4 * size_x * (size_y + 4) + 4 <= size_z
     depth = size_x * 16
+    main_below = shift(features[:, size_x - 2 :], "gx", 1)
+    main_above = shift(features[:, :2], "gx", -1)
     painted = call(
         functools.partial(paint_body, count_y, count_z),
         [((size_x, size_y, chans, size_z), BF16)]
         + [((chans + 2 * group, size_z), BF16)] * (count_z - 1)
         + [((2 * group, size_z), F32)],
-        fetched=(0, 2, 3, 4),
+        fetched=(2, 3, 4, 0),
+        late=(0,),
     )(features, live_counts[None, :], dest_bricks.T, cell_ids, cic_masses)
     planes, painted = painted[0], painted[1:]
-    main_below = shift(planes[size_x - 2 :], "gx", 1)
-    main_above = shift(planes[:2], "gx", -1)
     from_z = [shift(painted[s - 1], "gz", s) for s in range(1, count_z)]
     rows = [
         2 * depth + ((1 + 2 * size_x) * chans if s in (1, count_y - 1) else depth)
@@ -424,7 +477,7 @@
     from_y = [shift(packed[1 + s], "gy", s) for s in range(1, count_y)]
     modulated = call(
         modulate_body,
-        [((3 * chans, 9 * chans), BF16), ((2, chans, size_z), F32)] * 2,
+        [((3, 3 * chans, 3 * chans), BF16), ((2, chans, size_z), F32)] * 2,
         flops=1 << 22,
         fetched=tuple(range(9)),
     )(
@@ -442,30 +495,44 @@
         functools.partial(pack_x_body, count_y, size_x, size_y, chans),
         [
             ((2 * depth, size_z), F32),
-            (((1 + 4 * size_x) * chans + 2 * depth, size_z), BF16),
+            ((chans + 2 * depth, size_z), BF16),
         ],
     )(packed[0], packed[1], *from_y)
+    sides = call(
+        turn_body,
+        [((2, size_y, chans, size_z), BF16)] * 2 + [((8 * chans, size_z), BF16)] * 2,
+        flops=1 << 22,
+    )(main_below, main_above)
+    low = shift(sides[3], "gy", 1)
+    high = shift(sides[2], "gy", -1)
     edge_below = shift(edges, "gx", 1)
     edge_above = shift(edges, "gx", -1)
-    columns = (size_x + 2) * (size_y + 2) + size_x * size_y
+    flops = 2 * 9 * chans * chans * 2 * size_z
+    (partial,) = call(
+        functools.partial(own_body, size_x, size_y),
+        [((size_x + 2, size_y + 2, chans, 2 * size_z), F32)],
+        limit=16,
+        flops=flops * 3 * size_x * (size_y + 2),
+        scratch=[pltpu.VMEM((size_x, size_y + 4, chans, 2 * size_z), BF16)],
+    )(planes, from_y[0], from_y[-1], edges, modulated[0])
     (result,) = call(
-        functools.partial(both_body, size_x, size_y),
+        functools.partial(rest_body, size_x, size_y),
         [((chans, size_x, size_y, size_z), BF16)],
         limit=24,
-        flops=2 * 27 * chans * chans * 2 * size_z * columns,
+        flops=flops * (6 * (size_y + 2) + 3 * size_x * size_y),
         scratch=[
-            pltpu.VMEM((size_x + 4, size_y + 4, chans, 2 * size_z), BF16),
+            pltpu.VMEM((4, size_y + 4, chans, 2 * size_z), BF16),
             pltpu.VMEM((size_x + 2, size_y + 2, chans, 2 * size_z), BF16),
             pltpu.VMEM(((size_x + 2) * 16, 2 * size_z), F32),
             pltpu.VMEM((size_y, chans, size_z), F32),
         ],
     )(
-        planes,
-        edges,
-        main_below,
-        main_above,
+        partial,
+        *sides[:2],
         edge_below,
         edge_above,
+        low,
+        high,
         dens,
         *modulated,
     )

time: 38.4 us -> 33.6 us (0.88)
  waiting for transfers between devices: 13.6 us -> 8.6 us
  Pallas kernels: 9.57 us -> 10.3 us
  starting transfers between devices: 14.3 us -> 13.8 us
    ppermute x8 -> x10, waiting for transfers between devices: 13.6 us -> 8.6 us  [shift(): return lax.ppermute(cells, axis, pairs)]
    pallas_call x5 -> x7, Pallas kernels: 9.57 us -> 10.3 us  [run(): return kernel(*args)]
    ppermute x8 -> x10, starting transfers between devices: 14.3 us -> 13.8 us  [shift(): return lax.ppermute(cells, axis, pairs)]
  transfers between devices with their start and end apart: 8 -> 10, of which waited for: 5 -> 3; matrix products, arithmetic and copies ran while one was open for 0% -> 0% of each run, Pallas kernels for 6% -> 18%
where the time goes in v4:
time: 33.6 us; the launch traced here: 33.5 us
  starting transfers between devices  13.8 us (41%)
  Pallas kernels  10.3 us (31%)
  waiting for transfers between devices  8.6 us (26%)
  between operations  0.74 us (2%)
    ppermute x10, starting transfers between devices, shift(): return lax.ppermute(cells, axis, pairs)  13.8 us
    pallas_call x7, Pallas kernels, run(): return kernel(*args)  10.3 us
    ppermute x10, waiting for transfers between devices, shift(): return lax.ppermute(cells, axis, pairs)  8.6 us
  transfers between devices with their start and end apart: 10, of which 3 were waited for; matrix products, arithmetic and copies ran while one was open for 0% of the time, Pallas kernels for 18%

profile of v4, /device:TPU:0, one launch (start us, length us, event | category | flops | bytes accessed | tf_op | source)
XLA Modules:
  0.0 33.5 jit_solution(6400951043084153035)
XLA Ops:
  0.0 5.1 %collective-permute-start.5 = (bf16[64,2,8,128]{3,2,1,0:T(8,128)(2,1)}, bf16[64,2,8,128]{3,2,1,0:T(8,128)(2,1)S(1)}, u32[]{:S(2)}, u32[]{:S(2)}) collective-permute-start(bf16[64,2,8,128]{3,2,1,0:T(8,128)(2,1)} %refs_0_.1), channel_id=1, source_target_pairs={{0,24},{8,0},{16,8},{24,16},{1,25},{9,1},{17,9},{25,17},{2,26},{10... | collective-permute-start | bytes 786440 | tf_op jit(solution)/shard_map/ppermute | solution.py:18
  5.1 0.0 collective-permute-start.4
  5.7 1.5 %shard_map.136 = (bf16[2,8,64,128]{3,2,1,0:T(8,128)(2,1)S(1)}, bf16[192,128]{1,0:T(8,128)(2,1)S(1)}, f32[128,128]{1,0:T(8,128)S(1)}) custom-call(bf16[64,2,8,128]{3,2,1,0:T(8,128)(2,1)} %refs_0_.1, s32[1,1]{1,0:T(1,128)} %bitcast.9.refs_1_, s32[1,32]{1,0:T(1,128)} %bitcast.13, s32[32,64]{1,0:T(8,128)} %refs_3_.1, bf16[32,64]{1,0:T(8,128)(2,1)} %refs_4_.1), custom_call_target="tpu_custom_call" | custom-call | bytes 274564 | tf_op jit(solution)/shard_map/pallas_call | solution.py:66
  7.2 1.6 %collective-permute-start = (bf16[192,128]{1,0:T(8,128)(2,1)S(1)}, bf16[192,128]{1,0:T(8,128)(2,1)S(1)}, u32[]{:S(2)}, u32[]{:S(2)}) collective-permute-start(bf16[192,128]{1,0:T(8,128)(2,1)S(1)} %get-tuple-element.25), channel_id=1, source_target_pairs={{0,1},{1,0},{2,3},{3,2},{4,5},{5,4},{6,7},{7,6},{8,9},{9,8},{10,11... | collective-permute-start | bytes 147464 | tf_op jit(solution)/shard_map/ppermute | solution.py:18
  8.7 2.6 %collective-permute-done.refs_2_ = bf16[192,128]{1,0:T(8,128)(2,1)S(1)} collective-permute-done((bf16[192,128]{1,0:T(8,128)(2,1)S(1)}, bf16[192,128]{1,0:T(8,128)(2,1)S(1)}, u32[]{:S(2)}, u32[]{:S(2)}) %collective-permute-start) | collective-permute-done | bytes 49184 | tf_op jit(solution)/shard_map/ppermute | solution.py:18
  11.3 0.2 shard_map.137
  11.5 0.1 collective-permute-start.1
  11.6 1.7 %collective-permute-start.2 = (bf16[384,128]{1,0:T(8,128)(2,1)S(1)}, bf16[384,128]{1,0:T(8,128)(2,1)S(1)}, u32[]{:S(2)}, u32[]{:S(2)}) collective-permute-start(bf16[384,128]{1,0:T(8,128)(2,1)S(1)} %get-tuple-element.27), channel_id=1, source_target_pairs={{0,6},{2,0},{4,2},{6,4},{1,7},{3,1},{5,3},{7,5},{8,14},{10,8},{12,... | collective-permute-start | bytes 294920 | tf_op jit(solution)/shard_map/ppermute | solution.py:18
  13.3 1.5 %collective-permute-start.3 = (bf16[96,128]{1,0:T(8,128)(2,1)S(1)}, bf16[96,128]{1,0:T(8,128)(2,1)S(1)}, u32[]{:S(2)}, u32[]{:S(2)}) collective-permute-start(bf16[96,128]{1,0:T(8,128)(2,1)S(1)} %get-tuple-element.30), channel_id=1, source_target_pairs={{0,4},{2,6},{4,0},{6,2},{1,5},{3,7},{5,1},{7,3},{8,12},{10,14},{12... | collective-permute-start | bytes 73736 | tf_op jit(solution)/shard_map/ppermute | solution.py:18
  14.8 0.0 collective-permute-done.5.refs_1_
  14.8 2.5 %collective-permute-done.4.refs_0_ = bf16[64,2,8,128]{3,2,1,0:T(8,128)(2,1)S(1)} collective-permute-done((bf16[64,2,8,128]{3,2,1,0:T(8,128)(2,1)}, bf16[64,2,8,128]{3,2,1,0:T(8,128)(2,1)S(1)}, u32[]{:S(2)}, u32[]{:S(2)}) %collective-permute-start.4) | collective-permute-done | bytes 262176 | tf_op jit(solution)/shard_map/ppermute | solution.py:18
  17.4 0.3 shard_map.141
  17.7 0.1 collective-permute-start.8
  17.7 1.7 %collective-permute-start.9 = (bf16[512,128]{1,0:T(8,128)(2,1)S(1)}, bf16[512,128]{1,0:T(8,128)(2,1)S(1)}, u32[]{:S(2)}, u32[]{:S(2)}) collective-permute-start(bf16[512,128]{1,0:T(8,128)(2,1)S(1)} %get-tuple-element.36), channel_id=1, source_target_pairs={{0,6},{2,0},{4,2},{6,4},{1,7},{3,1},{5,3},{7,5},{8,14},{10,8},{12,... | collective-permute-start | bytes 393224 | tf_op jit(solution)/shard_map/ppermute | solution.py:18
  19.5 2.1 %shard_map.139 = (bf16[3,192,192]{2,1,0:T(8,128)(2,1)S(1)}, f32[2,64,128]{2,1,0:T(8,128)S(1)}, bf16[3,192,192]{2,1,0:T(8,128)(2,1)S(1)}, f32[2,64,128]{2,1,0:T(8,128)S(1)}) custom-call(f32[1,512]{1,0:T(1,128)} %bitcast.12, f32[64,512]{1,0:T(8,128)} %bitcast.10, bf16[27,64,64]{2,1,0:T(8,128)(2,1)} %refs_2_.1, f32[1,64]{1,0:T(1,128)} %bitcast.14, ...), custom_call_target="tpu_custom_call" | custom-call | flops 4194304 | bytes 707584 | tf_op jit(solution)/shard_map/pallas_call | solution.py:66
  21.6 0.0 collective-permute-done.1.refs_2_.refs_1_
  21.6 0.0 collective-permute-done.2.refs_4_.refs_2_
  21.6 0.2 shard_map.138
  21.8 1.8 %collective-permute-start.7 = (bf16[128,128]{1,0:T(8,128)(2,1)S(1)}, bf16[128,128]{1,0:T(8,128)(2,1)S(1)}, u32[]{:S(2)}, u32[]{:S(2)}) collective-permute-start(bf16[128,128]{1,0:T(8,128)(2,1)S(1)} %get-tuple-element.31.refs_3_), channel_id=1, source_target_pairs={{0,24},{8,0},{16,8},{24,16},{1,25},{9,1},{17,9},{25,17},{2,26},{10... | collective-permute-start | bytes 98312 | tf_op jit(solution)/shard_map/ppermute | solution.py:18
  23.5 0.3 collective-permute-start.6
  23.8 2.0 %shard_map.140.refs_0_ = f32[4,10,64,256]{3,2,1,0:T(8,128)S(1)} custom-call(bf16[2,8,64,128]{3,2,1,0:T(8,128)(2,1)S(1)} %get-tuple-element.23.refs_0_, bf16[384,128]{1,0:T(8,128)(2,1)S(1)} %collective-permute-done.1.refs_2_.refs_1_, bf16[384,128]{1,0:T(8,128)(2,1)S(1)} %collective-permute-done.2.refs_4_.refs_2_, ...), custom_call_target="tpu_custom_call" | custom-call | flops 1132462080 | bytes 712704 | tf_op jit(solution)/shard_map/pallas_call | solution.py:66
  25.8 0.0 collective-permute-done.7.refs_4_
  25.8 3.5 %collective-permute-done.6.refs_3_ = bf16[128,128]{1,0:T(8,128)(2,1)S(1)} collective-permute-done((bf16[128,128]{1,0:T(8,128)(2,1)S(1)}, bf16[128,128]{1,0:T(8,128)(2,1)S(1)}, u32[]{:S(2)}, u32[]{:S(2)}) %collective-permute-start.6) | collective-permute-done | bytes 32800 | tf_op jit(solution)/shard_map/ppermute | solution.py:18
  29.3 4.2 %shard_map.142 = bf16[64,2,8,128]{3,2,1,0:T(8,128)(2,1)} custom-call(f32[4,10,64,256]{3,2,1,0:T(8,128)S(1)} %shard_map.140.refs_0_, bf16[2,8,64,128]{3,2,1,0:T(8,128)(2,1)S(1)} %get-tuple-element.33.refs_1_, bf16[2,8,64,128]{3,2,1,0:T(8,128)(2,1)S(1)} %get-tuple-element.34.refs_2_, bf16[128,128]{1,0:T(8,128)(2,1)S(1)} %collective-permute-done.6.refs_3_, ...), custom_call_target="tpu_custom_call" | custom-call | flops 2038431744 | bytes 4079616 | tf_op jit(solution)/shard_map/pallas_call | solution.py:66
  (3 shorter events, 0.0 us)
Async XLA Ops:
  0.0 14.8 %collective-permute-start.5 = (bf16[64,2,8,128]{3,2,1,0:T(8,128)(2,1)}, bf16[64,2,8,128]{3,2,1,0:T(8,128)(2,1)S(1)}, u32[]{:S(2)}, u32[]{:S(2)}) collective-permute-start(bf16[64,2,8,128]{3,2,1,0:T(8,128)(2,1)} %refs_0_.1), channel_id=1, source_target_pairs={{0,24},{8,0},{16,8},{24,16},{1,25},{9,1},{17,9},{25,17},{2,26},{10... | collective-permute-start | bytes 786440 | tf_op jit(solution)/shard_map/ppermute | solution.py:18
  5.1 12.3 %collective-permute-start.4 = (bf16[64,2,8,128]{3,2,1,0:T(8,128)(2,1)}, bf16[64,2,8,128]{3,2,1,0:T(8,128)(2,1)S(1)}, u32[]{:S(2)}, u32[]{:S(2)}) collective-permute-start(bf16[64,2,8,128]{3,2,1,0:T(8,128)(2,1)} %refs_0_.1), channel_id=1, source_target_pairs={{0,8},{8,16},{16,24},{24,0},{1,9},{9,17},{17,25},{25,1},{2,10},{10... | collective-permute-start | bytes 786440 | tf_op jit(solution)/shard_map/ppermute | solution.py:18
  7.2 4.2 %collective-permute-start = (bf16[192,128]{1,0:T(8,128)(2,1)S(1)}, bf16[192,128]{1,0:T(8,128)(2,1)S(1)}, u32[]{:S(2)}, u32[]{:S(2)}) collective-permute-start(bf16[192,128]{1,0:T(8,128)(2,1)S(1)} %get-tuple-element.25), channel_id=1, source_target_pairs={{0,1},{1,0},{2,3},{3,2},{4,5},{5,4},{6,7},{7,6},{8,9},{9,8},{10,11... | collective-permute-start | bytes 147464 | tf_op jit(solution)/shard_map/ppermute | solution.py:18
  11.5 10.1 %collective-permute-start.1 = (bf16[384,128]{1,0:T(8,128)(2,1)S(1)}, bf16[384,128]{1,0:T(8,128)(2,1)S(1)}, u32[]{:S(2)}, u32[]{:S(2)}) collective-permute-start(bf16[384,128]{1,0:T(8,128)(2,1)S(1)} %get-tuple-element.26), channel_id=1, source_target_pairs={{0,2},{2,4},{4,6},{6,0},{1,3},{3,5},{5,7},{7,1},{8,10},{10,12},{12... | collective-permute-start | bytes 294920 | tf_op jit(solution)/shard_map/ppermute | solution.py:18
  11.6 10.0 %collective-permute-start.2 = (bf16[384,128]{1,0:T(8,128)(2,1)S(1)}, bf16[384,128]{1,0:T(8,128)(2,1)S(1)}, u32[]{:S(2)}, u32[]{:S(2)}) collective-permute-start(bf16[384,128]{1,0:T(8,128)(2,1)S(1)} %get-tuple-element.27), channel_id=1, source_target_pairs={{0,6},{2,0},{4,2},{6,4},{1,7},{3,1},{5,3},{7,5},{8,14},{10,8},{12,... | collective-permute-start | bytes 294920 | tf_op jit(solution)/shard_map/ppermute | solution.py:18
  13.3 8.3 %collective-permute-start.3 = (bf16[96,128]{1,0:T(8,128)(2,1)S(1)}, bf16[96,128]{1,0:T(8,128)(2,1)S(1)}, u32[]{:S(2)}, u32[]{:S(2)}) collective-permute-start(bf16[96,128]{1,0:T(8,128)(2,1)S(1)} %get-tuple-element.30), channel_id=1, source_target_pairs={{0,4},{2,6},{4,0},{6,2},{1,5},{3,7},{5,1},{7,3},{8,12},{10,14},{12... | collective-permute-start | bytes 73736 | tf_op jit(solution)/shard_map/ppermute | solution.py:18
  17.7 11.6 %collective-permute-start.8 = (bf16[512,128]{1,0:T(8,128)(2,1)S(1)}, bf16[512,128]{1,0:T(8,128)(2,1)S(1)}, u32[]{:S(2)}, u32[]{:S(2)}) collective-permute-start(bf16[512,128]{1,0:T(8,128)(2,1)S(1)} %get-tuple-element.35), channel_id=1, source_target_pairs={{0,2},{2,4},{4,6},{6,0},{1,3},{3,5},{5,7},{7,1},{8,10},{10,12},{12... | collective-permute-start | bytes 393224 | tf_op jit(solution)/shard_map/ppermute | solution.py:18
  17.7 11.5 %collective-permute-start.9 = (bf16[512,128]{1,0:T(8,128)(2,1)S(1)}, bf16[512,128]{1,0:T(8,128)(2,1)S(1)}, u32[]{:S(2)}, u32[]{:S(2)}) collective-permute-start(bf16[512,128]{1,0:T(8,128)(2,1)S(1)} %get-tuple-element.36), channel_id=1, source_target_pairs={{0,6},{2,0},{4,2},{6,4},{1,7},{3,1},{5,3},{7,5},{8,14},{10,8},{12,... | collective-permute-start | bytes 393224 | tf_op jit(solution)/shard_map/ppermute | solution.py:18
  21.8 4.0 %collective-permute-start.7 = (bf16[128,128]{1,0:T(8,128)(2,1)S(1)}, bf16[128,128]{1,0:T(8,128)(2,1)S(1)}, u32[]{:S(2)}, u32[]{:S(2)}) collective-permute-start(bf16[128,128]{1,0:T(8,128)(2,1)S(1)} %get-tuple-element.31.refs_3_), channel_id=1, source_target_pairs={{0,24},{8,0},{16,8},{24,16},{1,25},{9,1},{17,9},{25,17},{2,26},{10... | collective-permute-start | bytes 98312 | tf_op jit(solution)/shard_map/ppermute | solution.py:18
  23.5 5.7 %collective-permute-start.6 = (bf16[128,128]{1,0:T(8,128)(2,1)S(1)}, bf16[128,128]{1,0:T(8,128)(2,1)S(1)}, u32[]{:S(2)}, u32[]{:S(2)}) collective-permute-start(bf16[128,128]{1,0:T(8,128)(2,1)S(1)} %get-tuple-element.31.refs_3_), channel_id=1, source_target_pairs={{0,8},{8,16},{16,24},{24,0},{1,9},{9,17},{17,25},{25,1},{2,10},{10... | collective-permute-start | bytes 98312 | tf_op jit(solution)/shard_map/ppermute | solution.py:18

commit v5 on v4

--- a/solution.py
+++ b/solution.py
@@ -18,7 +18,7 @@
     return lax.ppermute(cells, axis, pairs)
 
 
-def call(body, outs, flops=0, scratch=(), limit=12, fetched=(), late=()):
+def call(body, outs, flops=0, scratch=(), limit=12, fetched=(), late=(), space=pltpu.VMEM):
     def run(*args):
         size = sum(a.size * a.dtype.itemsize for a in args)
         specs = [
@@ -52,7 +52,7 @@
             wrapped,
             out_shape=tuple(jax.ShapeDtypeStruct(s, d) for s, d in outs),
             in_specs=specs,
-            out_specs=tuple(pl.BlockSpec(memory_space=pltpu.VMEM) for _ in outs),
+            out_specs=tuple(pl.BlockSpec(memory_space=space) for _ in outs),
             scratch_shapes=list(scratch) + buffers + extra,
             compiler_params=pltpu.CompilerParams(vmem_limit_bytes=limit << 20),
             cost_estimate=pl.CostEstimate(
@@ -141,23 +141,18 @@
             total = total + scaled * scaled
         demod = lax.rsqrt(jnp.sum(total, axis=1, keepdims=True) + 1e-08)
         for e in range(3):
-            for g in range(3):
-                blocks = [
-                    (kernel[9 * e + 3 * f + g].astype(F32) * styles * demod).astype(
-                        BF16
-                    )
-                    for f in range(3)
-                ]
-                weights[e, g * chans : (g + 1) * chans, :] = jnp.concatenate(
-                    blocks, axis=1
-                )
+            blocks = [
+                (kernel[9 * e + k].astype(F32) * styles * demod).astype(BF16)
+                for k in range(9)
+            ]
+            weights[e] = jnp.concatenate(blocks, axis=1)
         columns[0] = jnp.broadcast_to(column_of(bias[...]), columns.shape[1:])
         columns[1] = jnp.broadcast_to(column_of(gain[...]), columns.shape[1:])
 
 
 def paint_body(count_y, count_z, pending, features, live, dest, cells, masses, *refs):
     size_x = features.shape[1]
-    planes, messages, own = refs[0], refs[1:-1], refs[-1]
+    planes, messages, own, own_tile = refs[0], refs[1:-2], refs[-2], refs[-1]
     size_y, chans, size_z = planes.shape[1:]
     blocks, per = cells.shape
     half = blocks // 2
@@ -219,9 +214,10 @@
     for x in range(size_x):
         for y in range(size_y):
             j = x * size_y + y
-            turned = rolled(planes[x, y].astype(F32), 4 * j + 2, 1)
-            tile = jnp.where((lane >= 4 * j) & (lane < 4 * j + 4), turned, tile)
-    base = 4 * size_x * size_y
+            turned = rolled(planes[x, y].astype(F32), 6 * j + 2, 1)
+            tile = jnp.where((lane >= 6 * j) & (lane < 6 * j + 4), turned, tile)
+    own_tile[...] = tile.astype(BF16)
+    base = 6 * size_x * size_y
     for s in range(1, count_z):
         message = messages[s - 1]
         message[:chans] = with_ends(tile, beside(s), base).astype(BF16)
@@ -229,16 +225,20 @@
 
 
 def pack_y_body(count_y, count_z, size_x, *refs):
-    planes, own = refs[:2]
-    received = refs[2 : 1 + count_z]
-    outs = refs[1 + count_z :]
+    planes, own, own_tile = refs[:3]
+    received = refs[3 : 2 + count_z]
+    outs = refs[2 + count_z :]
     size_y, chans, size_z = planes.shape[1:]
     group = own.shape[0] // 2
     lane = lanes_of((chans, size_z))
     before = received[0][:chans].astype(F32)
     after = received[-1][:chans].astype(F32)
-    tile = jnp.where(lane % 4 < 2, before, after)
-    base = 4 * size_x * size_y
+    mine = own_tile[...].astype(F32)
+    place = lane % 6
+    tile = jnp.where(place == 3, rolled(mine, 2, 1), rolled(after, 2, 1))
+    tile = jnp.where(place == 2, mine, tile)
+    tile = jnp.where(place < 2, before, tile)
+    base = 6 * size_x * size_y
     main, beside = own[:group], own[group:]
     for message in received:
         main = main + load_halves(message, chans, group)
@@ -279,7 +279,7 @@
     received = refs[: count_y - 1]
     dens, out = refs[count_y - 1], refs[count_y]
     depth = own.shape[0] // 2
-    base = 4 * size_x * size_y
+    base = 6 * size_x * size_y
     main, beside = own[:depth], own[depth:]
     for message in received:
         main = main + load_halves(message, 0, depth)
@@ -294,80 +294,143 @@
     low = below[base : base + chans].astype(F32)
     high = above[base : base + chans].astype(F32)
     tall = size_y + 4
-    edge = jnp.zeros((chans, size_z), F32)
+    beside = jnp.concatenate([beside, jnp.zeros((chans - depth, size_z), F32)], axis=0)
     for x in range(size_x):
-        first = 4 * x * size_y
-        to = 4 * x * tall
-        edge = jnp.where(
-            lane >= to, rolled(low, to - first - 4 * (size_y - 2), 1), edge
-        )
-        edge = jnp.where(lane >= to + 8, rolled(mine, to + 8 - first, 1), edge)
-        edge = jnp.where(
-            lane >= to + 8 + 4 * size_y,
-            rolled(high, to + 8 + 4 * size_y - first, 1),
-            edge,
-        )
-    beside = jnp.concatenate([beside, jnp.zeros((chans - depth, size_z), F32)], axis=0)
-    out[:chans] = with_ends(edge, beside, 4 * size_x * tall).astype(BF16)
-    store_halves(out, chans, main)
-
-
-def spread(tile, y):
-    lane = lanes_of(tile.shape)
-    size = tile.shape[1]
-    turned = rolled(tile, size - 2 - 4 * y, 1)
-    keep = (lane < 2) | (lane >= size - 2)
-    return jnp.where(keep, turned, 0.0).astype(BF16)
+        first = 6 * x * size_y
+        edge = rolled(low, -first - 6 * (size_y - 2), 1)
+        edge = jnp.where(lane >= 12, rolled(mine, 12 - first, 1), edge)
+        at = 12 + 6 * size_y
+        edge = jnp.where(lane >= at, rolled(high, at - first, 1), edge)
+        if x == 0:
+            edge = with_ends(edge, beside, 6 * tall)
+        out[x * chans : (x + 1) * chans] = edge.astype(BF16)
+    store_halves(out, size_x * chans, main)
 
 
 def activate(values):
     return jnp.where(values >= 0, values, 0.2 * values) * jnp.sqrt(jnp.float32(2.0))
 
 
-def taps_of(stack, weights, taps, y, chans):
-    found = None
-    for tap, plane in taps:
-        rows = stack[plane, pl.ds(y, 3)]
-        rows = rows.reshape(3 * chans, rows.shape[-1])
-        part = jnp.dot(weights[tap], rows, preferred_element_type=F32)
-        found = part if found is None else found + part
-    wide = found.shape[1]
-    return (
-        pltpu.roll(found[:chans], 1, 1)
-        + found[chans : 2 * chans]
-        + pltpu.roll(found[2 * chans :], wide - 1, 1)
-    )
-
-
 def finish(summed, columns, density):
-    copies = summed.shape[1] // columns.shape[2]
-    gain = jnp.concatenate([columns[1]] * copies, axis=1)
-    bias = jnp.concatenate([columns[0]] * copies, axis=1)
-    return activate(summed + gain * density + bias)
-
-
-def fill(stack, at, main, low, high, start, tile, x, size_y):
-    chans, size_z = main.shape[1:]
-    tall = size_y + 4
-    stack[at, 2 : 2 + size_y, :, :size_z] = main[...]
+    return activate(summed + columns[1] * density + columns[0])
+
+
+def product(weights, taps, stack, plane, rows):
+    chans = weights.shape[1]
+    flat = [stack[plane, y : y + 3].reshape(9 * chans, -1) for y in rows]
+    matrix = weights[taps].reshape(-1, 9 * chans)
+    found = jnp.dot(
+        matrix, jnp.concatenate(flat, axis=1), preferred_element_type=F32
+    )
+    size = flat[0].shape[1]
+    return [
+        [
+            found[e * chans : (e + 1) * chans, i * size : (i + 1) * size]
+            for e in range(found.shape[0] // chans)
+        ]
+        for i in range(len(rows))
+    ]
+
+
+def edge_product(weights, taps, tile, ends_too=False):
+    chans = weights.shape[1]
+    flat = [rolled(tile, 1 - g - 6 * f, 1) for f in range(3) for g in range(3)]
+    taken = jnp.concatenate(flat, axis=0)
+    if ends_too:
+        lane = lanes_of(tile.shape)
+        nothing = jnp.zeros(tile.shape, tile.dtype)
+        kept = []
+        for f in range(3):
+            turned = flat[3 * f + 1]
+            kept += [
+                jnp.where(lane % 6 == 1, turned, nothing),
+                nothing,
+                jnp.where(lane % 6 == 4, turned, nothing),
+            ]
+        taken = jnp.concatenate([taken, jnp.concatenate(kept, axis=0)], axis=1)
+    matrix = weights[taps].reshape(-1, 9 * chans)
+    found = jnp.dot(matrix, taken, preferred_element_type=F32)
+    return [found[e * chans : (e + 1) * chans] for e in range(found.shape[0] // chans)]
+
+
+def swapped(tile):
+    lane = lanes_of(tile.shape)
+    return jnp.where(lane % 6 == 1, rolled(tile, -3, 1), rolled(tile, 1, 1))
+
+
+def put(stack, plane, row, cells, inward):
+    lane = lanes_of(cells.shape)
+    last = cells.shape[1] - 1
+    ends_of = rolled(inward, -6 * row - 2, 1)
+    stack[plane, row, 0] = jnp.where(lane == 0, ends_of, rolled(cells, 1, 1))
+    stack[plane, row, 1] = cells
+    stack[plane, row, 2] = jnp.where(lane == last, ends_of, rolled(cells, -1, 1))
+
+
+def fill(stack, at, main, low, high, start, tile, size_y):
+    chans = main.shape[1]
+    inward = swapped(tile)
+    for y in range(size_y):
+        put(stack, at, 2 + y, main[y], inward)
     for i in range(2):
         rows = slice(start + i * chans, start + (i + 1) * chans)
-        stack[at, i, :, :size_z] = low[rows]
-        stack[at, tall - 2 + i, :, :size_z] = high[rows]
-    edge = tile[:chans].astype(F32)
-    for y in range(tall):
-        stack[at, y, :, size_z:] = spread(edge, x * tall + y)
-
-
-def own_body(size_x, size_y, planes, low, high, tile, weights, partial, stack):
-    chans = planes.shape[2]
+        put(stack, at, i, low[rows], inward)
+        put(stack, at, size_y + 2 + i, high[rows], inward)
+
+
+def pairs_of(rows):
+    return [range(y, min(y + 2, rows)) for y in range(0, rows, 2)]
+
+
+def sides_of(size_x, below, above):
+    return (
+        (0, below, ((0, slice(0, 1), (0,)), (1, slice(0, 2), (1, 0)))),
+        (
+            2,
+            above,
+            (
+                (0, slice(1, 3), (size_x + 1, size_x)),
+                (1, slice(2, 3), (size_x + 1,)),
+            ),
+        ),
+    )
+
+
+def own_body(size_x, size_y, *refs):
+    planes, low, high, tiles, below, above, weights = refs[:7]
+    partial, partial_edge, stack, beside = refs[7:]
+    chans, size_z = planes.shape[2:]
+    whole = slice(0, 3)
     for x in range(size_x):
         start = low.shape[0] - 2 * (size_x - x) * chans
-        fill(stack, x, planes.at[x], low, high, start, tile, x, size_y)
-    for at in range(size_x + 2):
-        taps = [(e, at + e - 2) for e in range(3) if 0 <= at + e - 2 < size_x]
-        for y in range(size_y + 2):
-            partial[at, y] = taps_of(stack, weights, taps, y, chans)
+        tile = tiles[x * chans : (x + 1) * chans]
+        fill(stack, x, planes.at[x], low, high, start, tile, size_y)
+
+        def add(out, at, values, fresh):
+            out[at] = values if fresh else out[at] + values
+
+        for e, values in enumerate(edge_product(weights, whole, tile)):
+            at = x + 2 - e
+            add(partial_edge, at, values, x == 0 or e == 0)
+        for rows in pairs_of(size_y + 2):
+            found = product(weights, whole, stack, x, rows)
+            for y, parts in zip(rows, found):
+                for e, values in enumerate(parts):
+                    at = x + 2 - e
+                    add(partial, (at, y), values, x == 0 or e == 0)
+    nothing = jnp.zeros((chans, size_z), BF16)
+    for side, main, plan in sides_of(size_x, below, above):
+        for plane, taps, targets in plan:
+            at = side + plane
+            for y in (0, 1, size_y + 2, size_y + 3):
+                beside[at, y] = jnp.zeros((3, chans, size_z), BF16)
+            for y in range(size_y):
+                put(beside, at, 2 + y, main[plane, y], nothing)
+            for rows in pairs_of(size_y + 2):
+                found = product(weights, taps, beside, at, rows)
+                for y, parts in zip(rows, found):
+                    for target, values in zip(targets, parts):
+                        partial[target, y] = partial[target, y] + values
 
 
 def turn_body(below, above, low_side, high_side, first, last):
@@ -384,52 +447,104 @@
 
 
 def rest_body(size_x, size_y, *refs):
-    partial, main_below, main_above, edge_below, edge_above, low, high = refs[:7]
-    dens, first, first_columns, second, second_columns = refs[7:12]
-    out, stack, hidden, dense, turned = refs[12:]
-    chans, size_z = main_below.shape[2:]
+    partial, partial_edge, edge_below, edge_above, low, high = refs[:6]
+    dens, first, first_columns, second, second_columns = refs[6:11]
+    out, stack, hidden, total, ready, done = refs[11:]
+    chans, size_z = partial.shape[2:]
     tall = size_y + 4
     width = 16
     depth = size_x * width
-    for i in range(2):
-        for side, main, edge, x in (
-            (0, main_below, edge_below, size_x - 2 + i),
-            (2, main_above, edge_above, i),
-        ):
-            at = side + i
-            fill(stack, at, main.at[i], low, high, 2 * at * chans, edge, x, size_y)
-    dense[width : width + depth, :size_z] = dens[:depth]
-    dense[width : width + depth, size_z:] = dens[depth:]
-    for edge, x, at in (
-        (edge_below, size_x - 1, 0),
-        (edge_above, 0, width + depth),
-    ):
-        main = load_halves(edge, chans, depth)
-        beside = ends(edge[:depth].astype(F32), 4 * size_x * tall)
-        dense[at : at + width, :size_z] = main[x * width : (x + 1) * width]
-        dense[at : at + width, size_z:] = beside[x * width : (x + 1) * width]
-    for at in range(size_x + 2):
-        taps = []
-        for e in range(3):
-            plane = at + e - 2
-            if plane < 0:
-                taps.append((e, plane + 2))
-            elif plane >= size_x:
-                taps.append((e, plane - size_x + 2))
+    own = dens[...]
+    density = []
+    for x in range(size_x):
+        rows = slice(x * width, (x + 1) * width)
+        density.append((own[:depth][rows], own[depth:][rows]))
+    for edge, x, at in ((edge_below, size_x - 1, 0), (edge_above, 0, size_x + 1)):
+        rows = slice(x * width, (x + 1) * width)
+        main = load_halves(edge, size_x * chans, depth)
+        beside = ends(edge[:depth].astype(F32), 6 * tall)
+        density.insert(at, (main[rows], beside[rows]))
+    lane = lanes_of((1, size_z))
+    edges_at = {at: partial_edge[at] for at in range(size_x + 2)}
+    fixes = {}
+    rows_at = {}
+    nothing = jnp.zeros((3, chans, size_z), BF16)
+    idle = jnp.zeros((chans, size_z), BF16)
+    for side, edge, plan in sides_of(size_x, edge_below, edge_above):
+        for plane, taps, targets in plan:
+            at = side + plane
+            x = size_x - 2 + plane if side == 0 else plane
+            tile = edge[x * chans : (x + 1) * chans]
+            found = edge_product(first, taps, tile, ends_too=True)
+            for target, values in zip(targets, found):
+                edges_at[target] = edges_at[target] + values[:, :size_z]
+                fix = values[:, size_z:]
+                fixes[target] = fixes[target] + fix if target in fixes else fix
+            for i in range(2):
+                start = (2 * at + i) * chans
+                put(stack, at, i, low[start : start + chans], idle)
+                stack[at, 2 + i] = nothing
+                put(stack, at, 4 + i, high[start : start + chans], idle)
+            for begin, rows in ((0, range(2)), (size_y, range(2, 4))):
+                found = product(first, taps, stack, at, rows)
+                for i, parts in enumerate(found):
+                    for target, values in zip(targets, parts):
+                        key = (target, begin + i)
+                        rows_at[key] = rows_at[key] + values if key in rows_at else values
+    wide = lanes_of((chans, size_z))
+    outside = (wide == 0) | (wide == size_z - 1)
+    for at in sorted(fixes):
+        beside = density[at][1]
+        ends_at = jnp.zeros((1, size_z), F32)
         for y in range(size_y + 2):
-            summed = partial[at, y]
-            if taps:
-                summed = summed + taps_of(stack, first, taps, y, chans)
-            density = dense[at * width + y : at * width + y + 1, :]
-            hidden[at, y] = finish(summed, first_columns, density).astype(BF16)
-    for x in range(size_x):
-        for y in range(size_y):
-            row = (x + 1) * width + y + 1
-            taps = [(e, x + e) for e in range(3)]
-            summed = taps_of(hidden, second, taps, y, chans)[:, :size_z]
-            density = dense[row : row + 1, :size_z]
-            turned[y] = finish(summed, second_columns, density)
-        out[:, x] = jnp.swapaxes(turned[...], 0, 1).astype(BF16)
+            row = beside[y : y + 1]
+            ends_at = jnp.where(lane == 6 * y + 1, rolled(row, 6 * y + 2, 1), ends_at)
+            ends_at = jnp.where(lane == 6 * y + 4, rolled(row, 6 * y + 4, 1), ends_at)
+        inward = swapped(finish(edges_at[at], first_columns, ends_at).astype(BF16))
+        fix = swapped(fixes[at])
+        for y in range(size_y + 2):
+            value = partial[at, y]
+            value = value + jnp.where(outside, rolled(fix, -6 * y - 2, 1), 0.0)
+            if (at, y) in rows_at:
+                value = value + rows_at[at, y]
+            cells = finish(value, first_columns, density[at][0][y : y + 1])
+            put(hidden, at, y, cells.astype(BF16), inward)
+    for x in range(1, size_x - 1):
+        beside = density[x + 1][1]
+        ends_at = jnp.zeros((1, size_z), F32)
+        for y in range(size_y + 2):
+            row = beside[y : y + 1]
+            ends_at = jnp.where(lane == 6 * y + 1, rolled(row, 6 * y + 2, 1), ends_at)
+            ends_at = jnp.where(lane == 6 * y + 4, rolled(row, 6 * y + 4, 1), ends_at)
+        edge = finish(partial_edge[x + 1], first_columns, ends_at).astype(BF16)
+        for y in range(size_y + 2):
+            cells = finish(
+                partial[x + 1, y], first_columns, density[x + 1][0][y : y + 1]
+            )
+            put(hidden, x + 1, y, cells.astype(BF16), swapped(edge))
+    copies = []
+    for plane in range(size_x + 2):
+        least = max(0, plane - size_x + 1)
+        most = min(2, plane)
+        for rows in pairs_of(size_y):
+            found = product(second, slice(least, most + 1), hidden, plane, rows)
+            for y, parts in zip(rows, found):
+                for e, values in enumerate(parts, least):
+                    x = plane - e
+                    if e > 0:
+                        values = total[x, y] + values
+                    if e == 2:
+                        values = finish(
+                            values, second_columns, density[x + 1][0][y + 1 : y + 2]
+                        )
+                    total[x, y] = values
+        x = plane - 2
+        if x >= 0:
+            ready[x] = jnp.swapaxes(total[x], 0, 1).astype(BF16)
+            copies.append(pltpu.make_async_copy(ready.at[x], out.at[:, x], done.at[x]))
+            copies[-1].start()
+    for copy in copies:
+        copy.wait()
 
 
 def shards(
@@ -451,7 +566,7 @@
     chans, size_x, size_y, size_z = features.shape
     count_y, count_z = lax.axis_size("gy"), lax.axis_size("gz")
     group = size_x * count_y * size_y
-    assert group == chans and 4 * size_x * (size_y + 4) + 4 <= size_z
+    assert group == chans and size_x >= 2 and 6 * size_x * size_y + 4 <= size_z
     depth = size_x * 16
     main_below = shift(features[:, size_x - 2 :], "gx", 1)
     main_above = shift(features[:, :2], "gx", -1)
@@ -459,7 +574,7 @@
         functools.partial(paint_body, count_y, count_z),
         [((size_x, size_y, chans, size_z), BF16)]
         + [((chans + 2 * group, size_z), BF16)] * (count_z - 1)
-        + [((2 * group, size_z), F32)],
+        + [((2 * group, size_z), F32), ((chans, size_z), BF16)],
         fetched=(2, 3, 4, 0),
         late=(0,),
     )(features, live_counts[None, :], dest_bricks.T, cell_ids, cic_masses)
@@ -473,11 +588,11 @@
         functools.partial(pack_y_body, count_y, count_z, size_x),
         [((chans, size_z), BF16), ((2 * depth, size_z), F32)]
         + [((r, size_z), BF16) for r in rows],
-    )(planes, painted[-1], *from_z)
+    )(planes, *painted[-2:], *from_z)
     from_y = [shift(packed[1 + s], "gy", s) for s in range(1, count_y)]
     modulated = call(
         modulate_body,
-        [((3, 3 * chans, 3 * chans), BF16), ((2, chans, size_z), F32)] * 2,
+        [((3, chans, 9 * chans), BF16), ((2, chans, size_z), F32)] * 2,
         flops=1 << 22,
         fetched=tuple(range(9)),
     )(
@@ -495,7 +610,7 @@
         functools.partial(pack_x_body, count_y, size_x, size_y, chans),
         [
             ((2 * depth, size_z), F32),
-            ((chans + 2 * depth, size_z), BF16),
+            ((size_x * chans + 2 * depth, size_z), BF16),
         ],
     )(packed[0], packed[1], *from_y)
     sides = call(
@@ -507,28 +622,35 @@
     high = shift(sides[2], "gy", -1)
     edge_below = shift(edges, "gx", 1)
     edge_above = shift(edges, "gx", -1)
-    flops = 2 * 9 * chans * chans * 2 * size_z
-    (partial,) = call(
+    flops = 2 * 9 * chans * chans * size_z
+    partial = call(
         functools.partial(own_body, size_x, size_y),
-        [((size_x + 2, size_y + 2, chans, 2 * size_z), F32)],
+        [
+            ((size_x + 2, size_y + 2, chans, size_z), F32),
+            ((size_x + 2, chans, size_z), F32),
+        ],
         limit=16,
         flops=flops * 3 * size_x * (size_y + 2),
-        scratch=[pltpu.VMEM((size_x, size_y + 4, chans, 2 * size_z), BF16)],
-    )(planes, from_y[0], from_y[-1], edges, modulated[0])
+        scratch=[
+            pltpu.VMEM((size_x, size_y + 4, 3, chans, size_z), BF16),
+            pltpu.VMEM((4, size_y + 4, 3, chans, size_z), BF16),
+        ],
+    )(planes, from_y[0], from_y[-1], edges, *sides[:2], modulated[0])
     (result,) = call(
         functools.partial(rest_body, size_x, size_y),
         [((chans, size_x, size_y, size_z), BF16)],
         limit=24,
+        space=pltpu.HBM,
         flops=flops * (6 * (size_y + 2) + 3 * size_x * size_y),
         scratch=[
-            pltpu.VMEM((4, size_y + 4, chans, 2 * size_z), BF16),
-            pltpu.VMEM((size_x + 2, size_y + 2, chans, 2 * size_z), BF16),
-            pltpu.VMEM(((size_x + 2) * 16, 2 * size_z), F32),
-            pltpu.VMEM((size_y, chans, size_z), F32),
+            pltpu.VMEM((4, 6, 3, chans, size_z), BF16),
+            pltpu.VMEM((size_x + 2, size_y + 2, 3, chans, size_z), BF16),
+            pltpu.VMEM((size_x, size_y, chans, size_z), F32),
+            pltpu.VMEM((size_x, chans, size_y, size_z), BF16),
+            pltpu.SemaphoreType.DMA((size_x,)),
         ],
     )(
-        partial,
-        *sides[:2],
+        *partial,
         edge_below,
         edge_above,
         low,

time: 33.6 us -> 33.2 us (0.988)
  starting transfers between devices: 13.8 us -> 15.8 us
  waiting for transfers between devices: 8.6 us -> 6.79 us
  Pallas kernels: 10.3 us -> 9.69 us
    ppermute x10, starting transfers between devices: 13.8 us -> 15.8 us  [shift(): return lax.ppermute(cells, axis, pairs)]
    ppermute x10, waiting for transfers between devices: 8.6 us -> 6.79 us  [shift(): return lax.ppermute(cells, axis, pairs)]
    pallas_call x7, Pallas kernels: 10.3 us -> 9.69 us  [run(): return kernel(*args)]
  transfers between devices with their start and end apart: 10 -> 10, of which waited for: 3 -> 3; matrix products, arithmetic and copies ran while one was open for 0% -> 0% of each run, Pallas kernels for 18% -> 20%
where the time goes in v5:
time: 33.2 us; the launch traced here: 33 us
  starting transfers between devices  15.8 us (48%)
  Pallas kernels  9.69 us (29%)
  waiting for transfers between devices  6.79 us (20%)
  between operations  0.74 us (2%)
    ppermute x10, starting transfers between devices, shift(): return lax.ppermute(cells, axis, pairs)  15.8 us
    pallas_call x7, Pallas kernels, run(): return kernel(*args)  9.69 us
    ppermute x10, waiting for transfers between devices, shift(): return lax.ppermute(cells, axis, pairs)  6.79 us
  transfers between devices with their start and end apart: 10, of which 3 were waited for; matrix products, arithmetic and copies ran while one was open for 0% of the time, Pallas kernels for 20%

profile of v5, /device:TPU:0, one launch (start us, length us, event | category | flops | bytes accessed | tf_op | source)
XLA Modules:
  0.0 33.0 jit_solution(9898113321165228336)
XLA Ops:
  0.0 3.1 %collective-permute-start.4 = (bf16[64,2,8,128]{3,2,1,0:T(8,128)(2,1)}, bf16[64,2,8,128]{3,2,1,0:T(8,128)(2,1)S(1)}, u32[]{:S(2)}, u32[]{:S(2)}) collective-permute-start(bf16[64,2,8,128]{3,2,1,0:T(8,128)(2,1)} %refs_0_.1), channel_id=1, source_target_pairs={{0,8},{8,16},{16,24},{24,0},{1,9},{9,17},{17,25},{25,1},{2,10},{10... | collective-permute-start | bytes 786440 | tf_op jit(solution)/shard_map/ppermute | solution.py:18
  3.1 2.0 %collective-permute-start.5 = (bf16[64,2,8,128]{3,2,1,0:T(8,128)(2,1)}, bf16[64,2,8,128]{3,2,1,0:T(8,128)(2,1)S(1)}, u32[]{:S(2)}, u32[]{:S(2)}) collective-permute-start(bf16[64,2,8,128]{3,2,1,0:T(8,128)(2,1)} %refs_0_.1), channel_id=1, source_target_pairs={{0,24},{8,0},{16,8},{24,16},{1,25},{9,1},{17,9},{25,17},{2,26},{10... | collective-permute-start | bytes 786440 | tf_op jit(solution)/shard_map/ppermute | solution.py:18
  5.7 1.5 %shard_map.136 = (bf16[2,8,64,128]{3,2,1,0:T(8,128)(2,1)S(1)}, bf16[192,128]{1,0:T(8,128)(2,1)S(1)}, f32[128,128]{1,0:T(8,128)S(1)}, bf16[64,128]{1,0:T(8,128)(2,1)S(1)}) custom-call(bf16[64,2,8,128]{3,2,1,0:T(8,128)(2,1)} %refs_0_.1, s32[1,1]{1,0:T(1,128)} %bitcast.9.refs_1_, s32[1,32]{1,0:T(1,128)} %bitcast.13, s32[32,64]{1,0:T(8,128)} %refs_3_.1, ...), custom_call_target="tpu_custom_call" | custom-call | bytes 274564 | tf_op jit(solution)/shard_map/pallas_call | solution.py:66
  7.2 1.8 %collective-permute-start = (bf16[192,128]{1,0:T(8,128)(2,1)S(1)}, bf16[192,128]{1,0:T(8,128)(2,1)S(1)}, u32[]{:S(2)}, u32[]{:S(2)}) collective-permute-start(bf16[192,128]{1,0:T(8,128)(2,1)S(1)} %get-tuple-element.29), channel_id=1, source_target_pairs={{0,1},{1,0},{2,3},{3,2},{4,5},{5,4},{6,7},{7,6},{8,9},{9,8},{10,11... | collective-permute-start | bytes 147464 | tf_op jit(solution)/shard_map/ppermute | solution.py:18
  9.0 2.4 %collective-permute-done.refs_3_ = bf16[192,128]{1,0:T(8,128)(2,1)S(1)} collective-permute-done((bf16[192,128]{1,0:T(8,128)(2,1)S(1)}, bf16[192,128]{1,0:T(8,128)(2,1)S(1)}, u32[]{:S(2)}, u32[]{:S(2)}) %collective-permute-start) | collective-permute-done | bytes 49184 | tf_op jit(solution)/shard_map/ppermute | solution.py:18
  11.3 0.2 shard_map.137
  11.5 0.1 collective-permute-start.1
  11.6 1.7 %collective-permute-start.2 = (bf16[384,128]{1,0:T(8,128)(2,1)S(1)}, bf16[384,128]{1,0:T(8,128)(2,1)S(1)}, u32[]{:S(2)}, u32[]{:S(2)}) collective-permute-start(bf16[384,128]{1,0:T(8,128)(2,1)S(1)} %get-tuple-element.31), channel_id=1, source_target_pairs={{0,6},{2,0},{4,2},{6,4},{1,7},{3,1},{5,3},{7,5},{8,14},{10,8},{12,... | collective-permute-start | bytes 294920 | tf_op jit(solution)/shard_map/ppermute | solution.py:18
  13.3 3.3 %collective-permute-done.5.refs_1_ = bf16[64,2,8,128]{3,2,1,0:T(8,128)(2,1)S(1)} collective-permute-done((bf16[64,2,8,128]{3,2,1,0:T(8,128)(2,1)}, bf16[64,2,8,128]{3,2,1,0:T(8,128)(2,1)S(1)}, u32[]{:S(2)}, u32[]{:S(2)}) %collective-permute-start.5) | collective-permute-done | bytes 262176 | tf_op jit(solution)/shard_map/ppermute | solution.py:18
  16.6 0.3 shard_map.139
  16.9 0.1 collective-permute-start.8
  17.0 1.7 %collective-permute-start.9 = (bf16[512,128]{1,0:T(8,128)(2,1)S(1)}, bf16[512,128]{1,0:T(8,128)(2,1)S(1)}, u32[]{:S(2)}, u32[]{:S(2)}) collective-permute-start(bf16[512,128]{1,0:T(8,128)(2,1)S(1)} %get-tuple-element.42), channel_id=1, source_target_pairs={{0,6},{2,0},{4,2},{6,4},{1,7},{3,1},{5,3},{7,5},{8,14},{10,8},{12,... | collective-permute-start | bytes 393224 | tf_op jit(solution)/shard_map/ppermute | solution.py:18
  18.7 1.5 %collective-permute-start.3 = (bf16[96,128]{1,0:T(8,128)(2,1)S(1)}, bf16[96,128]{1,0:T(8,128)(2,1)S(1)}, u32[]{:S(2)}, u32[]{:S(2)}) collective-permute-start(bf16[96,128]{1,0:T(8,128)(2,1)S(1)} %get-tuple-element.34), channel_id=1, source_target_pairs={{0,4},{2,6},{4,0},{6,2},{1,5},{3,7},{5,1},{7,3},{8,12},{10,14},{12... | collective-permute-start | bytes 73736 | tf_op jit(solution)/shard_map/ppermute | solution.py:18
  20.2 2.1 %shard_map.140 = (bf16[3,64,576]{2,1,0:T(8,128)(2,1)S(1)}, f32[2,64,128]{2,1,0:T(8,128)S(1)}, bf16[3,64,576]{2,1,0:T(8,128)(2,1)S(1)}, f32[2,64,128]{2,1,0:T(8,128)S(1)}) custom-call(f32[1,512]{1,0:T(1,128)} %bitcast.12, f32[64,512]{1,0:T(8,128)} %bitcast.10, bf16[27,64,64]{2,1,0:T(8,128)(2,1)} %refs_2_.1, f32[1,64]{1,0:T(1,128)} %bitcast.14, ...), custom_call_target="tpu_custom_call" | custom-call | flops 4194304 | bytes 707584 | tf_op jit(solution)/shard_map/pallas_call | solution.py:66
  22.4 1.1 %collective-permute-done.3.refs_3_ = bf16[96,128]{1,0:T(8,128)(2,1)S(1)} collective-permute-done((bf16[96,128]{1,0:T(8,128)(2,1)S(1)}, bf16[96,128]{1,0:T(8,128)(2,1)S(1)}, u32[]{:S(2)}, u32[]{:S(2)}) %collective-permute-start.3) | collective-permute-done | bytes 24608 | tf_op jit(solution)/shard_map/ppermute | solution.py:18
  23.4 0.0 collective-permute-done.1.refs_2_.refs_1_
  23.5 0.0 collective-permute-done.2.refs_4_.refs_2_
  23.5 0.2 shard_map.138
  23.6 1.2 %collective-permute-start.6 = (bf16[192,128]{1,0:T(8,128)(2,1)S(1)}, bf16[192,128]{1,0:T(8,128)(2,1)S(1)}, u32[]{:S(2)}, u32[]{:S(2)}) collective-permute-start(bf16[192,128]{1,0:T(8,128)(2,1)S(1)} %get-tuple-element.35.refs_3_), channel_id=1, source_target_pairs={{0,8},{8,16},{16,24},{24,0},{1,9},{9,17},{17,25},{25,1},{2,10},{10... | collective-permute-start | bytes 147464 | tf_op jit(solution)/shard_map/ppermute | solution.py:18
  24.8 2.7 %collective-permute-start.7 = (bf16[192,128]{1,0:T(8,128)(2,1)S(1)}, bf16[192,128]{1,0:T(8,128)(2,1)S(1)}, u32[]{:S(2)}, u32[]{:S(2)}) collective-permute-start(bf16[192,128]{1,0:T(8,128)(2,1)S(1)} %get-tuple-element.35.refs_3_), channel_id=1, source_target_pairs={{0,24},{8,0},{16,8},{24,16},{1,25},{9,1},{17,9},{25,17},{2,26},{10... | collective-permute-start | bytes 147464 | tf_op jit(solution)/shard_map/ppermute | solution.py:18
  27.5 2.3 %shard_map.141 = (f32[4,10,64,128]{3,2,1,0:T(8,128)S(1)}, f32[4,64,128]{2,1,0:T(8,128)S(1)}) custom-call(bf16[2,8,64,128]{3,2,1,0:T(8,128)(2,1)S(1)} %get-tuple-element.26.refs_0_, bf16[384,128]{1,0:T(8,128)(2,1)S(1)} %collective-permute-done.1.refs_2_.refs_1_, bf16[384,128]{1,0:T(8,128)(2,1)S(1)} %collective-permute-done.2.refs_4_.refs_2_, ...), custom_call_target="tpu_custom_call" | custom-call | flops 566231040 | bytes 1253376 | tf_op jit(solution)/shard_map/pallas_call | solution.py:66
  29.7 0.0 collective-permute-done.6.refs_2_
  29.8 0.0 collective-permute-done.7.refs_3_
  29.8 3.2 %shard_map.142 = bf16[64,2,8,128]{3,2,1,0:T(8,128)(2,1)} custom-call(f32[4,10,64,128]{3,2,1,0:T(8,128)S(1)} %get-tuple-element.39.refs_0_, f32[4,64,128]{2,1,0:T(8,128)S(1)} %get-tuple-element.40.refs_1_, bf16[192,128]{1,0:T(8,128)(2,1)S(1)} %collective-permute-done.6.refs_2_, bf16[192,128]{1,0:T(8,128)(2,1)S(1)} %collective-permute-done.7.refs_3_, ...), custom_call_target="tpu_custom_call" | custom-call | flops 1019215872 | bytes 2408448 | tf_op jit(solution)/shard_map/pallas_call | solution.py:66
  (3 shorter events, 0.0 us)
Async XLA Ops:
  0.0 13.3 %collective-permute-start.4 = (bf16[64,2,8,128]{3,2,1,0:T(8,128)(2,1)}, bf16[64,2,8,128]{3,2,1,0:T(8,128)(2,1)S(1)}, u32[]{:S(2)}, u32[]{:S(2)}) collective-permute-start(bf16[64,2,8,128]{3,2,1,0:T(8,128)(2,1)} %refs_0_.1), channel_id=1, source_target_pairs={{0,8},{8,16},{16,24},{24,0},{1,9},{9,17},{17,25},{25,1},{2,10},{10... | collective-permute-start | bytes 786440 | tf_op jit(solution)/shard_map/ppermute | solution.py:18
  3.1 13.6 %collective-permute-start.5 = (bf16[64,2,8,128]{3,2,1,0:T(8,128)(2,1)}, bf16[64,2,8,128]{3,2,1,0:T(8,128)(2,1)S(1)}, u32[]{:S(2)}, u32[]{:S(2)}) collective-permute-start(bf16[64,2,8,128]{3,2,1,0:T(8,128)(2,1)} %refs_0_.1), channel_id=1, source_target_pairs={{0,24},{8,0},{16,8},{24,16},{1,25},{9,1},{17,9},{25,17},{2,26},{10... | collective-permute-start | bytes 786440 | tf_op jit(solution)/shard_map/ppermute | solution.py:18
  7.2 4.2 %collective-permute-start = (bf16[192,128]{1,0:T(8,128)(2,1)S(1)}, bf16[192,128]{1,0:T(8,128)(2,1)S(1)}, u32[]{:S(2)}, u32[]{:S(2)}) collective-permute-start(bf16[192,128]{1,0:T(8,128)(2,1)S(1)} %get-tuple-element.29), channel_id=1, source_target_pairs={{0,1},{1,0},{2,3},{3,2},{4,5},{5,4},{6,7},{7,6},{8,9},{9,8},{10,11... | collective-permute-start | bytes 147464 | tf_op jit(solution)/shard_map/ppermute | solution.py:18
  11.5 11.9 %collective-permute-start.1 = (bf16[384,128]{1,0:T(8,128)(2,1)S(1)}, bf16[384,128]{1,0:T(8,128)(2,1)S(1)}, u32[]{:S(2)}, u32[]{:S(2)}) collective-permute-start(bf16[384,128]{1,0:T(8,128)(2,1)S(1)} %get-tuple-element.30), channel_id=1, source_target_pairs={{0,2},{2,4},{4,6},{6,0},{1,3},{3,5},{5,7},{7,1},{8,10},{10,12},{12... | collective-permute-start | bytes 294920 | tf_op jit(solution)/shard_map/ppermute | solution.py:18
  11.6 11.9 %collective-permute-start.2 = (bf16[384,128]{1,0:T(8,128)(2,1)S(1)}, bf16[384,128]{1,0:T(8,128)(2,1)S(1)}, u32[]{:S(2)}, u32[]{:S(2)}) collective-permute-start(bf16[384,128]{1,0:T(8,128)(2,1)S(1)} %get-tuple-element.31), channel_id=1, source_target_pairs={{0,6},{2,0},{4,2},{6,4},{1,7},{3,1},{5,3},{7,5},{8,14},{10,8},{12,... | collective-permute-start | bytes 294920 | tf_op jit(solution)/shard_map/ppermute | solution.py:18
  16.9 12.8 %collective-permute-start.8 = (bf16[512,128]{1,0:T(8,128)(2,1)S(1)}, bf16[512,128]{1,0:T(8,128)(2,1)S(1)}, u32[]{:S(2)}, u32[]{:S(2)}) collective-permute-start(bf16[512,128]{1,0:T(8,128)(2,1)S(1)} %get-tuple-element.41), channel_id=1, source_target_pairs={{0,2},{2,4},{4,6},{6,0},{1,3},{3,5},{5,7},{7,1},{8,10},{10,12},{12... | collective-permute-start | bytes 393224 | tf_op jit(solution)/shard_map/ppermute | solution.py:18
  17.0 12.8 %collective-permute-start.9 = (bf16[512,128]{1,0:T(8,128)(2,1)S(1)}, bf16[512,128]{1,0:T(8,128)(2,1)S(1)}, u32[]{:S(2)}, u32[]{:S(2)}) collective-permute-start(bf16[512,128]{1,0:T(8,128)(2,1)S(1)} %get-tuple-element.42), channel_id=1, source_target_pairs={{0,6},{2,0},{4,2},{6,4},{1,7},{3,1},{5,3},{7,5},{8,14},{10,8},{12,... | collective-permute-start | bytes 393224 | tf_op jit(solution)/shard_map/ppermute | solution.py:18
  18.7 4.7 %collective-permute-start.3 = (bf16[96,128]{1,0:T(8,128)(2,1)S(1)}, bf16[96,128]{1,0:T(8,128)(2,1)S(1)}, u32[]{:S(2)}, u32[]{:S(2)}) collective-permute-start(bf16[96,128]{1,0:T(8,128)(2,1)S(1)} %get-tuple-element.34), channel_id=1, source_target_pairs={{0,4},{2,6},{4,0},{6,2},{1,5},{3,7},{5,1},{7,3},{8,12},{10,14},{12... | collective-permute-start | bytes 73736 | tf_op jit(solution)/shard_map/ppermute | solution.py:18
  23.6 6.1 %collective-permute-start.6 = (bf16[192,128]{1,0:T(8,128)(2,1)S(1)}, bf16[192,128]{1,0:T(8,128)(2,1)S(1)}, u32[]{:S(2)}, u32[]{:S(2)}) collective-permute-start(bf16[192,128]{1,0:T(8,128)(2,1)S(1)} %get-tuple-element.35.refs_3_), channel_id=1, source_target_pairs={{0,8},{8,16},{16,24},{24,0},{1,9},{9,17},{17,25},{25,1},{2,10},{10... | collective-permute-start | bytes 147464 | tf_op jit(solution)/shard_map/ppermute | solution.py:18
  24.8 5.0 %collective-permute-start.7 = (bf16[192,128]{1,0:T(8,128)(2,1)S(1)}, bf16[192,128]{1,0:T(8,128)(2,1)S(1)}, u32[]{:S(2)}, u32[]{:S(2)}) collective-permute-start(bf16[192,128]{1,0:T(8,128)(2,1)S(1)} %get-tuple-element.35.refs_3_), channel_id=1, source_target_pairs={{0,24},{8,0},{16,8},{24,16},{1,25},{9,1},{17,9},{25,17},{2,26},{10... | collective-permute-start | bytes 147464 | tf_op jit(solution)/shard_map/ppermute | solution.py:18

commit v6 on v5

--- a/solution.py
+++ b/solution.py
@@ -277,7 +277,7 @@
 
 def pack_x_body(count_y, size_x, size_y, chans, tile, own, *refs):
     received = refs[: count_y - 1]
-    dens, out = refs[count_y - 1], refs[count_y]
+    dens, up, down = refs[count_y - 1 :]
     depth = own.shape[0] // 2
     base = 6 * size_x * size_y
     main, beside = own[:depth], own[depth:]
@@ -303,8 +303,11 @@
         edge = jnp.where(lane >= at, rolled(high, at - first, 1), edge)
         if x == 0:
             edge = with_ends(edge, beside, 6 * tall)
-        out[x * chans : (x + 1) * chans] = edge.astype(BF16)
-    store_halves(out, size_x * chans, main)
+        for out in (up, down):
+            out[x * chans : (x + 1) * chans] = edge.astype(BF16)
+    width = depth // size_x
+    store_halves(up, size_x * chans, main[depth - width :])
+    store_halves(down, size_x * chans, main[:width])
 
 
 def activate(values):
@@ -361,10 +364,24 @@
 def put(stack, plane, row, cells, inward):
     lane = lanes_of(cells.shape)
     last = cells.shape[1] - 1
-    ends_of = rolled(inward, -6 * row - 2, 1)
+    if inward is None:
+        ends_of = jnp.zeros(cells.shape, cells.dtype)
+    else:
+        ends_of = rolled(inward, -6 * row - 2, 1)
     stack[plane, row, 0] = jnp.where(lane == 0, ends_of, rolled(cells, 1, 1))
     stack[plane, row, 1] = cells
     stack[plane, row, 2] = jnp.where(lane == last, ends_of, rolled(cells, -1, 1))
+
+
+def ends_row(beside):
+    lane = lanes_of(beside.shape)
+    at = 6 * lax.broadcasted_iota(jnp.int32, beside.shape, 0)
+    before = pltpu.roll(beside, 2, 1, stride=6, stride_axis=0)
+    after = pltpu.roll(beside, 4, 1, stride=6, stride_axis=0)
+    kept = jnp.where(
+        lane == at + 1, before, jnp.where(lane == at + 4, after, jnp.zeros_like(beside))
+    )
+    return jnp.sum(kept, axis=0, keepdims=True)
 
 
 def fill(stack, at, main, low, high, start, tile, size_y):
@@ -418,14 +435,13 @@
                 for e, values in enumerate(parts):
                     at = x + 2 - e
                     add(partial, (at, y), values, x == 0 or e == 0)
-    nothing = jnp.zeros((chans, size_z), BF16)
     for side, main, plan in sides_of(size_x, below, above):
         for plane, taps, targets in plan:
             at = side + plane
             for y in (0, 1, size_y + 2, size_y + 3):
                 beside[at, y] = jnp.zeros((3, chans, size_z), BF16)
             for y in range(size_y):
-                put(beside, at, 2 + y, main[plane, y], nothing)
+                put(beside, at, 2 + y, main[plane, y], None)
             for rows in pairs_of(size_y + 2):
                 found = product(weights, taps, beside, at, rows)
                 for y, parts in zip(rows, found):
@@ -461,15 +477,13 @@
         density.append((own[:depth][rows], own[depth:][rows]))
     for edge, x, at in ((edge_below, size_x - 1, 0), (edge_above, 0, size_x + 1)):
         rows = slice(x * width, (x + 1) * width)
-        main = load_halves(edge, size_x * chans, depth)
+        main = load_halves(edge, size_x * chans, width)
         beside = ends(edge[:depth].astype(F32), 6 * tall)
-        density.insert(at, (main[rows], beside[rows]))
-    lane = lanes_of((1, size_z))
+        density.insert(at, (main, beside[rows]))
     edges_at = {at: partial_edge[at] for at in range(size_x + 2)}
     fixes = {}
     rows_at = {}
     nothing = jnp.zeros((3, chans, size_z), BF16)
-    idle = jnp.zeros((chans, size_z), BF16)
     for side, edge, plan in sides_of(size_x, edge_below, edge_above):
         for plane, taps, targets in plan:
             at = side + plane
@@ -482,9 +496,9 @@
                 fixes[target] = fixes[target] + fix if target in fixes else fix
             for i in range(2):
                 start = (2 * at + i) * chans
-                put(stack, at, i, low[start : start + chans], idle)
+                put(stack, at, i, low[start : start + chans], None)
                 stack[at, 2 + i] = nothing
-                put(stack, at, 4 + i, high[start : start + chans], idle)
+                put(stack, at, 4 + i, high[start : start + chans], None)
             for begin, rows in ((0, range(2)), (size_y, range(2, 4))):
                 found = product(first, taps, stack, at, rows)
                 for i, parts in enumerate(found):
@@ -495,11 +509,7 @@
     outside = (wide == 0) | (wide == size_z - 1)
     for at in sorted(fixes):
         beside = density[at][1]
-        ends_at = jnp.zeros((1, size_z), F32)
-        for y in range(size_y + 2):
-            row = beside[y : y + 1]
-            ends_at = jnp.where(lane == 6 * y + 1, rolled(row, 6 * y + 2, 1), ends_at)
-            ends_at = jnp.where(lane == 6 * y + 4, rolled(row, 6 * y + 4, 1), ends_at)
+        ends_at = ends_row(beside)
         inward = swapped(finish(edges_at[at], first_columns, ends_at).astype(BF16))
         fix = swapped(fixes[at])
         for y in range(size_y + 2):
@@ -511,11 +521,7 @@
             put(hidden, at, y, cells.astype(BF16), inward)
     for x in range(1, size_x - 1):
         beside = density[x + 1][1]
-        ends_at = jnp.zeros((1, size_z), F32)
-        for y in range(size_y + 2):
-            row = beside[y : y + 1]
-            ends_at = jnp.where(lane == 6 * y + 1, rolled(row, 6 * y + 2, 1), ends_at)
-            ends_at = jnp.where(lane == 6 * y + 4, rolled(row, 6 * y + 4, 1), ends_at)
+        ends_at = ends_row(beside)
         edge = finish(partial_edge[x + 1], first_columns, ends_at).astype(BF16)
         for y in range(size_y + 2):
             cells = finish(
@@ -606,11 +612,12 @@
         bias_second[None, :],
         gain_second[None, :],
     )
-    dens, edges = call(
+    dens, edges_up, edges = call(
         functools.partial(pack_x_body, count_y, size_x, size_y, chans),
         [
             ((2 * depth, size_z), F32),
-            ((size_x * chans + 2 * depth, size_z), BF16),
+            ((size_x * chans + 2 * depth // size_x, size_z), BF16),
+            ((size_x * chans + 2 * depth // size_x, size_z), BF16),
         ],
     )(packed[0], packed[1], *from_y)
     sides = call(
@@ -620,7 +627,7 @@
     )(main_below, main_above)
     low = shift(sides[3], "gy", 1)
     high = shift(sides[2], "gy", -1)
-    edge_below = shift(edges, "gx", 1)
+    edge_below = shift(edges_up, "gx", 1)
     edge_above = shift(edges, "gx", -1)
     flops = 2 * 9 * chans * chans * size_z
     partial = call(

time: 33.2 us -> 33.2 us (level)
  no operation moved by 1% of the time
where the time goes in v6:
time: 33.2 us; the launch traced here: 33 us
  starting transfers between devices  15.8 us (48%)
  Pallas kernels  9.67 us (29%)
  waiting for transfers between devices  6.79 us (20%)
  between operations  0.74 us (2%)
    ppermute x10, starting transfers between devices, shift(): return lax.ppermute(cells, axis, pairs)  15.8 us
    pallas_call x7, Pallas kernels, run(): return kernel(*args)  9.67 us
    ppermute x10, waiting for transfers between devices, shift(): return lax.ppermute(cells, axis, pairs)  6.79 us
  transfers between devices with their start and end apart: 10, of which 3 were waited for; matrix products, arithmetic and copies ran while one was open for 0% of the time, Pallas kernels for 20%

profile of v6, /device:TPU:0, one launch (start us, length us, event | category | flops | bytes accessed | tf_op | source)
XLA Modules:
  0.0 33.0 jit_solution(13074083808198228693)
XLA Ops:
  0.0 3.1 %collective-permute-start.4 = (bf16[64,2,8,128]{3,2,1,0:T(8,128)(2,1)}, bf16[64,2,8,128]{3,2,1,0:T(8,128)(2,1)S(1)}, u32[]{:S(2)}, u32[]{:S(2)}) collective-permute-start(bf16[64,2,8,128]{3,2,1,0:T(8,128)(2,1)} %refs_0_.1), channel_id=1, source_target_pairs={{0,8},{8,16},{16,24},{24,0},{1,9},{9,17},{17,25},{25,1},{2,10},{10... | collective-permute-start | bytes 786440 | tf_op jit(solution)/shard_map/ppermute | solution.py:18
  3.1 2.0 %collective-permute-start.5 = (bf16[64,2,8,128]{3,2,1,0:T(8,128)(2,1)}, bf16[64,2,8,128]{3,2,1,0:T(8,128)(2,1)S(1)}, u32[]{:S(2)}, u32[]{:S(2)}) collective-permute-start(bf16[64,2,8,128]{3,2,1,0:T(8,128)(2,1)} %refs_0_.1), channel_id=1, source_target_pairs={{0,24},{8,0},{16,8},{24,16},{1,25},{9,1},{17,9},{25,17},{2,26},{10... | collective-permute-start | bytes 786440 | tf_op jit(solution)/shard_map/ppermute | solution.py:18
  5.7 1.5 %shard_map.136 = (bf16[2,8,64,128]{3,2,1,0:T(8,128)(2,1)S(1)}, bf16[192,128]{1,0:T(8,128)(2,1)S(1)}, f32[128,128]{1,0:T(8,128)S(1)}, bf16[64,128]{1,0:T(8,128)(2,1)S(1)}) custom-call(bf16[64,2,8,128]{3,2,1,0:T(8,128)(2,1)} %refs_0_.1, s32[1,1]{1,0:T(1,128)} %bitcast.9.refs_1_, s32[1,32]{1,0:T(1,128)} %bitcast.13, s32[32,64]{1,0:T(8,128)} %refs_3_.1, ...), custom_call_target="tpu_custom_call" | custom-call | bytes 274564 | tf_op jit(solution)/shard_map/pallas_call | solution.py:66
  7.2 1.8 %collective-permute-start = (bf16[192,128]{1,0:T(8,128)(2,1)S(1)}, bf16[192,128]{1,0:T(8,128)(2,1)S(1)}, u32[]{:S(2)}, u32[]{:S(2)}) collective-permute-start(bf16[192,128]{1,0:T(8,128)(2,1)S(1)} %get-tuple-element.30), channel_id=1, source_target_pairs={{0,1},{1,0},{2,3},{3,2},{4,5},{5,4},{6,7},{7,6},{8,9},{9,8},{10,11... | collective-permute-start | bytes 147464 | tf_op jit(solution)/shard_map/ppermute | solution.py:18
  9.0 2.4 %collective-permute-done.refs_3_ = bf16[192,128]{1,0:T(8,128)(2,1)S(1)} collective-permute-done((bf16[192,128]{1,0:T(8,128)(2,1)S(1)}, bf16[192,128]{1,0:T(8,128)(2,1)S(1)}, u32[]{:S(2)}, u32[]{:S(2)}) %collective-permute-start) | collective-permute-done | bytes 49184 | tf_op jit(solution)/shard_map/ppermute | solution.py:18
  11.3 0.2 shard_map.137
  11.5 0.1 collective-permute-start.1
  11.6 1.7 %collective-permute-start.2 = (bf16[384,128]{1,0:T(8,128)(2,1)S(1)}, bf16[384,128]{1,0:T(8,128)(2,1)S(1)}, u32[]{:S(2)}, u32[]{:S(2)}) collective-permute-start(bf16[384,128]{1,0:T(8,128)(2,1)S(1)} %get-tuple-element.32), channel_id=1, source_target_pairs={{0,6},{2,0},{4,2},{6,4},{1,7},{3,1},{5,3},{7,5},{8,14},{10,8},{12,... | collective-permute-start | bytes 294920 | tf_op jit(solution)/shard_map/ppermute | solution.py:18
  13.3 0.0 collective-permute-done.4.refs_0_
  13.3 3.3 %collective-permute-done.5.refs_1_ = bf16[64,2,8,128]{3,2,1,0:T(8,128)(2,1)S(1)} collective-permute-done((bf16[64,2,8,128]{3,2,1,0:T(8,128)(2,1)}, bf16[64,2,8,128]{3,2,1,0:T(8,128)(2,1)S(1)}, u32[]{:S(2)}, u32[]{:S(2)}) %collective-permute-start.5) | collective-permute-done | bytes 262176 | tf_op jit(solution)/shard_map/ppermute | solution.py:18
  16.6 0.3 shard_map.139
  16.9 0.1 collective-permute-start.8
  17.0 1.7 %collective-permute-start.9 = (bf16[512,128]{1,0:T(8,128)(2,1)S(1)}, bf16[512,128]{1,0:T(8,128)(2,1)S(1)}, u32[]{:S(2)}, u32[]{:S(2)}) collective-permute-start(bf16[512,128]{1,0:T(8,128)(2,1)S(1)} %get-tuple-element.44), channel_id=1, source_target_pairs={{0,6},{2,0},{4,2},{6,4},{1,7},{3,1},{5,3},{7,5},{8,14},{10,8},{12,... | collective-permute-start | bytes 393224 | tf_op jit(solution)/shard_map/ppermute | solution.py:18
  18.7 1.5 %collective-permute-start.3 = (bf16[96,128]{1,0:T(8,128)(2,1)S(1)}, bf16[96,128]{1,0:T(8,128)(2,1)S(1)}, u32[]{:S(2)}, u32[]{:S(2)}) collective-permute-start(bf16[96,128]{1,0:T(8,128)(2,1)S(1)} %get-tuple-element.35), channel_id=1, source_target_pairs={{0,4},{2,6},{4,0},{6,2},{1,5},{3,7},{5,1},{7,3},{8,12},{10,14},{12... | collective-permute-start | bytes 73736 | tf_op jit(solution)/shard_map/ppermute | solution.py:18
  20.2 2.1 %shard_map.140 = (bf16[3,64,576]{2,1,0:T(8,128)(2,1)S(1)}, f32[2,64,128]{2,1,0:T(8,128)S(1)}, bf16[3,64,576]{2,1,0:T(8,128)(2,1)S(1)}, f32[2,64,128]{2,1,0:T(8,128)S(1)}) custom-call(f32[1,512]{1,0:T(1,128)} %bitcast.12, f32[64,512]{1,0:T(8,128)} %bitcast.10, bf16[27,64,64]{2,1,0:T(8,128)(2,1)} %refs_2_.1, f32[1,64]{1,0:T(1,128)} %bitcast.14, ...), custom_call_target="tpu_custom_call" | custom-call | flops 4194304 | bytes 707584 | tf_op jit(solution)/shard_map/pallas_call | solution.py:66
  22.4 1.1 %collective-permute-done.3.refs_3_ = bf16[96,128]{1,0:T(8,128)(2,1)S(1)} collective-permute-done((bf16[96,128]{1,0:T(8,128)(2,1)S(1)}, bf16[96,128]{1,0:T(8,128)(2,1)S(1)}, u32[]{:S(2)}, u32[]{:S(2)}) %collective-permute-start.3) | collective-permute-done | bytes 24608 | tf_op jit(solution)/shard_map/ppermute | solution.py:18
  23.5 0.0 collective-permute-done.1.refs_2_.refs_1_
  23.5 0.2 shard_map.138
  23.6 1.2 %collective-permute-start.6 = (bf16[160,128]{1,0:T(8,128)(2,1)S(1)}, bf16[160,128]{1,0:T(8,128)(2,1)S(1)}, u32[]{:S(2)}, u32[]{:S(2)}) collective-permute-start(bf16[160,128]{1,0:T(8,128)(2,1)S(1)} %get-tuple-element.42), channel_id=1, source_target_pairs={{0,8},{8,16},{16,24},{24,0},{1,9},{9,17},{17,25},{25,1},{2,10},{10... | collective-permute-start | bytes 122888 | tf_op jit(solution)/shard_map/ppermute | solution.py:18
  24.8 2.7 %collective-permute-start.7 = (bf16[160,128]{1,0:T(8,128)(2,1)S(1)}, bf16[160,128]{1,0:T(8,128)(2,1)S(1)}, u32[]{:S(2)}, u32[]{:S(2)}) collective-permute-start(bf16[160,128]{1,0:T(8,128)(2,1)S(1)} %get-tuple-element.36.refs_3_), channel_id=1, source_target_pairs={{0,24},{8,0},{16,8},{24,16},{1,25},{9,1},{17,9},{25,17},{2,26},{10... | collective-permute-start | bytes 122888 | tf_op jit(solution)/shard_map/ppermute | solution.py:18
  27.5 2.3 %shard_map.141 = (f32[4,10,64,128]{3,2,1,0:T(8,128)S(1)}, f32[4,64,128]{2,1,0:T(8,128)S(1)}) custom-call(bf16[2,8,64,128]{3,2,1,0:T(8,128)(2,1)S(1)} %get-tuple-element.27.refs_0_, bf16[384,128]{1,0:T(8,128)(2,1)S(1)} %collective-permute-done.1.refs_2_.refs_1_, bf16[384,128]{1,0:T(8,128)(2,1)S(1)} %collective-permute-done.2.refs_4_.refs_2_, ...), custom_call_target="tpu_custom_call" | custom-call | flops 566231040 | bytes 1245184 | tf_op jit(solution)/shard_map/pallas_call | solution.py:66
  29.8 0.0 collective-permute-done.7.refs_3_
  29.8 0.0 collective-permute-done.8.refs_4_
  29.8 3.2 %shard_map.142 = bf16[64,2,8,128]{3,2,1,0:T(8,128)(2,1)} custom-call(f32[4,10,64,128]{3,2,1,0:T(8,128)S(1)} %get-tuple-element.40.refs_0_, f32[4,64,128]{2,1,0:T(8,128)S(1)} %get-tuple-element.41.refs_1_, bf16[160,128]{1,0:T(8,128)(2,1)S(1)} %collective-permute-done.6.refs_2_, bf16[160,128]{1,0:T(8,128)(2,1)S(1)} %collective-permute-done.7.refs_3_, ...), custom_call_target="tpu_custom_call" | custom-call | flops 1019215872 | bytes 2392064 | tf_op jit(solution)/shard_map/pallas_call | solution.py:66
  (3 shorter events, 0.0 us)
Async XLA Ops:
  0.0 13.3 %collective-permute-start.4 = (bf16[64,2,8,128]{3,2,1,0:T(8,128)(2,1)}, bf16[64,2,8,128]{3,2,1,0:T(8,128)(2,1)S(1)}, u32[]{:S(2)}, u32[]{:S(2)}) collective-permute-start(bf16[64,2,8,128]{3,2,1,0:T(8,128)(2,1)} %refs_0_.1), channel_id=1, source_target_pairs={{0,8},{8,16},{16,24},{24,0},{1,9},{9,17},{17,25},{25,1},{2,10},{10... | collective-permute-start | bytes 786440 | tf_op jit(solution)/shard_map/ppermute | solution.py:18
  3.1 13.6 %collective-permute-start.5 = (bf16[64,2,8,128]{3,2,1,0:T(8,128)(2,1)}, bf16[64,2,8,128]{3,2,1,0:T(8,128)(2,1)S(1)}, u32[]{:S(2)}, u32[]{:S(2)}) collective-permute-start(bf16[64,2,8,128]{3,2,1,0:T(8,128)(2,1)} %refs_0_.1), channel_id=1, source_target_pairs={{0,24},{8,0},{16,8},{24,16},{1,25},{9,1},{17,9},{25,17},{2,26},{10... | collective-permute-start | bytes 786440 | tf_op jit(solution)/shard_map/ppermute | solution.py:18
  7.2 4.2 %collective-permute-start = (bf16[192,128]{1,0:T(8,128)(2,1)S(1)}, bf16[192,128]{1,0:T(8,128)(2,1)S(1)}, u32[]{:S(2)}, u32[]{:S(2)}) collective-permute-start(bf16[192,128]{1,0:T(8,128)(2,1)S(1)} %get-tuple-element.30), channel_id=1, source_target_pairs={{0,1},{1,0},{2,3},{3,2},{4,5},{5,4},{6,7},{7,6},{8,9},{9,8},{10,11... | collective-permute-start | bytes 147464 | tf_op jit(solution)/shard_map/ppermute | solution.py:18
  11.5 11.9 %collective-permute-start.1 = (bf16[384,128]{1,0:T(8,128)(2,1)S(1)}, bf16[384,128]{1,0:T(8,128)(2,1)S(1)}, u32[]{:S(2)}, u32[]{:S(2)}) collective-permute-start(bf16[384,128]{1,0:T(8,128)(2,1)S(1)} %get-tuple-element.31), channel_id=1, source_target_pairs={{0,2},{2,4},{4,6},{6,0},{1,3},{3,5},{5,7},{7,1},{8,10},{10,12},{12... | collective-permute-start | bytes 294920 | tf_op jit(solution)/shard_map/ppermute | solution.py:18
  11.6 11.9 %collective-permute-start.2 = (bf16[384,128]{1,0:T(8,128)(2,1)S(1)}, bf16[384,128]{1,0:T(8,128)(2,1)S(1)}, u32[]{:S(2)}, u32[]{:S(2)}) collective-permute-start(bf16[384,128]{1,0:T(8,128)(2,1)S(1)} %get-tuple-element.32), channel_id=1, source_target_pairs={{0,6},{2,0},{4,2},{6,4},{1,7},{3,1},{5,3},{7,5},{8,14},{10,8},{12,... | collective-permute-start | bytes 294920 | tf_op jit(solution)/shard_map/ppermute | solution.py:18
  16.9 12.9 %collective-permute-start.8 = (bf16[512,128]{1,0:T(8,128)(2,1)S(1)}, bf16[512,128]{1,0:T(8,128)(2,1)S(1)}, u32[]{:S(2)}, u32[]{:S(2)}) collective-permute-start(bf16[512,128]{1,0:T(8,128)(2,1)S(1)} %get-tuple-element.43), channel_id=1, source_target_pairs={{0,2},{2,4},{4,6},{6,0},{1,3},{3,5},{5,7},{7,1},{8,10},{10,12},{12... | collective-permute-start | bytes 393224 | tf_op jit(solution)/shard_map/ppermute | solution.py:18
  17.0 12.8 %collective-permute-start.9 = (bf16[512,128]{1,0:T(8,128)(2,1)S(1)}, bf16[512,128]{1,0:T(8,128)(2,1)S(1)}, u32[]{:S(2)}, u32[]{:S(2)}) collective-permute-start(bf16[512,128]{1,0:T(8,128)(2,1)S(1)} %get-tuple-element.44), channel_id=1, source_target_pairs={{0,6},{2,0},{4,2},{6,4},{1,7},{3,1},{5,3},{7,5},{8,14},{10,8},{12,... | collective-permute-start | bytes 393224 | tf_op jit(solution)/shard_map/ppermute | solution.py:18
  18.7 4.7 %collective-permute-start.3 = (bf16[96,128]{1,0:T(8,128)(2,1)S(1)}, bf16[96,128]{1,0:T(8,128)(2,1)S(1)}, u32[]{:S(2)}, u32[]{:S(2)}) collective-permute-start(bf16[96,128]{1,0:T(8,128)(2,1)S(1)} %get-tuple-element.35), channel_id=1, source_target_pairs={{0,4},{2,6},{4,0},{6,2},{1,5},{3,7},{5,1},{7,3},{8,12},{10,14},{12... | collective-permute-start | bytes 73736 | tf_op jit(solution)/shard_map/ppermute | solution.py:18
  23.6 6.2 %collective-permute-start.6 = (bf16[160,128]{1,0:T(8,128)(2,1)S(1)}, bf16[160,128]{1,0:T(8,128)(2,1)S(1)}, u32[]{:S(2)}, u32[]{:S(2)}) collective-permute-start(bf16[160,128]{1,0:T(8,128)(2,1)S(1)} %get-tuple-element.42), channel_id=1, source_target_pairs={{0,8},{8,16},{16,24},{24,0},{1,9},{9,17},{17,25},{25,1},{2,10},{10... | collective-permute-start | bytes 122888 | tf_op jit(solution)/shard_map/ppermute | solution.py:18
  24.8 5.0 %collective-permute-start.7 = (bf16[160,128]{1,0:T(8,128)(2,1)S(1)}, bf16[160,128]{1,0:T(8,128)(2,1)S(1)}, u32[]{:S(2)}, u32[]{:S(2)}) collective-permute-start(bf16[160,128]{1,0:T(8,128)(2,1)S(1)} %get-tuple-element.36.refs_3_), channel_id=1, source_target_pairs={{0,24},{8,0},{16,8},{24,16},{1,25},{9,1},{17,9},{25,17},{2,26},{10... | collective-permute-start | bytes 122888 | tf_op jit(solution)/shard_map/ppermute | solution.py:18
